TPU v7x, 768 devices: a whole 4x8x12 slice. The times are simulated.
768 devices in a mesh: along: 96 (over x, z, core), across: 8 (over y).
Axes of the slice: x: 4, y: 8, z: 12, core: 2. Of those that a mesh axis runs over, the one named last changes fastest.
Arguments:
- field_now: float32 [3072, 256, 128], P('along', 'across'), may hold values from -6 to 6
- field_before: float32 [3072, 256, 128], P('along', 'across'), may hold values from -6 to 6
- layer: int32 [3072, 256, 128], P('along', 'across'), may hold values from 0 to 7
- modulus_table: float32 [8], replicated, may hold values from 0.4 to 2
- fk_panel: bfloat16 [2, 192, 8, 12288], P(None, 'along', 'across'), may hold values from -6 to 6
- owner: int32 [8, 12288, 1], P('across', 'along'), may hold values from 0 to 7; in each aligned block of 128 rows (0 to 127, 128 to 255, ..., all dimensions but the last counted through in order) at most 64 rows name the same one
- local_cell: int32 [8, 12288], P('across', 'along'), may hold values from 0 to 131071
Outputs:
- field_next: float32 [3072, 256, 128], P('along', 'across')
- field_prior: float32 [3072, 256, 128], P('along', 'across')
Inputs may be any that keep to these rules, and one draw needn't show every extreme that they name: Among the 128 points of one tile (one row of owner and column block of 128), at most 64 have the same owner, and this many is reached.
All inputs are finite; a program needn't handle non-finite values.
Results may differ from a plain program's by a relative error of at most 0.0003.
Values may be sent and summed in bfloat16 or wider, within the bound.
No kernel may reach another device: no remote copies, remote signals or barrier semaphores. Data moves between devices by JAX's collectives and lax.ppermute only.
A program may use at most 192 MiB of HBM per device.

v0:
```python
import math

import jax
import jax.numpy as jnp
from jax import lax
from jax.sharding import PartitionSpec as P

STEPS = 8


def extended(array, sides, width):
    for axis, dim in sides:
        count, length = (lax.axis_size(axis), array.shape[dim])
        up = [(i, (i + 1) % count) for i in range(count - 1)]
        down = [(j, i) for i, j in up]
        last = lax.slice_in_dim(array, length - width, length, axis=dim)
        leading = lax.slice_in_dim(array, 0, width, axis=dim)
        before = lax.ppermute(last, axis, up)
        after = lax.ppermute(leading, axis, down)
        array = jnp.concatenate([before, array, after], axis=dim)
    return array


def stiffness(u_pad, mu_pad):
    uc = u_pad[1:-1, 1:-1, 1:-1]
    mc = mu_pad[1:-1, 1:-1, 1:-1]
    total = jnp.zeros_like(uc)
    for sx, sy, sz in ((2, 1, 1), (0, 1, 1), (1, 2, 1), (1, 0, 1), (1, 1, 2), (1, 1, 0)):
        ex = u_pad.shape[0] - 2 + sx
        ey = u_pad.shape[1] - 2 + sy
        ez = u_pad.shape[2] - 2 + sz
        un = u_pad[sx:ex, sy:ey, sz:ez]
        mn = mu_pad[sx:ex, sy:ey, sz:ez]
        total = total + 0.5 * (mc + mn) * (un - uc)
    return total


def freq_table(count, total_freqs):
    freq = jnp.arange(count, dtype=jnp.int32).astype(jnp.float32)
    times = jnp.arange(STEPS).astype(jnp.float32)
    phase = math.pi * times[:, None] * freq[None, :] / total_freqs
    return jnp.concatenate([jnp.cos(phase), -jnp.sin(phase)], axis=1) / math.sqrt(total_freqs)


def shards(field_now, field_before, layer, modulus_table, fk_panel, owner, local_cell):
    size_x, size_y, size_z = field_now.shape
    cells = size_x * size_y * size_z
    tiles_y = lax.axis_size("across")
    local_freqs = fk_panel.shape[1]
    total_freqs = local_freqs * lax.axis_size("along")
    points = owner.shape[1]
    modulus = jnp.zeros(field_now.shape, jnp.float32)
    for level in range(modulus_table.shape[0]):
        modulus = modulus + jnp.where(layer == level, modulus_table[level], 0.0)
    moved = lax.all_to_all(fk_panel, "along", split_axis=3, concat_axis=1, tiled=True)
    panel = moved.astype(jnp.float32).reshape(2 * total_freqs, points)
    table = freq_table(total_freqs, total_freqs)
    forcing = jnp.dot(table, panel, precision=lax.Precision.HIGHEST)
    owner_row = owner[0, :, 0]
    cell_row = local_cell[0]
    capacity = points // 2
    onehot = (owner_row[:, None] == jnp.arange(tiles_y, dtype=jnp.int32)[None, :]).astype(jnp.int32)
    rank = jnp.cumsum(onehot, axis=0) - onehot
    slot = jnp.sum(rank * onehot, axis=1)
    send_force = (
        jnp.zeros((tiles_y, STEPS, capacity), jnp.float32).at[owner_row, :, slot].set(forcing.T)
    )
    send_cell = jnp.full((tiles_y, capacity), cells, jnp.int32).at[owner_row, slot].set(cell_row)
    got_force, got_cell = (
        lax.all_to_all(send_force, "across", split_axis=0, concat_axis=0, tiled=True),
        lax.all_to_all(send_cell, "across", split_axis=0, concat_axis=0, tiled=True),
    )
    force_in = jnp.transpose(got_force, (1, 0, 2)).reshape(STEPS, tiles_y * capacity)
    cells_in = got_cell.reshape(tiles_y * capacity)
    now, before = (field_now, field_before)
    mu_rim = extended(modulus, (("along", 0), ("across", 1)), 1)
    mu_pad = jnp.pad(mu_rim, ((0, 0), (0, 0), (1, 1)))
    for step in range(STEPS):
        drive = (
            jnp.zeros((cells,), jnp.float32)
            .at[cells_in]
            .add(force_in[step], mode="drop")
            .reshape(size_x, size_y, size_z)
        )
        rim = extended(now, (("along", 0), ("across", 1)), 1)
        u_pad = jnp.pad(rim, ((0, 0), (0, 0), (1, 1)))
        new = 2.0 * now - before + 0.15 * stiffness(u_pad, mu_pad) + drive
        before = now
        now = new
    return (now, before)


def solution(mesh):
    placed = (
        P("along", "across", None),
        P("along", "across", None),
        P("along", "across", None),
        P(),
        P(None, "along", "across", None),
        P("across", "along", None),
        P("across", "along"),
    )
    return jax.shard_map(
        shards,
        mesh=mesh,
        in_specs=placed,
        out_specs=(P("along", "across", None), P("along", "across", None)),
        check_vma=False,
    )
```

profile of v0, /device:TPU:30, one launch (start us, length us, event | category | flops | bytes accessed | tf_op | source)
XLA Modules:
  0.0 320.5 jit_solution(11800331708556449323)
XLA Ops:
  2.3 6.5 %select_add_fusion = f32[32,32,128]{2,1,0:T(8,128)S(1)} fusion(s32[32,32,128]{2,1,0:T(8,128)} %param.9, f32[]{:T(128)} %bitcast.7, f32[]{:T(128)} %bitcast.6, f32[]{:T(128)} %bitcast.5, f32[]{:T(128)} %bitcast.4, f32[]{:T(128)} %bitcast.3, f32[]{:T(128)} %bitcast.2, f32[]{:T(128)} %bitcast.1, f32[]{:T(128)} %bitcast), kind=kLoop, calls=%fused_computation.288 | loop fusion | flops 3014656 | bytes 1048608 | tf_op jit(solution)/shard_map/add | solution.py:54
  8.8 14.3 %collective-permute-start = (f32[1,32,128]{2,1,0:T(8,128)S(1)}, f32[1,32,128]{2,1,0:T(8,128)S(1)}, u32[]{:S(2)}, u32[]{:S(2)}) collective-permute-start(f32[1,32,128]{2,1,0:T(8,128)S(1)} %get-tuple-element.46), channel_id=1, source_target_pairs={{8,0},{16,8},{24,16},{32,24},{40,32},{48,40},{56,48},{64,56},{72,6... | collective-permute-start | bytes 49160 | tf_op jit(solution)/shard_map/ppermute | solution.py:19
  23.1 1.9 collective-permute-start.2
  27.4 19.9 %scatter_fusion = s32[8,64]{1,0:T(8,128)} fusion(s32[8,64]{1,0:T(8,128)} %broadcast_in_dim.66, s32[128]{0:T(128)S(1)} %fusion.177, s32[128]{0:T(128)S(1)} %bitcast.66), kind=kCustom, calls=%fused_computation | custom fusion | bytes 2560 | tf_op jit(solution)/shard_map/scatter | solution.py:68
  47.3 7.3 %all-to-all-start = ((s32[8,1,64]{2,1,0:T(1,128)}), s32[8,1,64]{2,1,0:T(1,128)S(1)}, u32[]{:S(2)}, u32[]{:S(2)}) async-start(s32[8,1,64]{2,1,0:T(1,128)} %bitcast.14), calls=%async_computation | async-start | bytes 8192 | tf_op jit(solution)/shard_map/all_to_all | solution.py:71
  54.6 1.9 collective-permute-start.3
  56.5 5.8 %collective-permute-start.1 = (f32[1,32,128]{2,1,0:T(8,128)S(1)}, f32[1,32,128]{2,1,0:T(8,128)S(1)}, u32[]{:S(2)}, u32[]{:S(2)}) collective-permute-start(f32[1,32,128]{2,1,0:T(8,128)S(1)} %get-tuple-element.47), channel_id=1, source_target_pairs={{8,0},{16,8},{24,16},{32,24},{40,32},{48,40},{56,48},{64,56},{72,6... | collective-permute-start | bytes 49160 | tf_op jit(solution)/shard_map/ppermute | solution.py:19
  62.4 10.0 %copy.24 = bf16[2,2,1,12288]{1,0,2,3:T(2,128)(2,1)} copy(bf16[2,2,1,12288]{3,1,2,0:T(2,128)(2,1)S(1)} %copy-done.18) | data formatting | bytes 196608 | tf_op args[4]
  72.4 10.7 %reshape.288 = bf16[96,2,256]{2,1,0:T(2,128)(2,1)} reshape(bf16[12288,1,2,2]{3,2,1,0:T(2,128)(2,1)} %bitcast.42) | data formatting | bytes 196608
  83.1 6.1 %all-to-all-start.1 = ((bf16[96,2,256]{2,1,0:T(2,128)(2,1)}), bf16[96,2,256]{2,1,0:T(2,128)(2,1)S(1)}, u32[]{:S(2)}, u32[]{:S(2)}) async-start(bf16[96,2,256]{2,1,0:T(2,128)(2,1)} %reshape.288), calls=%async_computation.1 | async-start | bytes 196608 | tf_op jit(solution)/shard_map/all_to_all | solution.py:55
  90.6 2.5 collective-permute-start.4
  93.1 4.6 %collective-permute-start.6 = (f32[34,1,128]{2,1,0:T(1,128)S(1)}, f32[34,1,128]{2,1,0:T(1,128)S(1)}, u32[]{:S(2)}, u32[]{:S(2)}) collective-permute-start(f32[34,1,128]{2,1,0:T(1,128)S(1)} %get-tuple-element.27), channel_id=1, source_target_pairs={{0,1},{1,2},{2,3},{3,4},{4,5},{5,6},{6,7},{8,9},{9,10},{10,11},{11... | collective-permute-start | bytes 52232 | tf_op jit(solution)/shard_map/ppermute | solution.py:18
  97.8 1.9 collective-permute-start.5
  99.7 5.1 %collective-permute-start.7 = (f32[34,1,128]{2,1,0:T(1,128)S(1)}, f32[34,1,128]{2,1,0:T(1,128)S(1)}, u32[]{:S(2)}, u32[]{:S(2)}) collective-permute-start(f32[34,1,128]{2,1,0:T(1,128)S(1)} %get-tuple-element.29), channel_id=1, source_target_pairs={{0,1},{1,2},{2,3},{3,4},{4,5},{5,6},{6,7},{8,9},{9,10},{10,11},{11... | collective-permute-start | bytes 52232 | tf_op jit(solution)/shard_map/ppermute | solution.py:18
  106.5 14.5 %reshape.289 = bf16[12288,1,2,2]{3,2,1,0:T(2,128)(2,1)} reshape(bf16[96,2,256]{2,1,0:T(2,128)(2,1)S(1)} %all-to-all-done.1) | data formatting | bytes 196608
  121.1 9.0 %copy.29 = bf16[2,2,1,96,128]{4,3,1,0,2:T(8,128)(2,1)S(1)} copy(bf16[2,2,1,96,128]{1,0,4,3,2:T(2,128)(2,1)} %bitcast.41) | data formatting | bytes 196608 | tf_op jit(solution)/shard_map/all_to_all | solution.py:55
  130.5 6.9 %scatter_fusion.1 = f32[8,8,64]{1,2,0:T(8,128)S(1)} fusion(f32[8,8,64]{1,2,0:T(8,128)S(1)} %broadcast_in_dim.67, s32[128]{0:T(128)S(1)} %fusion.177, f32[128,8]{1,0:T(8,128)S(1)} %copy.27), kind=kCustom, calls=%fused_computation.1 | custom fusion | bytes 13312 | tf_op jit(solution)/shard_map/scatter | solution.py:66
  138.2 5.1 %all-to-all-start.2 = ((f32[8,1,512]{2,1,0:T(1,128)}), f32[8,1,512]{2,1,0:T(1,128)S(1)}, u32[]{:S(2)}, u32[]{:S(2)}) async-start(f32[8,1,512]{2,1,0:T(1,128)} %reshape.290), calls=%async_computation.2 | async-start | bytes 32768 | tf_op jit(solution)/shard_map/all_to_all | solution.py:70
  145.0 2.9 all-to-all-done.2
  149.4 3.6 %scatter_custom_fusion.2 = f32[131072]{0:T(1024)S(1)} fusion(s32[512]{0:T(512)S(1)} %bitcast.58, f32[512]{0:T(512)S(1)} %reshape.161, f32[]{:T(128)} %constant.20.clone.1), kind=kCustom, calls=%fused_computation.303 | custom fusion | flops 512 | bytes 524292 | tf_op jit(solution)/shard_map/scatter-add | solution.py:82
  153.0 3.7 %fusion.131 = (f32[32,32,128]{2,1,0:T(8,128)S(1)}, f32[32,32,128]{2,1,0:T(8,128)S(1)}, f32[32,32,128]{2,1,0:T(8,128)S(1)}) fusion(f32[32,32,128]{2,1,0:T(8,128)S(1)} %bitcast.52, f32[32,32,128]{2,1,0:T(8,128)S(1)} %copy-done.11, f32[34,34,130]{2,1,0:T(8,128)} %select_maximum_fusion.28, f32[34,32,128]{2,1,0:T(8,128)} %copy-done.15, ...), kind=kLoop, calls=%fused_computation.249 | loop fusion | flops 6029312 | bytes 6459392 | tf_op jit(solution)/shard_map/add | solution.py:87
  156.6 2.1 collective-permute-start.8
  158.7 2.3 collective-permute-start.9
  161.0 4.9 %collective-permute-done.9 = f32[1,32,128]{2,1,0:T(8,128)S(1)} collective-permute-done((f32[1,32,128]{2,1,0:T(8,128)S(1)}, f32[1,32,128]{2,1,0:T(8,128)S(1)}, u32[]{:S(2)}, u32[]{:S(2)}) %collective-permute-start.9) | collective-permute-done | bytes 16416 | tf_op jit(solution)/shard_map/ppermute | solution.py:18
  165.9 3.3 %collective-permute-start.10 = (f32[34,1,128]{2,1,0:T(1,128)S(1)}, f32[34,1,128]{2,1,0:T(1,128)S(1)}, u32[]{:S(2)}, u32[]{:S(2)}) collective-permute-start(f32[34,1,128]{2,1,0:T(1,128)S(1)} %get-tuple-element.26), channel_id=1, source_target_pairs={{1,0},{2,1},{3,2},{4,3},{5,4},{6,5},{7,6},{9,8},{10,9},{11,10},{12... | collective-permute-start | bytes 52232 | tf_op jit(solution)/shard_map/ppermute | solution.py:19
  169.2 3.7 %collective-permute-start.11 = (f32[34,1,128]{2,1,0:T(1,128)S(1)}, f32[34,1,128]{2,1,0:T(1,128)S(1)}, u32[]{:S(2)}, u32[]{:S(2)}) collective-permute-start(f32[34,1,128]{2,1,0:T(1,128)S(1)} %get-tuple-element.25), channel_id=1, source_target_pairs={{0,1},{1,2},{2,3},{3,4},{4,5},{5,6},{6,7},{8,9},{9,10},{10,11},{11... | collective-permute-start | bytes 52232 | tf_op jit(solution)/shard_map/ppermute | solution.py:18
  173.1 4.0 %scatter_custom_fusion.3 = f32[131072]{0:T(1024)} fusion(s32[512]{0:T(512)S(1)} %bitcast.59, f32[512]{0:T(512)S(1)} %reshape.169, f32[]{:T(128)} %constant.20.clone.1), kind=kCustom, calls=%fused_computation.301 | custom fusion | flops 512 | bytes 524292 | tf_op jit(solution)/shard_map/scatter-add | solution.py:82
  179.0 1.9 collective-permute-start.12
  180.9 2.4 collective-permute-start.13
  183.4 4.7 %collective-permute-done.13 = f32[1,32,128]{2,1,0:T(8,128)S(1)} collective-permute-done((f32[1,32,128]{2,1,0:T(8,128)S(1)}, f32[1,32,128]{2,1,0:T(8,128)S(1)}, u32[]{:S(2)}, u32[]{:S(2)}) %collective-permute-start.13) | collective-permute-done | bytes 16416 | tf_op jit(solution)/shard_map/ppermute | solution.py:18
  188.1 2.1 collective-permute-start.14
  190.2 5.0 %collective-permute-start.15 = (f32[34,1,128]{2,1,0:T(1,128)S(1)}, f32[34,1,128]{2,1,0:T(1,128)S(1)}, u32[]{:S(2)}, u32[]{:S(2)}) collective-permute-start(f32[34,1,128]{2,1,0:T(1,128)S(1)} %get-tuple-element.23), channel_id=1, source_target_pairs={{0,1},{1,2},{2,3},{3,4},{4,5},{5,6},{6,7},{8,9},{9,10},{10,11},{11... | collective-permute-start | bytes 52232 | tf_op jit(solution)/shard_map/ppermute | solution.py:18
  195.3 4.0 %scatter_custom_fusion.4 = f32[131072]{0:T(1024)} fusion(s32[512]{0:T(512)S(1)} %bitcast.60, f32[512]{0:T(512)S(1)} %reshape.177, f32[]{:T(128)} %constant.20.clone.1), kind=kCustom, calls=%fused_computation.299 | custom fusion | flops 512 | bytes 524292 | tf_op jit(solution)/shard_map/scatter-add | solution.py:82
  201.3 1.9 collective-permute-start.16
  203.2 2.4 collective-permute-start.17
  205.6 4.7 %collective-permute-done.17 = f32[1,32,128]{2,1,0:T(8,128)S(1)} collective-permute-done((f32[1,32,128]{2,1,0:T(8,128)S(1)}, f32[1,32,128]{2,1,0:T(8,128)S(1)}, u32[]{:S(2)}, u32[]{:S(2)}) %collective-permute-start.17) | collective-permute-done | bytes 16416 | tf_op jit(solution)/shard_map/ppermute | solution.py:18
  210.4 1.9 collective-permute-start.18
  212.3 5.1 %collective-permute-start.19 = (f32[34,1,128]{2,1,0:T(1,128)S(1)}, f32[34,1,128]{2,1,0:T(1,128)S(1)}, u32[]{:S(2)}, u32[]{:S(2)}) collective-permute-start(f32[34,1,128]{2,1,0:T(1,128)S(1)} %get-tuple-element.21), channel_id=1, source_target_pairs={{0,1},{1,2},{2,3},{3,4},{4,5},{5,6},{6,7},{8,9},{9,10},{10,11},{11... | collective-permute-start | bytes 52232 | tf_op jit(solution)/shard_map/ppermute | solution.py:18
  217.5 4.0 %scatter_custom_fusion.5 = f32[131072]{0:T(1024)} fusion(s32[512]{0:T(512)S(1)} %bitcast.61, f32[512]{0:T(512)S(1)} %reshape.185, f32[]{:T(128)} %constant.20.clone.1), kind=kCustom, calls=%fused_computation.297 | custom fusion | flops 512 | bytes 524292 | tf_op jit(solution)/shard_map/scatter-add | solution.py:82
  223.5 1.9 collective-permute-start.20
  225.4 2.4 collective-permute-start.21
  227.9 4.7 %collective-permute-done.21 = f32[1,32,128]{2,1,0:T(8,128)S(1)} collective-permute-done((f32[1,32,128]{2,1,0:T(8,128)S(1)}, f32[1,32,128]{2,1,0:T(8,128)S(1)}, u32[]{:S(2)}, u32[]{:S(2)}) %collective-permute-start.21) | collective-permute-done | bytes 16416 | tf_op jit(solution)/shard_map/ppermute | solution.py:18
  232.6 1.9 collective-permute-start.22
  234.6 5.1 %collective-permute-start.23 = (f32[34,1,128]{2,1,0:T(1,128)S(1)}, f32[34,1,128]{2,1,0:T(1,128)S(1)}, u32[]{:S(2)}, u32[]{:S(2)}) collective-permute-start(f32[34,1,128]{2,1,0:T(1,128)S(1)} %get-tuple-element.19), channel_id=1, source_target_pairs={{0,1},{1,2},{2,3},{3,4},{4,5},{5,6},{6,7},{8,9},{9,10},{10,11},{11... | collective-permute-start | bytes 52232 | tf_op jit(solution)/shard_map/ppermute | solution.py:18
  239.8 4.0 %scatter_custom_fusion.6 = f32[131072]{0:T(1024)} fusion(s32[512]{0:T(512)S(1)} %bitcast.62, f32[512]{0:T(512)S(1)} %reshape.193, f32[]{:T(128)} %constant.20.clone.1), kind=kCustom, calls=%fused_computation.295 | custom fusion | flops 512 | bytes 524292 | tf_op jit(solution)/shard_map/scatter-add | solution.py:82
  245.6 4.0 %fusion.59 = f32[32,32,128]{2,1,0:T(8,128)S(1)} fusion(f32[32,32,128]{2,1,0:T(8,128)} %bitcast.47, f32[32,32,128]{2,1,0:T(8,128)S(1)} %get-tuple-element.12, f32[32,32,128]{2,1,0:T(8,128)S(1)} %copy-done.9, f32[34,34,130]{2,1,0:T(8,128)S(1)} %select_maximum_fusion.12, f32[32,32,128]{2,1,0:T(8,128)S(1)} %get-tuple-element.11, ...), kind=kLoop, calls=%fused_computation.137 | loop fusion | flops 9961472 | bytes 7018496 | tf_op jit(solution)/shard_map/add | solution.py:87
  249.7 1.9 collective-permute-start.24
  251.6 2.4 collective-permute-start.25
  254.0 4.7 %collective-permute-done.25 = f32[1,32,128]{2,1,0:T(8,128)S(1)} collective-permute-done((f32[1,32,128]{2,1,0:T(8,128)S(1)}, f32[1,32,128]{2,1,0:T(8,128)S(1)}, u32[]{:S(2)}, u32[]{:S(2)}) %collective-permute-start.25) | collective-permute-done | bytes 16416 | tf_op jit(solution)/shard_map/ppermute | solution.py:18
  258.8 2.1 collective-permute-start.26
  260.9 5.1 %collective-permute-start.27 = (f32[34,1,128]{2,1,0:T(1,128)S(1)}, f32[34,1,128]{2,1,0:T(1,128)S(1)}, u32[]{:S(2)}, u32[]{:S(2)}) collective-permute-start(f32[34,1,128]{2,1,0:T(1,128)S(1)} %get-tuple-element.17), channel_id=1, source_target_pairs={{0,1},{1,2},{2,3},{3,4},{4,5},{5,6},{6,7},{8,9},{9,10},{10,11},{11... | collective-permute-start | bytes 52232 | tf_op jit(solution)/shard_map/ppermute | solution.py:18
  266.1 4.0 %scatter_custom_fusion.7 = f32[131072]{0:T(1024)} fusion(s32[512]{0:T(512)S(1)} %bitcast.63, f32[512]{0:T(512)S(1)} %reshape.201, f32[]{:T(128)} %constant.20.clone.1), kind=kCustom, calls=%fused_computation.293 | custom fusion | flops 512 | bytes 524292 | tf_op jit(solution)/shard_map/scatter-add | solution.py:82
  271.6 3.9 %fusion.41 = f32[32,32,128]{2,1,0:T(8,128)S(1)} fusion(f32[32,32,128]{2,1,0:T(8,128)} %bitcast.48, f32[32,32,128]{2,1,0:T(8,128)S(1)} %get-tuple-element.12, f32[32,32,128]{2,1,0:T(8,128)S(1)} %fusion.59, f32[34,34,130]{2,1,0:T(8,128)S(1)} %select_maximum_fusion.8, f32[32,32,128]{2,1,0:T(8,128)S(1)} %get-tuple-element.11, ...), kind=kLoop, calls=%fused_computation.109 | loop fusion | flops 9961472 | bytes 7018496 | tf_op jit(solution)/shard_map/add | solution.py:87
  275.5 1.9 collective-permute-start.28
  277.4 2.4 collective-permute-start.29
  279.9 4.7 %collective-permute-done.29 = f32[1,32,128]{2,1,0:T(8,128)S(1)} collective-permute-done((f32[1,32,128]{2,1,0:T(8,128)S(1)}, f32[1,32,128]{2,1,0:T(8,128)S(1)}, u32[]{:S(2)}, u32[]{:S(2)}) %collective-permute-start.29) | collective-permute-done | bytes 16416 | tf_op jit(solution)/shard_map/ppermute | solution.py:18
  284.7 2.1 collective-permute-start.30
  286.7 5.1 %collective-permute-start.31 = (f32[34,1,128]{2,1,0:T(1,128)S(1)}, f32[34,1,128]{2,1,0:T(1,128)S(1)}, u32[]{:S(2)}, u32[]{:S(2)}) collective-permute-start(f32[34,1,128]{2,1,0:T(1,128)S(1)} %get-tuple-element.15), channel_id=1, source_target_pairs={{0,1},{1,2},{2,3},{3,4},{4,5},{5,6},{6,7},{8,9},{9,10},{10,11},{11... | collective-permute-start | bytes 52232 | tf_op jit(solution)/shard_map/ppermute | solution.py:18
  291.9 4.0 %scatter_custom_fusion.8 = f32[131072]{0:T(1024)} fusion(s32[512]{0:T(512)S(1)} %bitcast.64, f32[512]{0:T(512)S(1)} %reshape.209, f32[]{:T(128)} %constant.20.clone.1), kind=kCustom, calls=%fused_computation.291 | custom fusion | flops 512 | bytes 524292 | tf_op jit(solution)/shard_map/scatter-add | solution.py:82
  298.6 1.9 collective-permute-start.32
  300.5 2.4 collective-permute-start.33
  302.9 4.7 %collective-permute-done.33 = f32[1,32,128]{2,1,0:T(8,128)S(1)} collective-permute-done((f32[1,32,128]{2,1,0:T(8,128)S(1)}, f32[1,32,128]{2,1,0:T(8,128)S(1)}, u32[]{:S(2)}, u32[]{:S(2)}) %collective-permute-start.33) | collective-permute-done | bytes 16416 | tf_op jit(solution)/shard_map/ppermute | solution.py:18
  309.6 5.1 %collective-permute-start.35 = (f32[34,1,128]{2,1,0:T(1,128)S(1)}, f32[34,1,128]{2,1,0:T(1,128)S(1)}, u32[]{:S(2)}, u32[]{:S(2)}) collective-permute-start(f32[34,1,128]{2,1,0:T(1,128)S(1)} %get-tuple-element.13), channel_id=1, source_target_pairs={{0,1},{1,2},{2,3},{3,4},{4,5},{5,6},{6,7},{8,9},{9,10},{10,11},{11... | collective-permute-start | bytes 52232 | tf_op jit(solution)/shard_map/ppermute | solution.py:18
  314.9 3.4 %scatter_custom_fusion.9 = f32[131072]{0:T(1024)S(1)} fusion(s32[512]{0:T(512)S(1)} %bitcast.65, f32[512]{0:T(512)S(1)} %reshape.217, f32[]{:T(128)} %constant.20.clone.1), kind=kCustom, calls=%fused_computation.289 | custom fusion | flops 512 | bytes 524292 | tf_op jit(solution)/shard_map/scatter-add | solution.py:82
  (140 shorter events, 28.0 us)
Async XLA Ops:
  0.6 26.2 %copy-start.19 = (s32[1,128,1]{1,2,0:T(1,128)S(1)}, s32[1,128,1]{1,2,0:T(1,128)}, u32[]{:S(2)}) copy-start(s32[1,128,1]{1,2,0:T(1,128)} %param.12) | copy-start | bytes 1540
  0.6 26.8 %copy-start.20 = (s32[1,128]{1,0:T(1,128)S(1)}, s32[1,128]{1,0:T(1,128)}, u32[]{:S(2)}) copy-start(s32[1,128]{1,0:T(1,128)} %param.13) | copy-start | bytes 1540
  0.7 53.9 %copy-start.11 = (f32[32,32,128]{2,1,0:T(8,128)S(1)}, f32[32,32,128]{2,1,0:T(8,128)}, u32[]{:S(2)}) copy-start(f32[32,32,128]{2,1,0:T(8,128)} %param.7) | copy-start | bytes 1572868
  0.7 61.8 %copy-start.18 = (bf16[2,2,1,12288]{3,1,2,0:T(2,128)(2,1)S(1)}, bf16[2,2,1,12288]{3,1,2,0:T(2,128)(2,1)}, u32[]{:S(2)}) copy-start(bf16[2,2,1,12288]{3,1,2,0:T(2,128)(2,1)} %param.11) | copy-start | bytes 294916
  8.8 81.7 %collective-permute-start = (f32[1,32,128]{2,1,0:T(8,128)S(1)}, f32[1,32,128]{2,1,0:T(8,128)S(1)}, u32[]{:S(2)}, u32[]{:S(2)}) collective-permute-start(f32[1,32,128]{2,1,0:T(8,128)S(1)} %get-tuple-element.46), channel_id=1, source_target_pairs={{8,0},{16,8},{24,16},{32,24},{40,32},{48,40},{56,48},{64,56},{72,6... | collective-permute-start | bytes 49160 | tf_op jit(solution)/shard_map/ppermute | solution.py:19
  23.1 67.4 %collective-permute-start.2 = (f32[1,32,128]{2,1,0:T(8,128)S(1)}, f32[1,32,128]{2,1,0:T(8,128)S(1)}, u32[]{:S(2)}, u32[]{:S(2)}) collective-permute-start(f32[1,32,128]{2,1,0:T(8,128)S(1)} %get-tuple-element.45), channel_id=1, source_target_pairs={{0,8},{8,16},{16,24},{24,32},{32,40},{40,48},{48,56},{56,64},{64,7... | collective-permute-start | bytes 49160 | tf_op jit(solution)/shard_map/ppermute | solution.py:18
  47.3 35.9 %all-to-all-start = ((s32[8,1,64]{2,1,0:T(1,128)}), s32[8,1,64]{2,1,0:T(1,128)S(1)}, u32[]{:S(2)}, u32[]{:S(2)}) async-start(s32[8,1,64]{2,1,0:T(1,128)} %bitcast.14), calls=%async_computation | async-start | bytes 8192 | tf_op jit(solution)/shard_map/all_to_all | solution.py:71
  54.6 43.0 %collective-permute-start.3 = (f32[1,32,128]{2,1,0:T(8,128)S(1)}, f32[1,32,128]{2,1,0:T(8,128)S(1)}, u32[]{:S(2)}, u32[]{:S(2)}) collective-permute-start(f32[1,32,128]{2,1,0:T(8,128)S(1)} %get-tuple-element.48), channel_id=1, source_target_pairs={{0,8},{8,16},{16,24},{24,32},{32,40},{40,48},{48,56},{56,64},{64,7... | collective-permute-start | bytes 49160 | tf_op jit(solution)/shard_map/ppermute | solution.py:18
  56.5 41.2 %collective-permute-start.1 = (f32[1,32,128]{2,1,0:T(8,128)S(1)}, f32[1,32,128]{2,1,0:T(8,128)S(1)}, u32[]{:S(2)}, u32[]{:S(2)}) collective-permute-start(f32[1,32,128]{2,1,0:T(8,128)S(1)} %get-tuple-element.47), channel_id=1, source_target_pairs={{8,0},{16,8},{24,16},{32,24},{40,32},{48,40},{56,48},{64,56},{72,6... | collective-permute-start | bytes 49160 | tf_op jit(solution)/shard_map/ppermute | solution.py:19
  83.1 23.4 %all-to-all-start.1 = ((bf16[96,2,256]{2,1,0:T(2,128)(2,1)}), bf16[96,2,256]{2,1,0:T(2,128)(2,1)S(1)}, u32[]{:S(2)}, u32[]{:S(2)}) async-start(bf16[96,2,256]{2,1,0:T(2,128)(2,1)} %reshape.288), calls=%async_computation.1 | async-start | bytes 196608 | tf_op jit(solution)/shard_map/all_to_all | solution.py:55
  90.6 14.3 %collective-permute-start.4 = (f32[34,1,128]{2,1,0:T(1,128)S(1)}, f32[34,1,128]{2,1,0:T(1,128)S(1)}, u32[]{:S(2)}, u32[]{:S(2)}) collective-permute-start(f32[34,1,128]{2,1,0:T(1,128)S(1)} %get-tuple-element.28), channel_id=1, source_target_pairs={{1,0},{2,1},{3,2},{4,3},{5,4},{6,5},{7,6},{9,8},{10,9},{11,10},{12... | collective-permute-start | bytes 52232 | tf_op jit(solution)/shard_map/ppermute | solution.py:19
  93.1 11.8 %collective-permute-start.6 = (f32[34,1,128]{2,1,0:T(1,128)S(1)}, f32[34,1,128]{2,1,0:T(1,128)S(1)}, u32[]{:S(2)}, u32[]{:S(2)}) collective-permute-start(f32[34,1,128]{2,1,0:T(1,128)S(1)} %get-tuple-element.27), channel_id=1, source_target_pairs={{0,1},{1,2},{2,3},{3,4},{4,5},{5,6},{6,7},{8,9},{9,10},{10,11},{11... | collective-permute-start | bytes 52232 | tf_op jit(solution)/shard_map/ppermute | solution.py:18
  97.7 45.6 %copy-start.15 = (f32[34,32,128]{2,1,0:T(8,128)}, f32[34,32,128]{2,1,0:T(8,128)S(1)}, u32[]{:S(2)}) copy-start(f32[34,32,128]{2,1,0:T(8,128)S(1)} %constant_dynamic-update-slice_fusion) | copy-start | bytes 1671172
  97.8 45.6 %collective-permute-start.5 = (f32[34,1,128]{2,1,0:T(1,128)S(1)}, f32[34,1,128]{2,1,0:T(1,128)S(1)}, u32[]{:S(2)}, u32[]{:S(2)}) collective-permute-start(f32[34,1,128]{2,1,0:T(1,128)S(1)} %get-tuple-element.30), channel_id=1, source_target_pairs={{1,0},{2,1},{3,2},{4,3},{5,4},{6,5},{7,6},{9,8},{10,9},{11,10},{12... | collective-permute-start | bytes 52232 | tf_op jit(solution)/shard_map/ppermute | solution.py:19
  99.7 43.6 %collective-permute-start.7 = (f32[34,1,128]{2,1,0:T(1,128)S(1)}, f32[34,1,128]{2,1,0:T(1,128)S(1)}, u32[]{:S(2)}, u32[]{:S(2)}) collective-permute-start(f32[34,1,128]{2,1,0:T(1,128)S(1)} %get-tuple-element.29), channel_id=1, source_target_pairs={{0,1},{1,2},{2,3},{3,4},{4,5},{5,6},{6,7},{8,9},{9,10},{10,11},{11... | collective-permute-start | bytes 52232 | tf_op jit(solution)/shard_map/ppermute | solution.py:18
  138.2 9.7 %all-to-all-start.2 = ((f32[8,1,512]{2,1,0:T(1,128)}), f32[8,1,512]{2,1,0:T(1,128)S(1)}, u32[]{:S(2)}, u32[]{:S(2)}) async-start(f32[8,1,512]{2,1,0:T(1,128)} %reshape.290), calls=%async_computation.2 | async-start | bytes 32768 | tf_op jit(solution)/shard_map/all_to_all | solution.py:70
  156.6 4.3 %collective-permute-start.8 = (f32[1,32,128]{2,1,0:T(8,128)S(1)}, f32[1,32,128]{2,1,0:T(8,128)S(1)}, u32[]{:S(2)}, u32[]{:S(2)}) collective-permute-start(f32[1,32,128]{2,1,0:T(8,128)S(1)} %get-tuple-element.44), channel_id=1, source_target_pairs={{8,0},{16,8},{24,16},{32,24},{40,32},{48,40},{56,48},{64,56},{72,6... | collective-permute-start | bytes 49160 | tf_op jit(solution)/shard_map/ppermute | solution.py:19
  158.7 7.2 %collective-permute-start.9 = (f32[1,32,128]{2,1,0:T(8,128)S(1)}, f32[1,32,128]{2,1,0:T(8,128)S(1)}, u32[]{:S(2)}, u32[]{:S(2)}) collective-permute-start(f32[1,32,128]{2,1,0:T(8,128)S(1)} %get-tuple-element.43), channel_id=1, source_target_pairs={{0,8},{8,16},{16,24},{24,32},{32,40},{40,48},{48,56},{56,64},{64,7... | collective-permute-start | bytes 49160 | tf_op jit(solution)/shard_map/ppermute | solution.py:18
  165.9 11.2 %collective-permute-start.10 = (f32[34,1,128]{2,1,0:T(1,128)S(1)}, f32[34,1,128]{2,1,0:T(1,128)S(1)}, u32[]{:S(2)}, u32[]{:S(2)}) collective-permute-start(f32[34,1,128]{2,1,0:T(1,128)S(1)} %get-tuple-element.26), channel_id=1, source_target_pairs={{1,0},{2,1},{3,2},{4,3},{5,4},{6,5},{7,6},{9,8},{10,9},{11,10},{12... | collective-permute-start | bytes 52232 | tf_op jit(solution)/shard_map/ppermute | solution.py:19
  169.2 7.9 %collective-permute-start.11 = (f32[34,1,128]{2,1,0:T(1,128)S(1)}, f32[34,1,128]{2,1,0:T(1,128)S(1)}, u32[]{:S(2)}, u32[]{:S(2)}) collective-permute-start(f32[34,1,128]{2,1,0:T(1,128)S(1)} %get-tuple-element.25), channel_id=1, source_target_pairs={{0,1},{1,2},{2,3},{3,4},{4,5},{5,6},{6,7},{8,9},{9,10},{10,11},{11... | collective-permute-start | bytes 52232 | tf_op jit(solution)/shard_map/ppermute | solution.py:18
  177.1 1.0 copy-start.16
  179.0 4.3 %collective-permute-start.12 = (f32[1,32,128]{2,1,0:T(8,128)S(1)}, f32[1,32,128]{2,1,0:T(8,128)S(1)}, u32[]{:S(2)}, u32[]{:S(2)}) collective-permute-start(f32[1,32,128]{2,1,0:T(8,128)S(1)} %get-tuple-element.42), channel_id=1, source_target_pairs={{8,0},{16,8},{24,16},{32,24},{40,32},{48,40},{56,48},{64,56},{72,6... | collective-permute-start | bytes 49160 | tf_op jit(solution)/shard_map/ppermute | solution.py:19
  180.9 7.2 %collective-permute-start.13 = (f32[1,32,128]{2,1,0:T(8,128)S(1)}, f32[1,32,128]{2,1,0:T(8,128)S(1)}, u32[]{:S(2)}, u32[]{:S(2)}) collective-permute-start(f32[1,32,128]{2,1,0:T(8,128)S(1)} %get-tuple-element.41), channel_id=1, source_target_pairs={{0,8},{8,16},{16,24},{24,32},{32,40},{40,48},{48,56},{56,64},{64,7... | collective-permute-start | bytes 49160 | tf_op jit(solution)/shard_map/ppermute | solution.py:18
  188.1 11.2 %collective-permute-start.14 = (f32[34,1,128]{2,1,0:T(1,128)S(1)}, f32[34,1,128]{2,1,0:T(1,128)S(1)}, u32[]{:S(2)}, u32[]{:S(2)}) collective-permute-start(f32[34,1,128]{2,1,0:T(1,128)S(1)} %get-tuple-element.24), channel_id=1, source_target_pairs={{1,0},{2,1},{3,2},{4,3},{5,4},{6,5},{7,6},{9,8},{10,9},{11,10},{12... | collective-permute-start | bytes 52232 | tf_op jit(solution)/shard_map/ppermute | solution.py:19
  190.2 9.1 %collective-permute-start.15 = (f32[34,1,128]{2,1,0:T(1,128)S(1)}, f32[34,1,128]{2,1,0:T(1,128)S(1)}, u32[]{:S(2)}, u32[]{:S(2)}) collective-permute-start(f32[34,1,128]{2,1,0:T(1,128)S(1)} %get-tuple-element.23), channel_id=1, source_target_pairs={{0,1},{1,2},{2,3},{3,4},{4,5},{5,6},{6,7},{8,9},{9,10},{10,11},{11... | collective-permute-start | bytes 52232 | tf_op jit(solution)/shard_map/ppermute | solution.py:18
  199.3 1.0 copy-start.14
  199.9 1.3 copy-start.6
  201.2 20.9 %copy-start = (f32[32,32,128]{2,1,0:T(8,128)}, f32[32,32,128]{2,1,0:T(8,128)S(1)}, u32[]{:S(2)}) copy-start(f32[32,32,128]{2,1,0:T(8,128)S(1)} %fusion.95) | copy-start | bytes 1572868
  201.3 4.3 %collective-permute-start.16 = (f32[1,32,128]{2,1,0:T(8,128)S(1)}, f32[1,32,128]{2,1,0:T(8,128)S(1)}, u32[]{:S(2)}, u32[]{:S(2)}) collective-permute-start(f32[1,32,128]{2,1,0:T(8,128)S(1)} %get-tuple-element.40), channel_id=1, source_target_pairs={{8,0},{16,8},{24,16},{32,24},{40,32},{48,40},{56,48},{64,56},{72,6... | collective-permute-start | bytes 49160 | tf_op jit(solution)/shard_map/ppermute | solution.py:19
  203.2 7.2 %collective-permute-start.17 = (f32[1,32,128]{2,1,0:T(8,128)S(1)}, f32[1,32,128]{2,1,0:T(8,128)S(1)}, u32[]{:S(2)}, u32[]{:S(2)}) collective-permute-start(f32[1,32,128]{2,1,0:T(8,128)S(1)} %get-tuple-element.39), channel_id=1, source_target_pairs={{0,8},{8,16},{16,24},{24,32},{32,40},{40,48},{48,56},{56,64},{64,7... | collective-permute-start | bytes 49160 | tf_op jit(solution)/shard_map/ppermute | solution.py:18
  210.4 11.2 %collective-permute-start.18 = (f32[34,1,128]{2,1,0:T(1,128)S(1)}, f32[34,1,128]{2,1,0:T(1,128)S(1)}, u32[]{:S(2)}, u32[]{:S(2)}) collective-permute-start(f32[34,1,128]{2,1,0:T(1,128)S(1)} %get-tuple-element.22), channel_id=1, source_target_pairs={{1,0},{2,1},{3,2},{4,3},{5,4},{6,5},{7,6},{9,8},{10,9},{11,10},{12... | collective-permute-start | bytes 52232 | tf_op jit(solution)/shard_map/ppermute | solution.py:19
  212.3 9.3 %collective-permute-start.19 = (f32[34,1,128]{2,1,0:T(1,128)S(1)}, f32[34,1,128]{2,1,0:T(1,128)S(1)}, u32[]{:S(2)}, u32[]{:S(2)}) collective-permute-start(f32[34,1,128]{2,1,0:T(1,128)S(1)} %get-tuple-element.21), channel_id=1, source_target_pairs={{0,1},{1,2},{2,3},{3,4},{4,5},{5,6},{6,7},{8,9},{9,10},{10,11},{11... | collective-permute-start | bytes 52232 | tf_op jit(solution)/shard_map/ppermute | solution.py:18
  221.6 1.0 copy-start.12
  222.2 1.3 copy-start.4
  223.5 9.1 %copy-start.8 = (f32[32,32,128]{2,1,0:T(8,128)}, f32[32,32,128]{2,1,0:T(8,128)S(1)}, u32[]{:S(2)}) copy-start(f32[32,32,128]{2,1,0:T(8,128)S(1)} %fusion.77) | copy-start | bytes 1572868
  223.5 4.3 %collective-permute-start.20 = (f32[1,32,128]{2,1,0:T(8,128)S(1)}, f32[1,32,128]{2,1,0:T(8,128)S(1)}, u32[]{:S(2)}, u32[]{:S(2)}) collective-permute-start(f32[1,32,128]{2,1,0:T(8,128)S(1)} %get-tuple-element.38), channel_id=1, source_target_pairs={{8,0},{16,8},{24,16},{32,24},{40,32},{48,40},{56,48},{64,56},{72,6... | collective-permute-start | bytes 49160 | tf_op jit(solution)/shard_map/ppermute | solution.py:19
  225.4 7.2 %collective-permute-start.21 = (f32[1,32,128]{2,1,0:T(8,128)S(1)}, f32[1,32,128]{2,1,0:T(8,128)S(1)}, u32[]{:S(2)}, u32[]{:S(2)}) collective-permute-start(f32[1,32,128]{2,1,0:T(8,128)S(1)} %get-tuple-element.37), channel_id=1, source_target_pairs={{0,8},{8,16},{16,24},{24,32},{32,40},{40,48},{48,56},{56,64},{64,7... | collective-permute-start | bytes 49160 | tf_op jit(solution)/shard_map/ppermute | solution.py:18
  232.6 11.2 %collective-permute-start.22 = (f32[34,1,128]{2,1,0:T(1,128)S(1)}, f32[34,1,128]{2,1,0:T(1,128)S(1)}, u32[]{:S(2)}, u32[]{:S(2)}) collective-permute-start(f32[34,1,128]{2,1,0:T(1,128)S(1)} %get-tuple-element.20), channel_id=1, source_target_pairs={{1,0},{2,1},{3,2},{4,3},{5,4},{6,5},{7,6},{9,8},{10,9},{11,10},{12... | collective-permute-start | bytes 52232 | tf_op jit(solution)/shard_map/ppermute | solution.py:19
  234.6 9.3 %collective-permute-start.23 = (f32[34,1,128]{2,1,0:T(1,128)S(1)}, f32[34,1,128]{2,1,0:T(1,128)S(1)}, u32[]{:S(2)}, u32[]{:S(2)}) collective-permute-start(f32[34,1,128]{2,1,0:T(1,128)S(1)} %get-tuple-element.19), channel_id=1, source_target_pairs={{0,1},{1,2},{2,3},{3,4},{4,5},{5,6},{6,7},{8,9},{9,10},{10,11},{11... | collective-permute-start | bytes 52232 | tf_op jit(solution)/shard_map/ppermute | solution.py:18
  243.8 1.8 copy-start.7
  243.8 1.8 copy-start.9
  249.7 4.3 %collective-permute-start.24 = (f32[1,32,128]{2,1,0:T(8,128)S(1)}, f32[1,32,128]{2,1,0:T(8,128)S(1)}, u32[]{:S(2)}, u32[]{:S(2)}) collective-permute-start(f32[1,32,128]{2,1,0:T(8,128)S(1)} %get-tuple-element.36), channel_id=1, source_target_pairs={{8,0},{16,8},{24,16},{32,24},{40,32},{48,40},{56,48},{64,56},{72,6... | collective-permute-start | bytes 49160 | tf_op jit(solution)/shard_map/ppermute | solution.py:19
  251.6 7.2 %collective-permute-start.25 = (f32[1,32,128]{2,1,0:T(8,128)S(1)}, f32[1,32,128]{2,1,0:T(8,128)S(1)}, u32[]{:S(2)}, u32[]{:S(2)}) collective-permute-start(f32[1,32,128]{2,1,0:T(8,128)S(1)} %get-tuple-element.35), channel_id=1, source_target_pairs={{0,8},{8,16},{16,24},{24,32},{32,40},{40,48},{48,56},{56,64},{64,7... | collective-permute-start | bytes 49160 | tf_op jit(solution)/shard_map/ppermute | solution.py:18
  258.8 11.9 %copy-start.1 = (f32[32,32,128]{2,1,0:T(8,128)S(1)}, f32[32,32,128]{2,1,0:T(8,128)}, u32[]{:S(2)}) copy-start(f32[32,32,128]{2,1,0:T(8,128)} %copy-done) | copy-start | bytes 1572868
  258.8 11.3 %collective-permute-start.26 = (f32[34,1,128]{2,1,0:T(1,128)S(1)}, f32[34,1,128]{2,1,0:T(1,128)S(1)}, u32[]{:S(2)}, u32[]{:S(2)}) collective-permute-start(f32[34,1,128]{2,1,0:T(1,128)S(1)} %get-tuple-element.18), channel_id=1, source_target_pairs={{1,0},{2,1},{3,2},{4,3},{5,4},{6,5},{7,6},{9,8},{10,9},{11,10},{12... | collective-permute-start | bytes 52232 | tf_op jit(solution)/shard_map/ppermute | solution.py:19
  260.9 9.3 %collective-permute-start.27 = (f32[34,1,128]{2,1,0:T(1,128)S(1)}, f32[34,1,128]{2,1,0:T(1,128)S(1)}, u32[]{:S(2)}, u32[]{:S(2)}) collective-permute-start(f32[34,1,128]{2,1,0:T(1,128)S(1)} %get-tuple-element.17), channel_id=1, source_target_pairs={{0,1},{1,2},{2,3},{3,4},{4,5},{5,6},{6,7},{8,9},{9,10},{10,11},{11... | collective-permute-start | bytes 52232 | tf_op jit(solution)/shard_map/ppermute | solution.py:18
  270.1 1.3 copy-start.5
  270.1 1.5 copy-start.13
  275.5 9.1 %copy-start.2 = (f32[32,32,128]{2,1,0:T(8,128)}, f32[32,32,128]{2,1,0:T(8,128)S(1)}, u32[]{:S(2)}) copy-start(f32[32,32,128]{2,1,0:T(8,128)S(1)} %fusion.41) | copy-start | bytes 1572868
  275.5 4.3 %collective-permute-start.28 = (f32[1,32,128]{2,1,0:T(8,128)S(1)}, f32[1,32,128]{2,1,0:T(8,128)S(1)}, u32[]{:S(2)}, u32[]{:S(2)}) collective-permute-start(f32[1,32,128]{2,1,0:T(8,128)S(1)} %get-tuple-element.34), channel_id=1, source_target_pairs={{8,0},{16,8},{24,16},{32,24},{40,32},{48,40},{56,48},{64,56},{72,6... | collective-permute-start | bytes 49160 | tf_op jit(solution)/shard_map/ppermute | solution.py:19
  277.4 7.2 %collective-permute-start.29 = (f32[1,32,128]{2,1,0:T(8,128)S(1)}, f32[1,32,128]{2,1,0:T(8,128)S(1)}, u32[]{:S(2)}, u32[]{:S(2)}) collective-permute-start(f32[1,32,128]{2,1,0:T(8,128)S(1)} %get-tuple-element.33), channel_id=1, source_target_pairs={{0,8},{8,16},{16,24},{24,32},{32,40},{40,48},{48,56},{56,64},{64,7... | collective-permute-start | bytes 49160 | tf_op jit(solution)/shard_map/ppermute | solution.py:18
  284.6 13.0 %copy-start.3 = (f32[32,32,128]{2,1,0:T(8,128)S(1)}, f32[32,32,128]{2,1,0:T(8,128)}, u32[]{:S(2)}) copy-start(f32[32,32,128]{2,1,0:T(8,128)} %copy-done.2) | copy-start | bytes 1572868
  284.7 11.3 %collective-permute-start.30 = (f32[34,1,128]{2,1,0:T(1,128)S(1)}, f32[34,1,128]{2,1,0:T(1,128)S(1)}, u32[]{:S(2)}, u32[]{:S(2)}) collective-permute-start(f32[34,1,128]{2,1,0:T(1,128)S(1)} %get-tuple-element.16), channel_id=1, source_target_pairs={{1,0},{2,1},{3,2},{4,3},{5,4},{6,5},{7,6},{9,8},{10,9},{11,10},{12... | collective-permute-start | bytes 52232 | tf_op jit(solution)/shard_map/ppermute | solution.py:19
  286.7 9.3 %collective-permute-start.31 = (f32[34,1,128]{2,1,0:T(1,128)S(1)}, f32[34,1,128]{2,1,0:T(1,128)S(1)}, u32[]{:S(2)}, u32[]{:S(2)}) collective-permute-start(f32[34,1,128]{2,1,0:T(1,128)S(1)} %get-tuple-element.15), channel_id=1, source_target_pairs={{0,1},{1,2},{2,3},{3,4},{4,5},{5,6},{6,7},{8,9},{9,10},{10,11},{11... | collective-permute-start | bytes 52232 | tf_op jit(solution)/shard_map/ppermute | solution.py:18
  296.0 1.7 copy-start.17
  298.6 20.3 %copy-start.10 = (f32[32,32,128]{2,1,0:T(8,128)}, f32[32,32,128]{2,1,0:T(8,128)S(1)}, u32[]{:S(2)}) copy-start(f32[32,32,128]{2,1,0:T(8,128)S(1)} %fusion.23) | copy-start | bytes 1572868
  298.6 4.3 %collective-permute-start.32 = (f32[1,32,128]{2,1,0:T(8,128)S(1)}, f32[1,32,128]{2,1,0:T(8,128)S(1)}, u32[]{:S(2)}, u32[]{:S(2)}) collective-permute-start(f32[1,32,128]{2,1,0:T(8,128)S(1)} %get-tuple-element.32), channel_id=1, source_target_pairs={{8,0},{16,8},{24,16},{32,24},{40,32},{48,40},{56,48},{64,56},{72,6... | collective-permute-start | bytes 49160 | tf_op jit(solution)/shard_map/ppermute | solution.py:19
  300.5 7.2 %collective-permute-start.33 = (f32[1,32,128]{2,1,0:T(8,128)S(1)}, f32[1,32,128]{2,1,0:T(8,128)S(1)}, u32[]{:S(2)}, u32[]{:S(2)}) collective-permute-start(f32[1,32,128]{2,1,0:T(8,128)S(1)} %get-tuple-element.31), channel_id=1, source_target_pairs={{0,8},{8,16},{16,24},{24,32},{32,40},{40,48},{48,56},{56,64},{64,7... | collective-permute-start | bytes 49160 | tf_op jit(solution)/shard_map/ppermute | solution.py:18
  307.7 10.5 %collective-permute-start.34 = (f32[34,1,128]{2,1,0:T(1,128)S(1)}, f32[34,1,128]{2,1,0:T(1,128)S(1)}, u32[]{:S(2)}, u32[]{:S(2)}) collective-permute-start(f32[34,1,128]{2,1,0:T(1,128)S(1)} %get-tuple-element.14), channel_id=1, source_target_pairs={{1,0},{2,1},{3,2},{4,3},{5,4},{6,5},{7,6},{9,8},{10,9},{11,10},{12... | collective-permute-start | bytes 52232 | tf_op jit(solution)/shard_map/ppermute | solution.py:19
  309.6 8.6 %collective-permute-start.35 = (f32[34,1,128]{2,1,0:T(1,128)S(1)}, f32[34,1,128]{2,1,0:T(1,128)S(1)}, u32[]{:S(2)}, u32[]{:S(2)}) collective-permute-start(f32[34,1,128]{2,1,0:T(1,128)S(1)} %get-tuple-element.13), channel_id=1, source_target_pairs={{0,1},{1,2},{2,3},{3,4},{4,5},{5,6},{6,7},{8,9},{9,10},{10,11},{11... | collective-permute-start | bytes 52232 | tf_op jit(solution)/shard_map/ppermute | solution.py:18
where the time goes:
time: 323 us; the launch traced here: 321 us
  starting transfers between devices  136 us (42%)
  local copies, waits for them, and re-layouts  78.4 us (24%)
  other arithmetic  67.5 us (21%)
  waiting for transfers between devices  36.3 us (11%)
    ppermute x18, starting transfers between devices, extended(): before = lax.ppermute(last, axis, up)  64.6 us
    ppermute x18, starting transfers between devices, extended(): after = lax.ppermute(leading, axis, down)  53.3 us
    unnamed x49, local copies, waits for them, and re-layouts  38.3 us
    ppermute x18, waiting for transfers between devices, extended(): before = lax.ppermute(last, axis, up)  33.4 us
    scatter-add x8, other arithmetic, shards(): drive = jnp.zeros((cells,), jnp.float32).at[cells_in].add(force_in[step],...  31.2 us
    scatter x1, local copies, waits for them, and re-layouts, shards(): jnp.full((tiles_y, capacity), cells, jnp.int32).at[owner_row, slot]  19.9 us
    add x8, other arithmetic, shards(): new = 2.0 * now - before + 0.15 * stiffness(u_pad, mu_pad) + drive  16.7 us
    concatenate x17, other arithmetic, extended(): array = jnp.concatenate([before, array, after], axis=dim)  9.93 us
  transfers between devices with their start and end apart: 39, of which 8 were waited for; matrix products, arithmetic and copies ran while one was open for 34% of the time, Pallas kernels for 0%

commit v1 on v0

v1 whole, which is shorter than its diff:
```python
import math

import jax
import jax.numpy as jnp
import ml_dtypes
import numpy as np
from jax import lax
from jax.experimental import pallas as pl
from jax.experimental.pallas import tpu as pltpu
from jax.sharding import PartitionSpec as P

STEPS = 8
H = 8
CX, CY, CZ = 32, 32, 128
EX, EY = CX + 2 * H, CY + 2 * H
PY = EY + 2 * H
ROWS = EX * EY
CELLS = CX * CY * CZ
NPT = 128
ROW_BITS, Z_BITS, P_BITS = 12, 7, 12
LIMIT = 56 * 1024 * 1024


def vmem_spec():
    return pl.BlockSpec(memory_space=pltpu.VMEM)


def any_spec():
    return pl.BlockSpec(memory_space=pl.ANY)


def split_table(sources, local_freqs):
    total = sources * local_freqs
    freq = np.arange(total, dtype=np.float64).reshape(sources, 1, local_freqs)
    times = np.arange(STEPS, dtype=np.float64).reshape(STEPS, 1, 1, 1)
    phase = math.pi * times * freq[None] / total
    table = np.concatenate([np.cos(phase), -np.sin(phase)], axis=2) / math.sqrt(total)
    rest = table.reshape(STEPS, 2 * total).astype(np.float32)
    parts = []
    for _ in range(3):
        part = rest.astype(ml_dtypes.bfloat16)
        parts.append(part)
        rest = rest - part.astype(np.float32)
    return np.concatenate(parts, axis=0)


def deal_kernel(fk_ref, out_ref):
    for i in range(out_ref.shape[0]):
        for c in range(2):
            out_ref[i, pl.ds(2 * c, 2), :] = fk_ref[c, :, pl.ds(i * NPT, NPT)]


def transform_kernel(moved_ref, table_ref, owner_ref, cell_ref, out_ref, wide_ref):
    for i in range(moved_ref.shape[0]):
        wide_ref[pl.ds(4 * i, 4), :] = moved_ref[i].astype(jnp.float32)
    panel = wide_ref[...].astype(jnp.bfloat16)
    parts = jnp.dot(table_ref[...], panel, preferred_element_type=jnp.float32)
    force = parts[0:8] + parts[8:16] + parts[16:24]
    key = (owner_ref[...] * CELLS + cell_ref[...] + 1).astype(jnp.float32)
    keys = jnp.broadcast_to(key, (8, NPT))
    for a in range(out_ref.shape[0]):
        out_ref[a, 0:8, :] = force
        out_ref[a, 8:16, :] = keys


def window_kernel(place_ref, now_hbm, before_hbm, mod_hbm, xlo_hbm, xhi_hbm, ylo_hbm, yhi_hbm,
                  fl_ref, fc_ref, fr_ref, next_hbm, prior_hbm,
                  a_ref, b_ref, m_ref, kx_ref, ky_ref, kz_ref, kc_ref, d_ref, code_ref, code_smem, list_smem,
                  sems, sem_code, sem_out):
    tiles = fc_ref.shape[0]
    copies = []
    for k, (own, ext) in enumerate(((now_hbm, a_ref), (before_hbm, b_ref), (mod_hbm, m_ref))):
        pieces = (
            (own, ext.at[pl.ds(H, CX), pl.ds(2 * H, CY)]),
            (xlo_hbm.at[pl.ds(k * H, H)], ext.at[pl.ds(0, H), pl.ds(2 * H, CY)]),
            (xhi_hbm.at[pl.ds(k * H, H)], ext.at[pl.ds(H + CX, H), pl.ds(2 * H, CY)]),
            (ylo_hbm.at[pl.ds(k * EX, EX)], ext.at[:, pl.ds(H, H)]),
            (yhi_hbm.at[pl.ds(k * EX, EX)], ext.at[:, pl.ds(2 * H + CY, H)]),
        )
        for n, (src, dst) in enumerate(pieces):
            copies.append(pltpu.make_async_copy(src, dst, sems.at[k, n]))
    for c in copies:
        c.start()

    my_y = place_ref[0]
    lane = lax.broadcasted_iota(jnp.int32, (tiles, NPT), 1)
    part = lax.broadcasted_iota(jnp.int32, (tiles, NPT), 0)
    for side, f_ref in enumerate((fl_ref, fc_ref, fr_ref)):
        key = f_ref[:, 8, :].astype(jnp.int32) - 1
        own = key >> 17
        cell = key & (CELLS - 1)
        gx = (cell >> 12) + (side - 1) * CX + H
        gy = (own - my_y) * CY + ((cell >> 7) & (CY - 1)) + H
        inside = (key >= 0) & (gx >= 1) & (gx < EX - 1) & (gy >= 1) & (gy < EY - 1)
        row = gx * EY + gy
        place = (side * tiles + part) * NPT + lane
        packed = (row << (Z_BITS + P_BITS)) | ((cell & (CZ - 1)) << P_BITS) | place
        code_ref[pl.ds(side * tiles, tiles), :] = jnp.where(inside, packed, -1)
    code_copy = pltpu.make_async_copy(code_ref, code_smem, sem_code)
    code_copy.start()

    def clear(i, _):
        base = pl.multiple_of(i * 64, 64)
        for j in range(8):
            d_ref[pl.ds(base + 8 * j, 8), :] = jnp.zeros((8, CZ), jnp.float32)
        return 0

    lax.fori_loop(0, ROWS * STEPS // 64, clear, 0)
    code_copy.wait()

    def pick_row(r, count):
        for c in range(NPT):
            code = code_smem[r, c]
            list_smem[count] = code
            count = count + jnp.where(code >= 0, 1, 0)
        return count

    count = lax.fori_loop(0, 3 * tiles, pick_row, 0)
    for j in range(4):
        list_smem[count + j] = 0

    zline = lax.broadcasted_iota(jnp.int32, (STEPS, CZ), 1)

    def put(f_ref, tile, code):
        place = code & ((1 << P_BITS) - 1)
        z = (code >> P_BITS) & (CZ - 1)
        row = code >> (Z_BITS + P_BITS)
        force = f_ref[tile, 0:8, :]
        column = jnp.take_along_axis(force, jnp.full((STEPS, CZ), place & (NPT - 1), jnp.int32), axis=1)
        at = pl.ds(pl.multiple_of(row * STEPS, STEPS), STEPS)
        d_ref[at, :] = d_ref[at, :] + jnp.where(zline == z, column, 0.0)

    def add_point(i, _):
        for j in range(4):
            code = list_smem[4 * i + j]
            tile = (code & ((1 << P_BITS) - 1)) >> 7
            put(f_all, tile, code)
        return 0

    f_all = kc_ref
    for side, f_ref in enumerate((fl_ref, fc_ref, fr_ref)):
        for a in range(tiles):
            kc_ref[side * tiles + a, 0:8, :] = f_ref[a, 0:8, :]
    lax.fori_loop(0, (count + 3) // 4, add_point, 0)

    for c in copies:
        c.wait()

    zpos = lax.broadcasted_iota(jnp.int32, (8, CZ), 1)

    def face(c, n):
        return jnp.where(jnp.minimum(c, n) > 0.0, 0.075 * (c + n), 0.0)

    def coefficients(x, _):
        for j in range(EY // 8):
            y = H + 8 * j
            c = m_ref[x, pl.ds(y, 8), :]
            xp = m_ref[x + 1, pl.ds(y, 8), :]
            xm = m_ref[jnp.maximum(x - 1, 0), pl.ds(y, 8), :]
            yp = m_ref[x, pl.ds(y + 1, 8), :]
            ym = m_ref[x, pl.ds(y - 1, 8), :]
            zp = jnp.where(zpos == CZ - 1, 0.0, pltpu.roll(c, CZ - 1, 1))
            zm = jnp.where(zpos == 0, 0.0, pltpu.roll(c, 1, 1))
            kx_ref[x, pl.ds(y, 8), :] = face(c, xp)
            ky_ref[x, pl.ds(y, 8), :] = face(c, yp)
            kz_ref[x, pl.ds(y, 8), :] = face(c, zp)
            kc_ref[x, pl.ds(y, 8), :] = 2.0 - 0.075 * (6.0 * c + ((xp + xm) + (yp + ym) + (zp + zm)))
        return 0

    lax.fori_loop(0, EX - 1, coefficients, 0)

    for step in range(STEPS):
        u_ref, w_ref = (a_ref, b_ref) if step % 2 == 0 else (b_ref, a_ref)

        def advance(x, _, u_ref=u_ref, w_ref=w_ref, step=step):
            for j in range(EY // 8):
                y = H + 8 * j
                u = u_ref[x, pl.ds(y, 8), :]
                kz = kz_ref[x, pl.ds(y, 8), :]
                in_x = (kx_ref[x, pl.ds(y, 8), :] * u_ref[x + 1, pl.ds(y, 8), :]
                        + kx_ref[x - 1, pl.ds(y, 8), :] * u_ref[x - 1, pl.ds(y, 8), :])
                in_y = (ky_ref[x, pl.ds(y, 8), :] * u_ref[x, pl.ds(y + 1, 8), :]
                        + ky_ref[x, pl.ds(y - 1, 8), :] * u_ref[x, pl.ds(y - 1, 8), :])
                in_z = kz * pltpu.roll(u, CZ - 1, 1) + pltpu.roll(kz * u, 1, 1)
                drive = d_ref[pl.ds((x * EY + 8 * j) * STEPS + step, 8, stride=STEPS), :]
                own = kc_ref[x, pl.ds(y, 8), :] * u - w_ref[x, pl.ds(y, 8), :]
                w_ref[x, pl.ds(y, 8), :] = (own + drive) + ((in_x + in_y) + in_z)
            return 0

        lax.fori_loop(step + 1, EX - step - 1, advance, 0)

    outs = [
        pltpu.make_async_copy(ref.at[pl.ds(H, CX), pl.ds(2 * H, CY)], hbm, sem_out.at[n])
        for n, (ref, hbm) in enumerate(((a_ref, next_hbm), (b_ref, prior_hbm)))
    ]
    for c in outs:
        c.start()
    for c in outs:
        c.wait()


def window(place, fields, forces):
    tiles = forces[0].shape[0]
    grid = jax.ShapeDtypeStruct((CX, CY, CZ), jnp.float32)
    buffer = pltpu.VMEM((EX, PY, CZ), jnp.float32)
    return pl.pallas_call(
        window_kernel,
        out_shape=(grid, grid),
        in_specs=[pl.BlockSpec(memory_space=pltpu.SMEM)] + [any_spec()] * 7 + [vmem_spec()] * 3,
        out_specs=(any_spec(), any_spec()),
        scratch_shapes=[buffer] * 7 + [
            pltpu.VMEM((ROWS * STEPS, CZ), jnp.float32),
            pltpu.VMEM((3 * tiles, NPT), jnp.int32),
            pltpu.SMEM((3 * tiles, NPT), jnp.int32),
            pltpu.SMEM((3 * tiles * NPT + 8,), jnp.int32),
            pltpu.SemaphoreType.DMA((3, 5)),
            pltpu.SemaphoreType.DMA,
            pltpu.SemaphoreType.DMA((2,)),
        ],
        compiler_params=pltpu.CompilerParams(vmem_limit_bytes=LIMIT),
    )(place, *fields, *forces)


def neighbours(low, high, axis):
    count = lax.axis_size(axis)
    up = [(i, i + 1) for i in range(count - 1)]
    down = [(i + 1, i) for i in range(count - 1)]
    return lax.ppermute(high, axis, up), lax.ppermute(low, axis, down)


def shards(field_now, field_before, layer, modulus_table, fk_panel, owner, local_cell):
    sources, tiles = lax.axis_size("along"), lax.axis_size("across")
    local_freqs = fk_panel.shape[1]
    modulus = jnp.zeros(field_now.shape, jnp.float32)
    for level in range(modulus_table.shape[0]):
        modulus = modulus + jnp.where(layer == level, modulus_table[level], 0.0)
    arrays = (field_now, field_before, modulus)

    dealt = pl.pallas_call(
        deal_kernel,
        out_shape=jax.ShapeDtypeStruct((sources, 2 * local_freqs, NPT), jnp.bfloat16),
        in_specs=[vmem_spec()],
        out_specs=vmem_spec(),
    )(fk_panel.reshape(2, local_freqs, sources * NPT))

    xlo, xhi = neighbours(
        jnp.concatenate([a[:H] for a in arrays], axis=0),
        jnp.concatenate([a[-H:] for a in arrays], axis=0),
        "along",
    )
    moved = lax.all_to_all(dealt, "along", 0, 0, tiled=True)

    def side(rows):
        return jnp.concatenate(
            [p[:, rows] for k, a in enumerate(arrays) for p in (xlo[k * H:k * H + H], a, xhi[k * H:k * H + H])],
            axis=0,
        )

    ylo, yhi = neighbours(side(slice(0, H)), side(slice(CY - H, CY)), "across")

    payload = pl.pallas_call(
        transform_kernel,
        out_shape=jax.ShapeDtypeStruct((tiles, 16, NPT), jnp.float32),
        in_specs=[vmem_spec()] * 4,
        out_specs=vmem_spec(),
        scratch_shapes=[pltpu.VMEM((2 * local_freqs * sources, NPT), jnp.float32)],
    )(moved, jnp.asarray(split_table(sources, local_freqs)), owner.reshape(1, NPT), local_cell)
    center = lax.all_to_all(payload, "across", 0, 0, tiled=True)
    left, right = neighbours(center, center, "along")
    place = lax.axis_index("across").astype(jnp.int32).reshape(1)
    return window(place, (*arrays, xlo, xhi, ylo, yhi), (left, center, right))


def solution(mesh):
    placed = (
        P("along", "across", None),
        P("along", "across", None),
        P("along", "across", None),
        P(),
        P(None, "along", "across", None),
        P("across", "along", None),
        P("across", "along"),
    )
    return jax.shard_map(
        shards,
        mesh=mesh,
        in_specs=placed,
        out_specs=(P("along", "across", None), P("along", "across", None)),
        check_vma=False,
    )
```

time: 323 us -> 144 us (0.45)
  the two profiles are of different devices: /device:TPU:30 before, /device:TPU:58 now
where the time goes in v1:
time: 144 us; the launch traced here: 143 us
  Pallas kernels  57.1 us (40%)
  blocking collectives  37.5 us (26%)
  starting transfers between devices  29.4 us (20%)
  waiting for transfers between devices  7.1 us (5%)
  other arithmetic  6.7 us (5%)
  local copies, waits for them, and re-layouts  4.64 us (3%)
    pallas_call x1, Pallas kernels, window(): pl.pallas_call(window_kernel, out_shape=(grid, grid), in_specs=[pl.BlockS...  53.8 us
    ppermute x6, starting transfers between devices, neighbours(): return (lax.ppermute(high, axis, up), lax.ppermute(low, axis, down))  29.4 us
    all_to_all x1, blocking collectives, shards(): moved = lax.all_to_all(dealt, 'along', 0, 0, tiled=True)  24.1 us
    all_to_all x1, blocking collectives, shards(): center = lax.all_to_all(payload, 'across', 0, 0, tiled=True)  13.4 us
    ppermute x6, waiting for transfers between devices, neighbours(): return (lax.ppermute(high, axis, up), lax.ppermute(low, axis, down))  7.1 us
    add x1, other arithmetic, shards(): modulus = modulus + jnp.where(layer == level, modulus_table[level], 0.0)  6.64 us
    unnamed x28, local copies, waits for them, and re-layouts  2.95 us
  transfers between devices with their start and end apart: 6, of which 3 were waited for; matrix products, arithmetic and copies ran while one was open for 0% of the time, Pallas kernels for 2%

profile of v1, /device:TPU:58, one launch (start us, length us, event | category | flops | bytes accessed | tf_op | source)
XLA Modules:
  0.0 143.3 jit_solution(6659998249457633215)
XLA Ops:
  0.6 1.6 %fusion.3 = (f32[1]{0:T(128)}, f32[1]{0:T(128)}, f32[1]{0:T(128)}, f32[1]{0:T(128)}, f32[1]{0:T(128)}, /*index=5*/f32[1]{0:T(128)}, f32[1]{0:T(128)}, f32[1]{0:T(128)}) fusion(f32[8]{0:T(128)} %param.11), kind=kLoop, calls=%fused_computation.24 | loop fusion | bytes 64 | tf_op jit(solution)/shard_map/slice | solution.py:236
  2.3 0.0 copy-start.2
  2.3 6.6 %select_add_fusion.mod_hbm = f32[32,32,128]{2,1,0:T(8,128)S(1)} fusion(s32[32,32,128]{2,1,0:T(8,128)} %param.10, f32[]{:T(128)} %bitcast.8, f32[]{:T(128)} %bitcast.7, f32[]{:T(128)} %bitcast.6, f32[]{:T(128)} %bitcast.5, f32[]{:T(128)} %bitcast.4, f32[]{:T(128)} %bitcast.3, f32[]{:T(128)} %bitcast.2, f32[]{:T(128)} %bitcast.1), kind=kLoop, calls=%fused_computation | loop fusion | flops 3014656 | bytes 1048608 | tf_op jit(solution)/shard_map/add | solution.py:236
  8.9 0.0 copy-start
  8.9 0.0 copy-start.1
  9.0 0.0 copy-done.2
  9.0 1.2 copy-done.1
  10.2 1.9 %collective-permute-start = (f32[24,32,128]{2,1,0:T(8,128)S(1)}, f32[24,32,128]{2,1,0:T(8,128)S(1)}, u32[]{:S(2)}, u32[]{:S(2)}) collective-permute-start(f32[24,32,128]{2,1,0:T(8,128)S(1)} %pad_maximum_fusion), channel_id=1, source_target_pairs={{0,8},{8,16},{16,24},{24,32},{32,40},{40,48},{48,56},{56,64},{64,7... | collective-permute-start | bytes 1179656 | tf_op jit(solution)/shard_map/ppermute | solution.py:228
  12.2 14.0 %collective-permute-start.1 = (f32[24,32,128]{2,1,0:T(8,128)S(1)}, f32[24,32,128]{2,1,0:T(8,128)S(1)}, u32[]{:S(2)}, u32[]{:S(2)}) collective-permute-start(f32[24,32,128]{2,1,0:T(8,128)S(1)} %pad_maximum_fusion.1), channel_id=1, source_target_pairs={{8,0},{16,8},{24,16},{32,24},{40,32},{48,40},{56,48},{64,56},{72,6... | collective-permute-start | bytes 1179656 | tf_op jit(solution)/shard_map/ppermute | solution.py:228
  26.2 3.5 %collective-permute-done.xlo_hbm = f32[24,32,128]{2,1,0:T(8,128)S(1)} collective-permute-done((f32[24,32,128]{2,1,0:T(8,128)S(1)}, f32[24,32,128]{2,1,0:T(8,128)S(1)}, u32[]{:S(2)}, u32[]{:S(2)}) %collective-permute-start) | collective-permute-done | bytes 393248 | tf_op jit(solution)/shard_map/ppermute | solution.py:228
  29.7 0.0 copy-start.3
  29.7 1.8 %collective-permute-done.1.xhi_hbm = f32[24,32,128]{2,1,0:T(8,128)S(1)} collective-permute-done((f32[24,32,128]{2,1,0:T(8,128)S(1)}, f32[24,32,128]{2,1,0:T(8,128)S(1)}, u32[]{:S(2)}, u32[]{:S(2)}) %collective-permute-start.1) | collective-permute-done | bytes 393248 | tf_op jit(solution)/shard_map/ppermute | solution.py:228
  31.5 0.0 copy-start.4
  31.5 0.0 copy-done.3
  31.6 0.0 copy-done
  31.6 0.6 copy-done.4
  32.2 1.3 collective-permute-start.2
  33.5 4.6 %collective-permute-start.3 = (f32[144,8,128]{2,1,0:T(8,128)S(1)}, f32[144,8,128]{2,1,0:T(8,128)S(1)}, u32[]{:S(2)}, u32[]{:S(2)}) collective-permute-start(f32[144,8,128]{2,1,0:T(8,128)S(1)} %get-tuple-element.14), channel_id=1, source_target_pairs={{1,0},{2,1},{3,2},{4,3},{5,4},{6,5},{7,6},{9,8},{10,9},{11,10},{12... | collective-permute-start | bytes 1769480 | tf_op jit(solution)/shard_map/ppermute | solution.py:228
  38.1 1.6 %shard_map.95 = bf16[96,4,128]{2,1,0:T(4,128)(2,1)} custom-call(bf16[2,2,12288]{2,1,0:T(2,128)(2,1)} %bitcast.11), custom_call_target="tpu_custom_call" | custom-call | tf_op jit(solution)/shard_map/pallas_call | solution.py:239
  39.7 24.1 %all_to_all.10.moved_ref = bf16[96,4,128]{2,1,0:T(4,128)(2,1)} all-to-all(bf16[96,4,128]{2,1,0:T(4,128)(2,1)} %shard_map.95), channel_id=1, replica_groups=mesh['along'=96,'across'=8] {'along'}, dimensions={0} | all-to-all | bytes 196608 | tf_op jit(solution)/shard_map/all_to_all | solution.py:251
  63.8 1.7 %shard_map.96 = f32[8,16,128]{2,1,0:T(8,128)} custom-call(bf16[96,4,128]{2,1,0:T(4,128)(2,1)} %all_to_all.10.moved_ref, bf16[24,384]{1,0:T(8,128)(2,1)} %constant.24.clone.table_ref, s32[1,128]{1,0:T(1,128)} %bitcast.12, s32[1,128]{1,0:T(1,128)} %cell_ref.1), custom_call_target="tpu_custom_call" | custom-call | tf_op jit(solution)/shard_map/pallas_call | solution.py:261
  65.5 13.4 %all_to_all.11.fc_ref = f32[8,16,128]{2,1,0:T(8,128)S(1)} all-to-all(f32[8,16,128]{2,1,0:T(8,128)} %shard_map.96), channel_id=1, replica_groups=mesh['along'=96,'across'=8] {'across'}, dimensions={0} | all-to-all | bytes 131072 | tf_op jit(solution)/shard_map/all_to_all | solution.py:268
  79.0 0.0 copy-start.7
  79.0 1.9 %collective-permute-start.4 = (f32[8,16,128]{2,1,0:T(8,128)S(1)}, f32[8,16,128]{2,1,0:T(8,128)S(1)}, u32[]{:S(2)}, u32[]{:S(2)}) collective-permute-start(f32[8,16,128]{2,1,0:T(8,128)S(1)} %all_to_all.11.fc_ref), channel_id=1, source_target_pairs={{0,8},{8,16},{16,24},{24,32},{32,40},{40,48},{48,56},{56,64},{64,7... | collective-permute-start | bytes 196616 | tf_op jit(solution)/shard_map/ppermute | solution.py:228
  80.9 5.8 %collective-permute-start.5 = (f32[8,16,128]{2,1,0:T(8,128)S(1)}, f32[8,16,128]{2,1,0:T(8,128)S(1)}, u32[]{:S(2)}, u32[]{:S(2)}) collective-permute-start(f32[8,16,128]{2,1,0:T(8,128)S(1)} %all_to_all.11.fc_ref), channel_id=1, source_target_pairs={{8,0},{16,8},{24,16},{32,24},{40,32},{48,40},{56,48},{64,56},{72,6... | collective-permute-start | bytes 196616 | tf_op jit(solution)/shard_map/ppermute | solution.py:228
  86.6 0.0 collective-permute-done.4.fl_ref
  86.6 0.0 copy-start.8
  86.7 1.9 %collective-permute-done.5.fr_ref = f32[8,16,128]{2,1,0:T(8,128)S(1)} collective-permute-done((f32[8,16,128]{2,1,0:T(8,128)S(1)}, f32[8,16,128]{2,1,0:T(8,128)S(1)}, u32[]{:S(2)}, u32[]{:S(2)}) %collective-permute-start.5) | collective-permute-done | bytes 65568 | tf_op jit(solution)/shard_map/ppermute | solution.py:228
  88.5 0.0 copy-start.9
  88.5 0.0 collective-permute-done.2.ylo_hbm
  88.5 0.0 copy-start.5
  88.5 0.0 collective-permute-done.3.yhi_hbm
  88.5 0.0 copy-start.6
  88.5 0.0 copy-done.7
  88.6 0.0 copy-done.8
  88.6 0.6 copy-done.9
  89.1 0.2 copy-done.5
  89.4 0.2 copy-done.6
  89.6 53.8 %shard_map.97 = (f32[32,32,128]{2,1,0:T(8,128)}, f32[32,32,128]{2,1,0:T(8,128)}) custom-call(s32[1]{0:T(128)} %bitcast.place_ref, f32[32,32,128]{2,1,0:T(8,128)} %now_hbm.1, f32[32,32,128]{2,1,0:T(8,128)} %before_hbm.1, f32[32,32,128]{2,1,0:T(8,128)} %copy-done, f32[24,32,128]{2,1,0:T(8,128)} %copy-done.3, f32[24,32,128]{2,1,0:T(8,128)} %copy-done.4, ...), custom_call_target="tpu_custom_call" | custom-call | tf_op jit(solution)/shard_map/pallas_call | solution.py:206
  (13 shorter events, 0.2 us)
Async XLA Ops:
  2.3 6.7 %copy-start.2 = (f32[32,32,128]{2,1,0:T(8,128)S(1)}, f32[32,32,128]{2,1,0:T(8,128)}, u32[]{:S(2)}) copy-start(f32[32,32,128]{2,1,0:T(8,128)} %before_hbm.1) | copy-start | bytes 1572868
  8.9 22.6 %copy-start = (f32[32,32,128]{2,1,0:T(8,128)}, f32[32,32,128]{2,1,0:T(8,128)S(1)}, u32[]{:S(2)}) copy-start(f32[32,32,128]{2,1,0:T(8,128)S(1)} %select_add_fusion.mod_hbm) | copy-start | bytes 1572868
  8.9 1.2 copy-start.1
  10.2 19.5 %collective-permute-start = (f32[24,32,128]{2,1,0:T(8,128)S(1)}, f32[24,32,128]{2,1,0:T(8,128)S(1)}, u32[]{:S(2)}, u32[]{:S(2)}) collective-permute-start(f32[24,32,128]{2,1,0:T(8,128)S(1)} %pad_maximum_fusion), channel_id=1, source_target_pairs={{0,8},{8,16},{16,24},{24,32},{32,40},{40,48},{48,56},{56,64},{64,7... | collective-permute-start | bytes 1179656 | tf_op jit(solution)/shard_map/ppermute | solution.py:228
  12.2 19.3 %collective-permute-start.1 = (f32[24,32,128]{2,1,0:T(8,128)S(1)}, f32[24,32,128]{2,1,0:T(8,128)S(1)}, u32[]{:S(2)}, u32[]{:S(2)}) collective-permute-start(f32[24,32,128]{2,1,0:T(8,128)S(1)} %pad_maximum_fusion.1), channel_id=1, source_target_pairs={{8,0},{16,8},{24,16},{32,24},{40,32},{48,40},{56,48},{64,56},{72,6... | collective-permute-start | bytes 1179656 | tf_op jit(solution)/shard_map/ppermute | solution.py:228
  29.7 1.9 %copy-start.3 = (f32[24,32,128]{2,1,0:T(8,128)}, f32[24,32,128]{2,1,0:T(8,128)S(1)}, u32[]{:S(2)}) copy-start(f32[24,32,128]{2,1,0:T(8,128)S(1)} %collective-permute-done.xlo_hbm) | copy-start | bytes 1179652
  31.5 0.7 copy-start.4
  32.2 56.3 %collective-permute-start.2 = (f32[144,8,128]{2,1,0:T(8,128)S(1)}, f32[144,8,128]{2,1,0:T(8,128)S(1)}, u32[]{:S(2)}, u32[]{:S(2)}) collective-permute-start(f32[144,8,128]{2,1,0:T(8,128)S(1)} %get-tuple-element.15), channel_id=1, source_target_pairs={{0,1},{1,2},{2,3},{3,4},{4,5},{5,6},{6,7},{8,9},{9,10},{10,11},{11... | collective-permute-start | bytes 1769480 | tf_op jit(solution)/shard_map/ppermute | solution.py:228
  33.5 55.0 %collective-permute-start.3 = (f32[144,8,128]{2,1,0:T(8,128)S(1)}, f32[144,8,128]{2,1,0:T(8,128)S(1)}, u32[]{:S(2)}, u32[]{:S(2)}) collective-permute-start(f32[144,8,128]{2,1,0:T(8,128)S(1)} %get-tuple-element.14), channel_id=1, source_target_pairs={{1,0},{2,1},{3,2},{4,3},{5,4},{6,5},{7,6},{9,8},{10,9},{11,10},{12... | collective-permute-start | bytes 1769480 | tf_op jit(solution)/shard_map/ppermute | solution.py:228
  79.0 9.6 %copy-start.7 = (f32[8,16,128]{2,1,0:T(8,128)}, f32[8,16,128]{2,1,0:T(8,128)S(1)}, u32[]{:S(2)}) copy-start(f32[8,16,128]{2,1,0:T(8,128)S(1)} %all_to_all.11.fc_ref) | copy-start | bytes 196612
  79.0 7.7 %collective-permute-start.4 = (f32[8,16,128]{2,1,0:T(8,128)S(1)}, f32[8,16,128]{2,1,0:T(8,128)S(1)}, u32[]{:S(2)}, u32[]{:S(2)}) collective-permute-start(f32[8,16,128]{2,1,0:T(8,128)S(1)} %all_to_all.11.fc_ref), channel_id=1, source_target_pairs={{0,8},{8,16},{16,24},{24,32},{32,40},{40,48},{48,56},{56,64},{64,7... | collective-permute-start | bytes 196616 | tf_op jit(solution)/shard_map/ppermute | solution.py:228
  80.9 7.6 %collective-permute-start.5 = (f32[8,16,128]{2,1,0:T(8,128)S(1)}, f32[8,16,128]{2,1,0:T(8,128)S(1)}, u32[]{:S(2)}, u32[]{:S(2)}) collective-permute-start(f32[8,16,128]{2,1,0:T(8,128)S(1)} %all_to_all.11.fc_ref), channel_id=1, source_target_pairs={{8,0},{16,8},{24,16},{32,24},{40,32},{48,40},{56,48},{64,56},{72,6... | collective-permute-start | bytes 196616 | tf_op jit(solution)/shard_map/ppermute | solution.py:228
  86.6 1.9 %copy-start.8 = (f32[8,16,128]{2,1,0:T(8,128)}, f32[8,16,128]{2,1,0:T(8,128)S(1)}, u32[]{:S(2)}) copy-start(f32[8,16,128]{2,1,0:T(8,128)S(1)} %collective-permute-done.4.fl_ref) | copy-start | bytes 196612
  88.5 0.6 copy-start.9
  88.5 0.9 copy-start.5
  88.5 1.1 copy-start.6

commit v2 on v1

--- a/solution.py
+++ b/solution.py
@@ -18,6 +18,8 @@
 CELLS = CX * CY * CZ
 NPT = 128
 ROW_BITS, Z_BITS, P_BITS = 12, 7, 12
+BODY = (12, 11, 11, 10, 10, 9, 9, 8)
+GROUP = 16
 LIMIT = 56 * 1024 * 1024
 
 
@@ -44,10 +46,23 @@
     return np.concatenate(parts, axis=0)
 
 
-def deal_kernel(fk_ref, out_ref):
-    for i in range(out_ref.shape[0]):
+def prepare_kernel(table_ref, now_ref, before_ref, layer_ref, fk_ref, low_ref, high_ref, dealt_ref, mod_ref):
+    for i in range(dealt_ref.shape[0]):
         for c in range(2):
-            out_ref[i, pl.ds(2 * c, 2), :] = fk_ref[c, :, pl.ds(i * NPT, NPT)]
+            dealt_ref[i, pl.ds(2 * c, 2), :] = fk_ref[c, :, pl.ds(i * NPT, NPT)]
+
+    def fill(x, _):
+        level = layer_ref[x]
+        modulus = jnp.full(level.shape, table_ref[0], jnp.float32)
+        for k in range(1, table_ref.shape[0]):
+            modulus = jnp.where(level == k, table_ref[k], modulus)
+        mod_ref[x] = modulus
+        return 0
+
+    lax.fori_loop(0, CX, fill, 0, unroll=2)
+    for k, ref in enumerate((now_ref, before_ref, mod_ref)):
+        low_ref[pl.ds(k * H, H)] = ref[pl.ds(0, H)]
+        high_ref[pl.ds(k * H, H)] = ref[pl.ds(CX - H, H)]
 
 
 def transform_kernel(moved_ref, table_ref, owner_ref, cell_ref, out_ref, wide_ref):
@@ -71,11 +86,11 @@
     copies = []
     for k, (own, ext) in enumerate(((now_hbm, a_ref), (before_hbm, b_ref), (mod_hbm, m_ref))):
         pieces = (
-            (own, ext.at[pl.ds(H, CX), pl.ds(2 * H, CY)]),
-            (xlo_hbm.at[pl.ds(k * H, H)], ext.at[pl.ds(0, H), pl.ds(2 * H, CY)]),
-            (xhi_hbm.at[pl.ds(k * H, H)], ext.at[pl.ds(H + CX, H), pl.ds(2 * H, CY)]),
-            (ylo_hbm.at[pl.ds(k * EX, EX)], ext.at[:, pl.ds(H, H)]),
-            (yhi_hbm.at[pl.ds(k * EX, EX)], ext.at[:, pl.ds(2 * H + CY, H)]),
+            (own, ext.at[pl.ds(1 + H, CX), pl.ds(2 * H, CY)]),
+            (xlo_hbm.at[pl.ds(k * H, H)], ext.at[pl.ds(1, H), pl.ds(2 * H, CY)]),
+            (xhi_hbm.at[pl.ds(k * H, H)], ext.at[pl.ds(1 + H + CX, H), pl.ds(2 * H, CY)]),
+            (ylo_hbm.at[pl.ds(k * EX, EX)], ext.at[pl.ds(1, EX), pl.ds(H, H)]),
+            (yhi_hbm.at[pl.ds(k * EX, EX)], ext.at[pl.ds(1, EX), pl.ds(2 * H + CY, H)]),
         )
         for n, (src, dst) in enumerate(pieces):
             copies.append(pltpu.make_async_copy(src, dst, sems.at[k, n]))
@@ -116,32 +131,30 @@
         return count
 
     count = lax.fori_loop(0, 3 * tiles, pick_row, 0)
-    for j in range(4):
+    for j in range(GROUP):
         list_smem[count + j] = 0
 
     zline = lax.broadcasted_iota(jnp.int32, (STEPS, CZ), 1)
 
-    def put(f_ref, tile, code):
-        place = code & ((1 << P_BITS) - 1)
-        z = (code >> P_BITS) & (CZ - 1)
-        row = code >> (Z_BITS + P_BITS)
-        force = f_ref[tile, 0:8, :]
-        column = jnp.take_along_axis(force, jnp.full((STEPS, CZ), place & (NPT - 1), jnp.int32), axis=1)
-        at = pl.ds(pl.multiple_of(row * STEPS, STEPS), STEPS)
-        d_ref[at, :] = d_ref[at, :] + jnp.where(zline == z, column, 0.0)
-
-    def add_point(i, _):
-        for j in range(4):
-            code = list_smem[4 * i + j]
-            tile = (code & ((1 << P_BITS) - 1)) >> 7
-            put(f_all, tile, code)
+    def add_points(i, _):
+        adds = []
+        for j in range(GROUP):
+            code = list_smem[GROUP * i + j]
+            place = code & ((1 << P_BITS) - 1)
+            z = (code >> P_BITS) & (CZ - 1)
+            row = code >> (Z_BITS + P_BITS)
+            force = f_all[place >> 7, 0:8, :]
+            column = jnp.take_along_axis(force, jnp.full((STEPS, CZ), place & (NPT - 1), jnp.int32), axis=1)
+            adds.append((pl.ds(pl.multiple_of(row * STEPS, STEPS), STEPS), jnp.where(zline == z, column, 0.0)))
+        for at, add in adds:
+            d_ref[at, :] = d_ref[at, :] + add
         return 0
 
     f_all = kc_ref
     for side, f_ref in enumerate((fl_ref, fc_ref, fr_ref)):
         for a in range(tiles):
             kc_ref[side * tiles + a, 0:8, :] = f_ref[a, 0:8, :]
-    lax.fori_loop(0, (count + 3) // 4, add_point, 0)
+    lax.fori_loop(0, (count + GROUP - 1) // GROUP, add_points, 0)
 
     for c in copies:
         c.wait()
@@ -151,46 +164,54 @@
     def face(c, n):
         return jnp.where(jnp.minimum(c, n) > 0.0, 0.075 * (c + n), 0.0)
 
-    def coefficients(x, _):
-        for j in range(EY // 8):
-            y = H + 8 * j
-            c = m_ref[x, pl.ds(y, 8), :]
-            xp = m_ref[x + 1, pl.ds(y, 8), :]
-            xm = m_ref[jnp.maximum(x - 1, 0), pl.ds(y, 8), :]
-            yp = m_ref[x, pl.ds(y + 1, 8), :]
-            ym = m_ref[x, pl.ds(y - 1, 8), :]
-            zp = jnp.where(zpos == CZ - 1, 0.0, pltpu.roll(c, CZ - 1, 1))
-            zm = jnp.where(zpos == 0, 0.0, pltpu.roll(c, 1, 1))
-            kx_ref[x, pl.ds(y, 8), :] = face(c, xp)
-            ky_ref[x, pl.ds(y, 8), :] = face(c, yp)
-            kz_ref[x, pl.ds(y, 8), :] = face(c, zp)
-            kc_ref[x, pl.ds(y, 8), :] = 2.0 - 0.075 * (6.0 * c + ((xp + xm) + (yp + ym) + (zp + zm)))
+    def coefficients(i, _):
+        for k in range(8):
+            x = 8 * i + k + 1
+            for j in range(EY // 8):
+                y = H + 8 * j
+                c = m_ref[x, pl.ds(y, 8), :]
+                xp = m_ref[x + 1, pl.ds(y, 8), :]
+                xm = m_ref[x - 1, pl.ds(y, 8), :]
+                yp = m_ref[x, pl.ds(y + 1, 8), :]
+                ym = m_ref[x, pl.ds(y - 1, 8), :]
+                zp = jnp.where(zpos == CZ - 1, 0.0, pltpu.roll(c, CZ - 1, 1))
+                zm = jnp.where(zpos == 0, 0.0, pltpu.roll(c, 1, 1))
+                kx_ref[x, pl.ds(y, 8), :] = face(c, xp)
+                ky_ref[x, pl.ds(y, 8), :] = face(c, yp)
+                kz_ref[x, pl.ds(y, 8), :] = face(c, zp)
+                kc_ref[x, pl.ds(y, 8), :] = 2.0 - 0.075 * (6.0 * c + ((xp + xm) + (yp + ym) + (zp + zm)))
         return 0
 
-    lax.fori_loop(0, EX - 1, coefficients, 0)
+    lax.fori_loop(0, EX // 8, coefficients, 0)
 
     for step in range(STEPS):
         u_ref, w_ref = (a_ref, b_ref) if step % 2 == 0 else (b_ref, a_ref)
 
-        def advance(x, _, u_ref=u_ref, w_ref=w_ref, step=step):
-            for j in range(EY // 8):
-                y = H + 8 * j
-                u = u_ref[x, pl.ds(y, 8), :]
-                kz = kz_ref[x, pl.ds(y, 8), :]
-                in_x = (kx_ref[x, pl.ds(y, 8), :] * u_ref[x + 1, pl.ds(y, 8), :]
-                        + kx_ref[x - 1, pl.ds(y, 8), :] * u_ref[x - 1, pl.ds(y, 8), :])
-                in_y = (ky_ref[x, pl.ds(y, 8), :] * u_ref[x, pl.ds(y + 1, 8), :]
-                        + ky_ref[x, pl.ds(y - 1, 8), :] * u_ref[x, pl.ds(y - 1, 8), :])
-                in_z = kz * pltpu.roll(u, CZ - 1, 1) + pltpu.roll(kz * u, 1, 1)
-                drive = d_ref[pl.ds((x * EY + 8 * j) * STEPS + step, 8, stride=STEPS), :]
-                own = kc_ref[x, pl.ds(y, 8), :] * u - w_ref[x, pl.ds(y, 8), :]
-                w_ref[x, pl.ds(y, 8), :] = (own + drive) + ((in_x + in_y) + in_z)
+        planes = BODY[step]
+        start = EX // 2 - 2 * planes
+        rows = range(0, EY // 8) if step < STEPS - 1 else range(1, 1 + CY // 8)
+
+        def advance(i, _, u_ref=u_ref, w_ref=w_ref, step=step, planes=planes, start=start, rows=rows):
+            for k in range(planes):
+                x = start + planes * i + k
+                for j in rows:
+                    y = H + 8 * j
+                    u = u_ref[x + 1, pl.ds(y, 8), :]
+                    kz = kz_ref[x + 1, pl.ds(y, 8), :]
+                    in_z = kz * pltpu.roll(u, CZ - 1, 1) + pltpu.roll(kz * u, 1, 1)
+                    in_x = (kx_ref[x + 1, pl.ds(y, 8), :] * u_ref[x + 2, pl.ds(y, 8), :]
+                            + kx_ref[x, pl.ds(y, 8), :] * u_ref[x, pl.ds(y, 8), :])
+                    in_y = (ky_ref[x + 1, pl.ds(y, 8), :] * u_ref[x + 1, pl.ds(y + 1, 8), :]
+                            + ky_ref[x + 1, pl.ds(y - 1, 8), :] * u_ref[x + 1, pl.ds(y - 1, 8), :])
+                    drive = d_ref[pl.ds((x * EY + 8 * j) * STEPS + step, 8, stride=STEPS), :]
+                    own = kc_ref[x + 1, pl.ds(y, 8), :] * u - w_ref[x + 1, pl.ds(y, 8), :]
+                    w_ref[x + 1, pl.ds(y, 8), :] = (own + drive) + ((in_x + in_y) + in_z)
             return 0
 
-        lax.fori_loop(step + 1, EX - step - 1, advance, 0)
+        lax.fori_loop(0, 4, advance, 0)
 
     outs = [
-        pltpu.make_async_copy(ref.at[pl.ds(H, CX), pl.ds(2 * H, CY)], hbm, sem_out.at[n])
+        pltpu.make_async_copy(ref.at[pl.ds(1 + H, CX), pl.ds(2 * H, CY)], hbm, sem_out.at[n])
         for n, (ref, hbm) in enumerate(((a_ref, next_hbm), (b_ref, prior_hbm)))
     ]
     for c in outs:
@@ -202,7 +223,7 @@
 def window(place, fields, forces):
     tiles = forces[0].shape[0]
     grid = jax.ShapeDtypeStruct((CX, CY, CZ), jnp.float32)
-    buffer = pltpu.VMEM((EX, PY, CZ), jnp.float32)
+    buffer = pltpu.VMEM((EX + 2, PY, CZ), jnp.float32)
     return pl.pallas_call(
         window_kernel,
         out_shape=(grid, grid),
@@ -231,24 +252,23 @@
 def shards(field_now, field_before, layer, modulus_table, fk_panel, owner, local_cell):
     sources, tiles = lax.axis_size("along"), lax.axis_size("across")
     local_freqs = fk_panel.shape[1]
-    modulus = jnp.zeros(field_now.shape, jnp.float32)
-    for level in range(modulus_table.shape[0]):
-        modulus = modulus + jnp.where(layer == level, modulus_table[level], 0.0)
+    slab = jax.ShapeDtypeStruct((3 * H, CY, CZ), jnp.float32)
+    low, high, dealt, modulus = pl.pallas_call(
+        prepare_kernel,
+        out_shape=(
+            slab,
+            slab,
+            jax.ShapeDtypeStruct((sources, 2 * local_freqs, NPT), jnp.bfloat16),
+            jax.ShapeDtypeStruct(field_now.shape, jnp.float32),
+        ),
+        in_specs=[pl.BlockSpec(memory_space=pltpu.SMEM)] + [vmem_spec()] * 4,
+        out_specs=(vmem_spec(),) * 4,
+        compiler_params=pltpu.CompilerParams(vmem_limit_bytes=LIMIT),
+    )(modulus_table, field_now, field_before, layer, fk_panel.reshape(2, local_freqs, sources * NPT))
     arrays = (field_now, field_before, modulus)
-
-    dealt = pl.pallas_call(
-        deal_kernel,
-        out_shape=jax.ShapeDtypeStruct((sources, 2 * local_freqs, NPT), jnp.bfloat16),
-        in_specs=[vmem_spec()],
-        out_specs=vmem_spec(),
-    )(fk_panel.reshape(2, local_freqs, sources * NPT))
-
-    xlo, xhi = neighbours(
-        jnp.concatenate([a[:H] for a in arrays], axis=0),
-        jnp.concatenate([a[-H:] for a in arrays], axis=0),
-        "along",
-    )
+    xlo, xhi = neighbours(low, high, "along")
     moved = lax.all_to_all(dealt, "along", 0, 0, tiled=True)
+    xlo, xhi, moved = lax.optimization_barrier((xlo, xhi, moved))
 
     def side(rows):
         return jnp.concatenate(

time: 144 us -> 102 us (0.71)
  Pallas kernels: 57.1 us -> 29.1 us
  other arithmetic: 6.7 us -> 0 us
  waiting for transfers between devices: 7.1 us -> 1.87 us
  local copies, waits for them, and re-layouts: 4.64 us -> 2.32 us
    pallas_call x1, Pallas kernels: 53.8 us -> 24.5 us  [window(): pl.pallas_call(window_kernel, out_shape=(grid, grid), in_specs=[pl.BlockS...]
    add x1 -> x0, other arithmetic: 6.64 us -> none  [shards(): modulus = modulus + jnp.where(layer == level, modulus_table[level], 0.0)]
    ppermute x6, waiting for transfers between devices: 7.1 us -> 1.87 us  [neighbours(): return (lax.ppermute(high, axis, up), lax.ppermute(low, axis, down))]
    all_to_all x1, blocking collectives: 13.4 us -> 15.3 us  [shards(): center = lax.all_to_all(payload, 'across', 0, 0, tiled=True)]
    all_to_all x1, blocking collectives: 24.1 us -> 22.3 us  [shards(): moved = lax.all_to_all(dealt, 'along', 0, 0, tiled=True)]
    slice x3 -> x0, local copies, waits for them, and re-layouts: 1.69 us -> none  [the longest x1 1.64 us: shards(): modulus = modulus + jnp.where(layer == level, modulus_table[level], 0.0)]
  transfers between devices with their start and end apart: 6 -> 6, of which waited for: 3 -> 1; matrix products, arithmetic and copies ran while one was open for 0% -> 0% of each run, Pallas kernels for 2% -> 2%
where the time goes in v2:
time: 102 us; the launch traced here: 101 us
  blocking collectives  37.5 us (37%)
  starting transfers between devices  29.4 us (29%)
  Pallas kernels  29.1 us (29%)
  local copies, waits for them, and re-layouts  2.32 us (2%)
  waiting for transfers between devices  1.87 us (2%)
    ppermute x6, starting transfers between devices, neighbours(): return (lax.ppermute(high, axis, up), lax.ppermute(low, axis, down))  29.4 us
    pallas_call x1, Pallas kernels, window(): pl.pallas_call(window_kernel, out_shape=(grid, grid), in_specs=[pl.BlockS...  24.5 us
    all_to_all x1, blocking collectives, shards(): moved = lax.all_to_all(dealt, 'along', 0, 0, tiled=True)  22.3 us
    all_to_all x1, blocking collectives, shards(): center = lax.all_to_all(payload, 'across', 0, 0, tiled=True)  15.3 us
    pallas_call x1, Pallas kernels, shards(): pl.pallas_call(prepare_kernel, out_shape=(slab, slab, jax.ShapeDtypeStruc...  2.95 us
    unnamed x28, local copies, waits for them, and re-layouts  2.31 us
  transfers between devices with their start and end apart: 6, of which 1 were waited for; matrix products, arithmetic and copies ran while one was open for 0% of the time, Pallas kernels for 2%

profile of v2, /device:TPU:58, one launch (start us, length us, event | category | flops | bytes accessed | tf_op | source)
XLA Modules:
  0.0 101.2 jit_solution(326439390203113486)
XLA Ops:
  0.6 0.0 copy-start
  0.6 2.9 %shard_map.95 = (f32[24,32,128]{2,1,0:T(8,128)}, f32[24,32,128]{2,1,0:T(8,128)}, bf16[96,4,128]{2,1,0:T(4,128)(2,1)}, f32[32,32,128]{2,1,0:T(8,128)}) custom-call(f32[8]{0:T(128)} %table_ref.2, f32[32,32,128]{2,1,0:T(8,128)} %now_hbm.1, f32[32,32,128]{2,1,0:T(8,128)} %before_hbm.1, s32[32,32,128]{2,1,0:T(8,128)} %layer_ref.1, bf16[2,2,12288]{2,1,0:T(2,128)(2,1)} %bitcast.3), custom_call_target="tpu_custom_call" | custom-call | tf_op jit(solution)/shard_map/pallas_call | solution.py:256
  3.6 1.9 %collective-permute-start = (f32[24,32,128]{2,1,0:T(8,128)}, f32[24,32,128]{2,1,0:T(8,128)S(1)}, u32[]{:S(2)}, u32[]{:S(2)}) collective-permute-start(f32[24,32,128]{2,1,0:T(8,128)} %get-tuple-element.10), channel_id=1, source_target_pairs={{0,8},{8,16},{16,24},{24,32},{32,40},{40,48},{48,56},{56,64},{64,7... | collective-permute-start | bytes 1179656 | tf_op jit(solution)/shard_map/ppermute | solution.py:249
  5.5 14.0 %collective-permute-start.1 = (f32[24,32,128]{2,1,0:T(8,128)}, f32[24,32,128]{2,1,0:T(8,128)S(1)}, u32[]{:S(2)}, u32[]{:S(2)}) collective-permute-start(f32[24,32,128]{2,1,0:T(8,128)} %get-tuple-element.11), channel_id=1, source_target_pairs={{8,0},{16,8},{24,16},{32,24},{40,32},{48,40},{56,48},{64,56},{72,6... | collective-permute-start | bytes 1179656 | tf_op jit(solution)/shard_map/ppermute | solution.py:249
  19.5 0.0 copy-start.1
  19.5 22.3 %all_to_all.10.moved_ref = bf16[96,4,128]{2,1,0:T(4,128)(2,1)} all-to-all(bf16[96,4,128]{2,1,0:T(4,128)(2,1)} %get-tuple-element.12), channel_id=1, replica_groups=mesh['along'=96,'across'=8] {'along'}, dimensions={0} | all-to-all | bytes 196608 | tf_op jit(solution)/shard_map/all_to_all | solution.py:270
  41.8 0.0 collective-permute-done.xlo_hbm
  41.8 0.0 copy-start.3
  41.8 0.0 collective-permute-done.1.xhi_hbm
  41.8 0.0 copy-start.4
  41.8 0.0 copy-done
  41.9 0.0 copy-start.2
  41.9 0.0 copy-done.1
  42.0 0.6 copy-done.3
  42.6 0.6 copy-done.2
  43.2 0.0 copy-done.4
  43.2 1.3 %collective-permute-start.2 = (f32[144,8,128]{2,1,0:T(8,128)S(1)}, f32[144,8,128]{2,1,0:T(8,128)S(1)}, u32[]{:S(2)}, u32[]{:S(2)}) collective-permute-start(f32[144,8,128]{2,1,0:T(8,128)S(1)} %get-tuple-element.23), channel_id=1, source_target_pairs={{0,1},{1,2},{2,3},{3,4},{4,5},{5,6},{6,7},{8,9},{9,10},{10,11},{11... | collective-permute-start | bytes 1769480 | tf_op jit(solution)/shard_map/ppermute | solution.py:249
  44.5 4.6 %collective-permute-start.3 = (f32[144,8,128]{2,1,0:T(8,128)S(1)}, f32[144,8,128]{2,1,0:T(8,128)S(1)}, u32[]{:S(2)}, u32[]{:S(2)}) collective-permute-start(f32[144,8,128]{2,1,0:T(8,128)S(1)} %get-tuple-element.22), channel_id=1, source_target_pairs={{1,0},{2,1},{3,2},{4,3},{5,4},{6,5},{7,6},{9,8},{10,9},{11,10},{12... | collective-permute-start | bytes 1769480 | tf_op jit(solution)/shard_map/ppermute | solution.py:249
  49.1 1.7 %shard_map.96 = f32[8,16,128]{2,1,0:T(8,128)} custom-call(bf16[96,4,128]{2,1,0:T(4,128)(2,1)} %all_to_all.10.moved_ref, bf16[24,384]{1,0:T(8,128)(2,1)} %constant.6.clone.table_ref, s32[1,128]{1,0:T(1,128)} %bitcast.4, s32[1,128]{1,0:T(1,128)} %cell_ref.1), custom_call_target="tpu_custom_call" | custom-call | tf_op jit(solution)/shard_map/pallas_call | solution.py:281
  50.8 15.3 %all_to_all.11.fc_ref = f32[8,16,128]{2,1,0:T(8,128)S(1)} all-to-all(f32[8,16,128]{2,1,0:T(8,128)} %shard_map.96), channel_id=1, replica_groups=mesh['along'=96,'across'=8] {'across'}, dimensions={0} | all-to-all | bytes 131072 | tf_op jit(solution)/shard_map/all_to_all | solution.py:288
  66.0 0.0 copy-start.7
  66.0 1.9 %collective-permute-start.4 = (f32[8,16,128]{2,1,0:T(8,128)S(1)}, f32[8,16,128]{2,1,0:T(8,128)S(1)}, u32[]{:S(2)}, u32[]{:S(2)}) collective-permute-start(f32[8,16,128]{2,1,0:T(8,128)S(1)} %all_to_all.11.fc_ref), channel_id=1, source_target_pairs={{0,8},{8,16},{16,24},{24,32},{32,40},{40,48},{48,56},{56,64},{64,7... | collective-permute-start | bytes 196616 | tf_op jit(solution)/shard_map/ppermute | solution.py:249
  68.0 5.8 %collective-permute-start.5 = (f32[8,16,128]{2,1,0:T(8,128)S(1)}, f32[8,16,128]{2,1,0:T(8,128)S(1)}, u32[]{:S(2)}, u32[]{:S(2)}) collective-permute-start(f32[8,16,128]{2,1,0:T(8,128)S(1)} %all_to_all.11.fc_ref), channel_id=1, source_target_pairs={{8,0},{16,8},{24,16},{32,24},{40,32},{48,40},{56,48},{64,56},{72,6... | collective-permute-start | bytes 196616 | tf_op jit(solution)/shard_map/ppermute | solution.py:249
  73.7 0.0 collective-permute-done.4.fl_ref
  73.7 0.0 copy-start.8
  73.7 1.9 %collective-permute-done.5.fr_ref = f32[8,16,128]{2,1,0:T(8,128)S(1)} collective-permute-done((f32[8,16,128]{2,1,0:T(8,128)S(1)}, f32[8,16,128]{2,1,0:T(8,128)S(1)}, u32[]{:S(2)}, u32[]{:S(2)}) %collective-permute-start.5) | collective-permute-done | bytes 65568 | tf_op jit(solution)/shard_map/ppermute | solution.py:249
  75.6 0.0 copy-start.9
  75.6 0.0 collective-permute-done.2.ylo_hbm
  75.6 0.0 copy-start.5
  75.6 0.0 collective-permute-done.3.yhi_hbm
  75.6 0.0 copy-start.6
  75.6 0.0 copy-done.7
  75.6 0.0 copy-done.8
  75.6 0.6 copy-done.9
  76.2 0.2 copy-done.5
  76.5 0.2 copy-done.6
  76.7 24.5 %shard_map.97 = (f32[32,32,128]{2,1,0:T(8,128)}, f32[32,32,128]{2,1,0:T(8,128)}) custom-call(s32[1]{0:T(128)} %bitcast.place_ref, f32[32,32,128]{2,1,0:T(8,128)} %now_hbm.1, f32[32,32,128]{2,1,0:T(8,128)} %before_hbm.1, f32[32,32,128]{2,1,0:T(8,128)} %get-tuple-element.9.mod_hbm, f32[24,32,128]{2,1,0:T(8,128)} %copy-done.3, f32[24,32,128]{2,1,0:T(8,128)} %copy-done.4, ...), custom_call_target="tpu_custom_call" | custom-call | tf_op jit(solution)/shard_map/pallas_call | solution.py:227
  (9 shorter events, 0.1 us)
Async XLA Ops:
  0.6 41.2 %copy-start = (f32[32,32,128]{2,1,0:T(8,128)S(1)}, f32[32,32,128]{2,1,0:T(8,128)}, u32[]{:S(2)}) copy-start(f32[32,32,128]{2,1,0:T(8,128)} %now_hbm.1) | copy-start | bytes 1572868
  3.6 38.2 %collective-permute-start = (f32[24,32,128]{2,1,0:T(8,128)}, f32[24,32,128]{2,1,0:T(8,128)S(1)}, u32[]{:S(2)}, u32[]{:S(2)}) collective-permute-start(f32[24,32,128]{2,1,0:T(8,128)} %get-tuple-element.10), channel_id=1, source_target_pairs={{0,8},{8,16},{16,24},{24,32},{32,40},{40,48},{48,56},{56,64},{64,7... | collective-permute-start | bytes 1179656 | tf_op jit(solution)/shard_map/ppermute | solution.py:249
  5.5 36.3 %collective-permute-start.1 = (f32[24,32,128]{2,1,0:T(8,128)}, f32[24,32,128]{2,1,0:T(8,128)S(1)}, u32[]{:S(2)}, u32[]{:S(2)}) collective-permute-start(f32[24,32,128]{2,1,0:T(8,128)} %get-tuple-element.11), channel_id=1, source_target_pairs={{8,0},{16,8},{24,16},{32,24},{40,32},{48,40},{56,48},{64,56},{72,6... | collective-permute-start | bytes 1179656 | tf_op jit(solution)/shard_map/ppermute | solution.py:249
  19.5 22.4 %copy-start.1 = (f32[32,32,128]{2,1,0:T(8,128)S(1)}, f32[32,32,128]{2,1,0:T(8,128)}, u32[]{:S(2)}) copy-start(f32[32,32,128]{2,1,0:T(8,128)} %before_hbm.1) | copy-start | bytes 1572868
  41.8 0.8 copy-start.3
  41.8 1.4 %copy-start.4 = (f32[24,32,128]{2,1,0:T(8,128)}, f32[24,32,128]{2,1,0:T(8,128)S(1)}, u32[]{:S(2)}) copy-start(f32[24,32,128]{2,1,0:T(8,128)S(1)} %collective-permute-done.1.xhi_hbm) | copy-start | bytes 1179652
  41.9 1.3 %copy-start.2 = (f32[32,32,128]{2,1,0:T(8,128)S(1)}, f32[32,32,128]{2,1,0:T(8,128)}, u32[]{:S(2)}) copy-start(f32[32,32,128]{2,1,0:T(8,128)} %get-tuple-element.9.mod_hbm) | copy-start | bytes 1572868
  43.2 32.4 %collective-permute-start.2 = (f32[144,8,128]{2,1,0:T(8,128)S(1)}, f32[144,8,128]{2,1,0:T(8,128)S(1)}, u32[]{:S(2)}, u32[]{:S(2)}) collective-permute-start(f32[144,8,128]{2,1,0:T(8,128)S(1)} %get-tuple-element.23), channel_id=1, source_target_pairs={{0,1},{1,2},{2,3},{3,4},{4,5},{5,6},{6,7},{8,9},{9,10},{10,11},{11... | collective-permute-start | bytes 1769480 | tf_op jit(solution)/shard_map/ppermute | solution.py:249
  44.5 31.1 %collective-permute-start.3 = (f32[144,8,128]{2,1,0:T(8,128)S(1)}, f32[144,8,128]{2,1,0:T(8,128)S(1)}, u32[]{:S(2)}, u32[]{:S(2)}) collective-permute-start(f32[144,8,128]{2,1,0:T(8,128)S(1)} %get-tuple-element.22), channel_id=1, source_target_pairs={{1,0},{2,1},{3,2},{4,3},{5,4},{6,5},{7,6},{9,8},{10,9},{11,10},{12... | collective-permute-start | bytes 1769480 | tf_op jit(solution)/shard_map/ppermute | solution.py:249
  66.0 9.6 %copy-start.7 = (f32[8,16,128]{2,1,0:T(8,128)}, f32[8,16,128]{2,1,0:T(8,128)S(1)}, u32[]{:S(2)}) copy-start(f32[8,16,128]{2,1,0:T(8,128)S(1)} %all_to_all.11.fc_ref) | copy-start | bytes 196612
  66.0 7.7 %collective-permute-start.4 = (f32[8,16,128]{2,1,0:T(8,128)S(1)}, f32[8,16,128]{2,1,0:T(8,128)S(1)}, u32[]{:S(2)}, u32[]{:S(2)}) collective-permute-start(f32[8,16,128]{2,1,0:T(8,128)S(1)} %all_to_all.11.fc_ref), channel_id=1, source_target_pairs={{0,8},{8,16},{16,24},{24,32},{32,40},{40,48},{48,56},{56,64},{64,7... | collective-permute-start | bytes 196616 | tf_op jit(solution)/shard_map/ppermute | solution.py:249
  68.0 7.6 %collective-permute-start.5 = (f32[8,16,128]{2,1,0:T(8,128)S(1)}, f32[8,16,128]{2,1,0:T(8,128)S(1)}, u32[]{:S(2)}, u32[]{:S(2)}) collective-permute-start(f32[8,16,128]{2,1,0:T(8,128)S(1)} %all_to_all.11.fc_ref), channel_id=1, source_target_pairs={{8,0},{16,8},{24,16},{32,24},{40,32},{48,40},{56,48},{64,56},{72,6... | collective-permute-start | bytes 196616 | tf_op jit(solution)/shard_map/ppermute | solution.py:249
  73.7 1.9 %copy-start.8 = (f32[8,16,128]{2,1,0:T(8,128)}, f32[8,16,128]{2,1,0:T(8,128)S(1)}, u32[]{:S(2)}) copy-start(f32[8,16,128]{2,1,0:T(8,128)S(1)} %collective-permute-done.4.fl_ref) | copy-start | bytes 196612
  75.6 0.6 copy-start.9
  75.6 0.9 copy-start.5
  75.6 1.0 %copy-start.6 = (f32[144,8,128]{2,1,0:T(8,128)}, f32[144,8,128]{2,1,0:T(8,128)S(1)}, u32[]{:S(2)}) copy-start(f32[144,8,128]{2,1,0:T(8,128)S(1)} %collective-permute-done.3.yhi_hbm) | copy-start | bytes 1769476

commit v3 on v2

--- a/solution.py
+++ b/solution.py
@@ -20,7 +20,7 @@
 ROW_BITS, Z_BITS, P_BITS = 12, 7, 12
 BODY = (12, 11, 11, 10, 10, 9, 9, 8)
 GROUP = 16
-LIMIT = 56 * 1024 * 1024
+LIMIT = 28 * 1024 * 1024
 
 
 def vmem_spec():
@@ -61,11 +61,24 @@
 
     lax.fori_loop(0, CX, fill, 0, unroll=2)
     for k, ref in enumerate((now_ref, before_ref, mod_ref)):
-        low_ref[pl.ds(k * H, H)] = ref[pl.ds(0, H)]
-        high_ref[pl.ds(k * H, H)] = ref[pl.ds(CX - H, H)]
-
-
-def transform_kernel(moved_ref, table_ref, owner_ref, cell_ref, out_ref, wide_ref):
+        low_ref[pl.ds(k * CX, CX)] = ref[:, pl.ds(0, H), :]
+        high_ref[pl.ds(k * CX, CX)] = ref[:, pl.ds(CY - H, H), :]
+
+
+def middle_kernel(moved_ref, table_ref, owner_ref, cell_ref, now_hbm, before_hbm, mod_hbm, ylo_hbm, yhi_hbm,
+                  out_ref, low_hbm, high_hbm, wide_ref, sems):
+    copies = []
+    for k, own in enumerate((now_hbm, before_hbm, mod_hbm)):
+        for n, (slab, x) in enumerate(((low_hbm, 0), (high_hbm, CX - H))):
+            rows = slab.at[pl.ds(k * H, H)]
+            for m, (src, y, wide) in enumerate((
+                (ylo_hbm.at[pl.ds(k * CX + x, H)], 0, H),
+                (own.at[pl.ds(x, H)], H, CY),
+                (yhi_hbm.at[pl.ds(k * CX + x, H)], H + CY, H),
+            )):
+                copies.append(pltpu.make_async_copy(src, rows.at[:, pl.ds(y, wide)], sems.at[k, n, m]))
+    for c in copies:
+        c.start()
     for i in range(moved_ref.shape[0]):
         wide_ref[pl.ds(4 * i, 4), :] = moved_ref[i].astype(jnp.float32)
     panel = wide_ref[...].astype(jnp.bfloat16)
@@ -76,21 +89,23 @@
     for a in range(out_ref.shape[0]):
         out_ref[a, 0:8, :] = force
         out_ref[a, 8:16, :] = keys
-
-
-def window_kernel(place_ref, now_hbm, before_hbm, mod_hbm, xlo_hbm, xhi_hbm, ylo_hbm, yhi_hbm,
+    for c in copies:
+        c.wait()
+
+
+def window_kernel(place_ref, now_hbm, before_hbm, mod_hbm, ylo_hbm, yhi_hbm, xlo_hbm, xhi_hbm,
                   fl_ref, fc_ref, fr_ref, next_hbm, prior_hbm,
-                  a_ref, b_ref, m_ref, kx_ref, ky_ref, kz_ref, kc_ref, d_ref, code_ref, code_smem, list_smem,
+                  a_ref, b_ref, m_ref, kx_ref, ky_ref, kz_ref, kc_ref, d_ref, code_ref, rank_ref, code_smem, rank_smem, list_smem,
                   sems, sem_code, sem_out):
     tiles = fc_ref.shape[0]
     copies = []
     for k, (own, ext) in enumerate(((now_hbm, a_ref), (before_hbm, b_ref), (mod_hbm, m_ref))):
         pieces = (
             (own, ext.at[pl.ds(1 + H, CX), pl.ds(2 * H, CY)]),
-            (xlo_hbm.at[pl.ds(k * H, H)], ext.at[pl.ds(1, H), pl.ds(2 * H, CY)]),
-            (xhi_hbm.at[pl.ds(k * H, H)], ext.at[pl.ds(1 + H + CX, H), pl.ds(2 * H, CY)]),
-            (ylo_hbm.at[pl.ds(k * EX, EX)], ext.at[pl.ds(1, EX), pl.ds(H, H)]),
-            (yhi_hbm.at[pl.ds(k * EX, EX)], ext.at[pl.ds(1, EX), pl.ds(2 * H + CY, H)]),
+            (ylo_hbm.at[pl.ds(k * CX, CX)], ext.at[pl.ds(1 + H, CX), pl.ds(H, H)]),
+            (yhi_hbm.at[pl.ds(k * CX, CX)], ext.at[pl.ds(1 + H, CX), pl.ds(2 * H + CY, H)]),
+            (xlo_hbm.at[pl.ds(k * H, H)], ext.at[pl.ds(1, H), pl.ds(H, EY)]),
+            (xhi_hbm.at[pl.ds(k * H, H)], ext.at[pl.ds(1 + H + CX, H), pl.ds(H, EY)]),
         )
         for n, (src, dst) in enumerate(pieces):
             copies.append(pltpu.make_async_copy(src, dst, sems.at[k, n]))
@@ -111,8 +126,25 @@
         place = (side * tiles + part) * NPT + lane
         packed = (row << (Z_BITS + P_BITS)) | ((cell & (CZ - 1)) << P_BITS) | place
         code_ref[pl.ds(side * tiles, tiles), :] = jnp.where(inside, packed, -1)
-    code_copy = pltpu.make_async_copy(code_ref, code_smem, sem_code)
-    code_copy.start()
+    code = code_ref[...]
+    found = jnp.where(code >= 0, 1.0, 0.0)
+    ahead = jnp.where(
+        lax.broadcasted_iota(jnp.int32, (NPT, NPT), 0) < lax.broadcasted_iota(jnp.int32, (NPT, NPT), 1), 1.0, 0.0)
+    in_row = jnp.dot(found.astype(jnp.bfloat16), ahead.astype(jnp.bfloat16), preferred_element_type=jnp.float32)
+    below = jnp.where(
+        lax.broadcasted_iota(jnp.int32, (4 * tiles, 3 * tiles), 0) > lax.broadcasted_iota(jnp.int32, (4 * tiles, 3 * tiles), 1),
+        1.0, 0.0)
+    rows_before = jnp.dot(below.astype(jnp.bfloat16), found.astype(jnp.bfloat16), preferred_element_type=jnp.float32)
+    before = jnp.sum(rows_before, axis=1, keepdims=True)
+    rank_ref[pl.ds(0, 3 * tiles), :] = jnp.where(
+        code >= 0, in_row + before[0:3 * tiles], 3.0 * tiles * NPT + GROUP).astype(jnp.int32)
+    rank_ref[pl.ds(3 * tiles, tiles), :] = jnp.broadcast_to(before[3 * tiles:4 * tiles], (tiles, NPT)).astype(jnp.int32)
+    code_copies = (
+        pltpu.make_async_copy(code_ref, code_smem, sem_code.at[0]),
+        pltpu.make_async_copy(rank_ref, rank_smem, sem_code.at[1]),
+    )
+    for c in code_copies:
+        c.start()
 
     def clear(i, _):
         base = pl.multiple_of(i * 64, 64)
@@ -121,16 +153,16 @@
         return 0
 
     lax.fori_loop(0, ROWS * STEPS // 64, clear, 0)
-    code_copy.wait()
-
-    def pick_row(r, count):
+    for c in code_copies:
+        c.wait()
+
+    def pick_row(r, _):
         for c in range(NPT):
-            code = code_smem[r, c]
-            list_smem[count] = code
-            count = count + jnp.where(code >= 0, 1, 0)
-        return count
-
-    count = lax.fori_loop(0, 3 * tiles, pick_row, 0)
+            list_smem[rank_smem[r, c]] = code_smem[r, c]
+        return 0
+
+    lax.fori_loop(0, 3 * tiles, pick_row, 0)
+    count = rank_smem[3 * tiles, 0]
     for j in range(GROUP):
         list_smem[count + j] = 0
 
@@ -184,6 +216,10 @@
 
     lax.fori_loop(0, EX // 8, coefficients, 0)
 
+    next_copy, prior_copy = (
+        pltpu.make_async_copy(ref.at[pl.ds(1 + H, CX), pl.ds(2 * H, CY)], hbm, sem_out.at[n])
+        for n, (ref, hbm) in enumerate(((a_ref, next_hbm), (b_ref, prior_hbm)))
+    )
     for step in range(STEPS):
         u_ref, w_ref = (a_ref, b_ref) if step % 2 == 0 else (b_ref, a_ref)
 
@@ -210,14 +246,11 @@
 
         lax.fori_loop(0, 4, advance, 0)
 
-    outs = [
-        pltpu.make_async_copy(ref.at[pl.ds(1 + H, CX), pl.ds(2 * H, CY)], hbm, sem_out.at[n])
-        for n, (ref, hbm) in enumerate(((a_ref, next_hbm), (b_ref, prior_hbm)))
-    ]
-    for c in outs:
-        c.start()
-    for c in outs:
-        c.wait()
+        if step == STEPS - 2:
+            prior_copy.start()
+    next_copy.start()
+    next_copy.wait()
+    prior_copy.wait()
 
 
 def window(place, fields, forces):
@@ -232,10 +265,12 @@
         scratch_shapes=[buffer] * 7 + [
             pltpu.VMEM((ROWS * STEPS, CZ), jnp.float32),
             pltpu.VMEM((3 * tiles, NPT), jnp.int32),
+            pltpu.VMEM((4 * tiles, NPT), jnp.int32),
             pltpu.SMEM((3 * tiles, NPT), jnp.int32),
-            pltpu.SMEM((3 * tiles * NPT + 8,), jnp.int32),
+            pltpu.SMEM((4 * tiles, NPT), jnp.int32),
+            pltpu.SMEM((3 * tiles * NPT + 2 * GROUP,), jnp.int32),
             pltpu.SemaphoreType.DMA((3, 5)),
-            pltpu.SemaphoreType.DMA,
+            pltpu.SemaphoreType.DMA((2,)),
             pltpu.SemaphoreType.DMA((2,)),
         ],
         compiler_params=pltpu.CompilerParams(vmem_limit_bytes=LIMIT),
@@ -252,7 +287,7 @@
 def shards(field_now, field_before, layer, modulus_table, fk_panel, owner, local_cell):
     sources, tiles = lax.axis_size("along"), lax.axis_size("across")
     local_freqs = fk_panel.shape[1]
-    slab = jax.ShapeDtypeStruct((3 * H, CY, CZ), jnp.float32)
+    slab = jax.ShapeDtypeStruct((3 * CX, H, CZ), jnp.float32)
     low, high, dealt, modulus = pl.pallas_call(
         prepare_kernel,
         out_shape=(
@@ -266,29 +301,26 @@
         compiler_params=pltpu.CompilerParams(vmem_limit_bytes=LIMIT),
     )(modulus_table, field_now, field_before, layer, fk_panel.reshape(2, local_freqs, sources * NPT))
     arrays = (field_now, field_before, modulus)
+    ylo, yhi = neighbours(low, high, "across")
+    moved = lax.all_to_all(dealt, "along", 0, 0, tiled=True)
+    ylo, yhi, moved = lax.optimization_barrier((ylo, yhi, moved))
+
+    slab = jax.ShapeDtypeStruct((3 * H, EY, CZ), jnp.float32)
+    payload, low, high = pl.pallas_call(
+        middle_kernel,
+        out_shape=(jax.ShapeDtypeStruct((tiles, 16, NPT), jnp.float32), slab, slab),
+        in_specs=[vmem_spec()] * 4 + [any_spec()] * 5,
+        out_specs=(vmem_spec(), any_spec(), any_spec()),
+        scratch_shapes=[
+            pltpu.VMEM((2 * local_freqs * sources, NPT), jnp.float32),
+            pltpu.SemaphoreType.DMA((3, 2, 3)),
+        ],
+    )(moved, jnp.asarray(split_table(sources, local_freqs)), owner.reshape(1, NPT), local_cell, *arrays, ylo, yhi)
     xlo, xhi = neighbours(low, high, "along")
-    moved = lax.all_to_all(dealt, "along", 0, 0, tiled=True)
-    xlo, xhi, moved = lax.optimization_barrier((xlo, xhi, moved))
-
-    def side(rows):
-        return jnp.concatenate(
-            [p[:, rows] for k, a in enumerate(arrays) for p in (xlo[k * H:k * H + H], a, xhi[k * H:k * H + H])],
-            axis=0,
-        )
-
-    ylo, yhi = neighbours(side(slice(0, H)), side(slice(CY - H, CY)), "across")
-
-    payload = pl.pallas_call(
-        transform_kernel,
-        out_shape=jax.ShapeDtypeStruct((tiles, 16, NPT), jnp.float32),
-        in_specs=[vmem_spec()] * 4,
-        out_specs=vmem_spec(),
-        scratch_shapes=[pltpu.VMEM((2 * local_freqs * sources, NPT), jnp.float32)],
-    )(moved, jnp.asarray(split_table(sources, local_freqs)), owner.reshape(1, NPT), local_cell)
     center = lax.all_to_all(payload, "across", 0, 0, tiled=True)
     left, right = neighbours(center, center, "along")
     place = lax.axis_index("across").astype(jnp.int32).reshape(1)
-    return window(place, (*arrays, xlo, xhi, ylo, yhi), (left, center, right))
+    return window(place, (*arrays, ylo, yhi, xlo, xhi), (left, center, right))
 
 
 def solution(mesh):

time: 102 us -> 140 us (1.37)
  the two profiles are of different devices: /device:TPU:58 before, /device:TPU:2 now
where the time goes in v3:
time: 140 us; the launch traced here: 139 us
  Pallas kernels  58.3 us (42%)
  blocking collectives  50 us (36%)
  starting transfers between devices  16.8 us (12%)
  local copies, waits for them, and re-layouts  8.3 us (6%)
  waiting for transfers between devices  5.28 us (4%)
    pallas_call x1, Pallas kernels, shards(): pl.pallas_call(middle_kernel, out_shape=(jax.ShapeDtypeStruct((tiles, 16,...  38.7 us
    all_to_all x1, blocking collectives, shards(): moved = lax.all_to_all(dealt, 'along', 0, 0, tiled=True)  32.3 us
    pallas_call x1, Pallas kernels, window(): pl.pallas_call(window_kernel, out_shape=(grid, grid), in_specs=[pl.BlockS...  18.7 us
    all_to_all x1, blocking collectives, shards(): center = lax.all_to_all(payload, 'across', 0, 0, tiled=True)  17.7 us
    ppermute x6, starting transfers between devices, neighbours(): return (lax.ppermute(high, axis, up), lax.ppermute(low, axis, down))  16.8 us
    unnamed x26, local copies, waits for them, and re-layouts  8.3 us
    ppermute x6, waiting for transfers between devices, neighbours(): return (lax.ppermute(high, axis, up), lax.ppermute(low, axis, down))  5.28 us
  transfers between devices with their start and end apart: 6, of which 1 were waited for; matrix products, arithmetic and copies ran while one was open for 0% of the time, Pallas kernels for 0%

profile of v3, /device:TPU:2, one launch (start us, length us, event | category | flops | bytes accessed | tf_op | source)
XLA Modules:
  0.0 139.5 jit_solution(18276471966394902624)
XLA Ops:
  0.6 0.0 copy-start.12
  0.6 0.6 copy-done.12
  1.3 0.0 copy-start
  1.3 1.0 copy-done
  2.3 0.0 copy-start.2
  2.3 1.0 copy-done.2
  3.4 0.0 copy-start.10
  3.4 1.0 copy-done.10
  4.4 0.0 copy-start.11
  4.4 0.9 copy-done.11
  5.3 1.0 shard_map.95
  6.3 0.0 copy-start.4
  6.3 0.8 copy-done.4
  7.1 3.5 %collective-permute-start = (f32[96,8,128]{2,1,0:T(8,128)S(1)}, f32[96,8,128]{2,1,0:T(8,128)S(1)}, u32[]{:S(2)}, u32[]{:S(2)}) collective-permute-start(f32[96,8,128]{2,1,0:T(8,128)S(1)} %get-tuple-element.13), channel_id=1, source_target_pairs={{0,1},{1,2},{2,3},{3,4},{4,5},{5,6},{6,7},{8,9},{9,10},{10,11},{11... | collective-permute-start | bytes 1179656 | tf_op jit(solution)/shard_map/ppermute | solution.py:284
  10.6 1.3 collective-permute-start.1
  11.9 32.3 %all_to_all.10.moved_ref = bf16[96,4,128]{2,1,0:T(4,128)(2,1)} all-to-all(bf16[96,4,128]{2,1,0:T(4,128)(2,1)S(1)} %get-tuple-element.15), channel_id=1, replica_groups=mesh['along'=96,'across'=8] {'along'}, dimensions={0} | all-to-all | bytes 196608 | tf_op jit(solution)/shard_map/all_to_all | solution.py:305
  44.2 0.0 collective-permute-done.ylo_hbm
  44.2 0.0 copy-start.6
  44.2 0.0 collective-permute-done.1.yhi_hbm
  44.2 0.0 copy-start.8
  44.2 0.7 copy-done.6
  44.9 0.1 copy-done.8
  45.1 0.0 copy-start.1
  45.1 0.0 copy-start.3
  45.1 0.0 copy-start.5
  45.1 38.7 %shard_map.96 = (f32[8,16,128]{2,1,0:T(8,128)}, f32[24,48,128]{2,1,0:T(8,128)}, f32[24,48,128]{2,1,0:T(8,128)}) custom-call(bf16[96,4,128]{2,1,0:T(4,128)(2,1)} %all_to_all.10.moved_ref, bf16[24,384]{1,0:T(8,128)(2,1)} %constant.6.clone.table_ref, s32[1,128]{1,0:T(1,128)} %bitcast.4, s32[1,128]{1,0:T(1,128)} %cell_ref.1, f32[32,32,128]{2,1,0:T(8,128)} %now_hbm.3, ...), custom_call_target="tpu_custom_call" | custom-call | tf_op jit(solution)/shard_map/pallas_call | solution.py:309
  83.7 1.9 %collective-permute-start.2 = (f32[24,48,128]{2,1,0:T(8,128)}, f32[24,48,128]{2,1,0:T(8,128)S(1)}, u32[]{:S(2)}, u32[]{:S(2)}) collective-permute-start(f32[24,48,128]{2,1,0:T(8,128)} %get-tuple-element.19), channel_id=1, source_target_pairs={{0,8},{8,16},{16,24},{24,32},{32,40},{40,48},{48,56},{56,64},{64,7... | collective-permute-start | bytes 1769480 | tf_op jit(solution)/shard_map/ppermute | solution.py:284
  85.7 5.8 %collective-permute-start.3 = (f32[24,48,128]{2,1,0:T(8,128)}, f32[24,48,128]{2,1,0:T(8,128)S(1)}, u32[]{:S(2)}, u32[]{:S(2)}) collective-permute-start(f32[24,48,128]{2,1,0:T(8,128)} %get-tuple-element.20), channel_id=1, source_target_pairs={{8,0},{16,8},{24,16},{32,24},{40,32},{48,40},{56,48},{64,56},{72,6... | collective-permute-start | bytes 1769480 | tf_op jit(solution)/shard_map/ppermute | solution.py:284
  91.4 17.7 %all_to_all.11.fc_ref = f32[8,16,128]{2,1,0:T(8,128)S(1)} all-to-all(f32[8,16,128]{2,1,0:T(8,128)} %get-tuple-element.21), channel_id=1, replica_groups=mesh['along'=96,'across'=8] {'across'}, dimensions={0} | all-to-all | bytes 131072 | tf_op jit(solution)/shard_map/all_to_all | solution.py:320
  109.2 1.9 %collective-permute-start.5 = (f32[8,16,128]{2,1,0:T(8,128)S(1)}, f32[8,16,128]{2,1,0:T(8,128)S(1)}, u32[]{:S(2)}, u32[]{:S(2)}) collective-permute-start(f32[8,16,128]{2,1,0:T(8,128)S(1)} %all_to_all.11.fc_ref), channel_id=1, source_target_pairs={{8,0},{16,8},{24,16},{32,24},{40,32},{48,40},{56,48},{64,56},{72,6... | collective-permute-start | bytes 196616 | tf_op jit(solution)/shard_map/ppermute | solution.py:284
  111.1 2.4 %collective-permute-start.4 = (f32[8,16,128]{2,1,0:T(8,128)S(1)}, f32[8,16,128]{2,1,0:T(8,128)S(1)}, u32[]{:S(2)}, u32[]{:S(2)}) collective-permute-start(f32[8,16,128]{2,1,0:T(8,128)S(1)} %all_to_all.11.fc_ref), channel_id=1, source_target_pairs={{0,8},{8,16},{16,24},{24,32},{32,40},{40,48},{48,56},{56,64},{64,7... | collective-permute-start | bytes 196616 | tf_op jit(solution)/shard_map/ppermute | solution.py:284
  113.5 0.0 collective-permute-done.5.fr_ref
  113.5 5.3 %collective-permute-done.4.fl_ref = f32[8,16,128]{2,1,0:T(8,128)S(1)} collective-permute-done((f32[8,16,128]{2,1,0:T(8,128)S(1)}, f32[8,16,128]{2,1,0:T(8,128)S(1)}, u32[]{:S(2)}, u32[]{:S(2)}) %collective-permute-start.4) | collective-permute-done | bytes 65568 | tf_op jit(solution)/shard_map/ppermute | solution.py:284
  118.8 0.0 collective-permute-done.2.xlo_hbm
  118.8 0.0 collective-permute-done.3.xhi_hbm
  118.8 0.0 copy-done.1
  118.8 0.0 copy-done.3
  118.8 0.0 copy-done.5
  118.8 0.0 copy-start.7
  118.8 1.0 copy-done.7
  119.8 0.0 copy-start.9
  119.8 1.0 copy-done.9
  120.8 18.7 %shard_map.97 = (f32[32,32,128]{2,1,0:T(8,128)}, f32[32,32,128]{2,1,0:T(8,128)}) custom-call(s32[1]{0:T(128)} %bitcast.place_ref, f32[32,32,128]{2,1,0:T(8,128)S(1)} %copy-done.1, f32[32,32,128]{2,1,0:T(8,128)S(1)} %copy-done.3, f32[32,32,128]{2,1,0:T(8,128)S(1)} %copy-done.5, f32[96,8,128]{2,1,0:T(8,128)S(1)} %copy-done.7, f32[96,8,128]{2,1,0:T(8,128)S(1)} %copy-done.9, ...), custom_call_target="tpu_custom_call" | custom-call | tf_op jit(solution)/shard_map/pallas_call | solution.py:260
Async XLA Ops:
  0.6 0.7 copy-start.12
  1.3 1.0 copy-start
  2.3 1.0 copy-start.2
  3.4 1.0 copy-start.10
  4.4 0.9 copy-start.11
  6.3 0.8 copy-start.4
  7.1 37.1 %collective-permute-start = (f32[96,8,128]{2,1,0:T(8,128)S(1)}, f32[96,8,128]{2,1,0:T(8,128)S(1)}, u32[]{:S(2)}, u32[]{:S(2)}) collective-permute-start(f32[96,8,128]{2,1,0:T(8,128)S(1)} %get-tuple-element.13), channel_id=1, source_target_pairs={{0,1},{1,2},{2,3},{3,4},{4,5},{5,6},{6,7},{8,9},{9,10},{10,11},{11... | collective-permute-start | bytes 1179656 | tf_op jit(solution)/shard_map/ppermute | solution.py:284
  10.6 33.6 %collective-permute-start.1 = (f32[96,8,128]{2,1,0:T(8,128)S(1)}, f32[96,8,128]{2,1,0:T(8,128)S(1)}, u32[]{:S(2)}, u32[]{:S(2)}) collective-permute-start(f32[96,8,128]{2,1,0:T(8,128)S(1)} %get-tuple-element.14), channel_id=1, source_target_pairs={{1,0},{2,1},{3,2},{4,3},{5,4},{6,5},{7,6},{9,8},{10,9},{11,10},{12... | collective-permute-start | bytes 1179656 | tf_op jit(solution)/shard_map/ppermute | solution.py:284
  44.2 0.7 copy-start.6
  44.2 0.9 copy-start.8
  45.1 73.7 %copy-start.1 = (f32[32,32,128]{2,1,0:T(8,128)S(1)}, f32[32,32,128]{2,1,0:T(8,128)}, u32[]{:S(2)}) copy-start(f32[32,32,128]{2,1,0:T(8,128)} %now_hbm.3) | copy-start | bytes 1572868
  45.1 73.7 %copy-start.3 = (f32[32,32,128]{2,1,0:T(8,128)S(1)}, f32[32,32,128]{2,1,0:T(8,128)}, u32[]{:S(2)}) copy-start(f32[32,32,128]{2,1,0:T(8,128)} %before_hbm.3) | copy-start | bytes 1572868
  45.1 73.7 %copy-start.5 = (f32[32,32,128]{2,1,0:T(8,128)S(1)}, f32[32,32,128]{2,1,0:T(8,128)}, u32[]{:S(2)}) copy-start(f32[32,32,128]{2,1,0:T(8,128)} %copy-done.4) | copy-start | bytes 1572868
  83.7 35.0 %collective-permute-start.2 = (f32[24,48,128]{2,1,0:T(8,128)}, f32[24,48,128]{2,1,0:T(8,128)S(1)}, u32[]{:S(2)}, u32[]{:S(2)}) collective-permute-start(f32[24,48,128]{2,1,0:T(8,128)} %get-tuple-element.19), channel_id=1, source_target_pairs={{0,8},{8,16},{16,24},{24,32},{32,40},{40,48},{48,56},{56,64},{64,7... | collective-permute-start | bytes 1769480 | tf_op jit(solution)/shard_map/ppermute | solution.py:284
  85.7 33.1 %collective-permute-start.3 = (f32[24,48,128]{2,1,0:T(8,128)}, f32[24,48,128]{2,1,0:T(8,128)S(1)}, u32[]{:S(2)}, u32[]{:S(2)}) collective-permute-start(f32[24,48,128]{2,1,0:T(8,128)} %get-tuple-element.20), channel_id=1, source_target_pairs={{8,0},{16,8},{24,16},{32,24},{40,32},{48,40},{56,48},{64,56},{72,6... | collective-permute-start | bytes 1769480 | tf_op jit(solution)/shard_map/ppermute | solution.py:284
  109.2 4.3 %collective-permute-start.5 = (f32[8,16,128]{2,1,0:T(8,128)S(1)}, f32[8,16,128]{2,1,0:T(8,128)S(1)}, u32[]{:S(2)}, u32[]{:S(2)}) collective-permute-start(f32[8,16,128]{2,1,0:T(8,128)S(1)} %all_to_all.11.fc_ref), channel_id=1, source_target_pairs={{8,0},{16,8},{24,16},{32,24},{40,32},{48,40},{56,48},{64,56},{72,6... | collective-permute-start | bytes 196616 | tf_op jit(solution)/shard_map/ppermute | solution.py:284
  111.1 7.7 %collective-permute-start.4 = (f32[8,16,128]{2,1,0:T(8,128)S(1)}, f32[8,16,128]{2,1,0:T(8,128)S(1)}, u32[]{:S(2)}, u32[]{:S(2)}) collective-permute-start(f32[8,16,128]{2,1,0:T(8,128)S(1)} %all_to_all.11.fc_ref), channel_id=1, source_target_pairs={{0,8},{8,16},{16,24},{24,32},{32,40},{40,48},{48,56},{56,64},{64,7... | collective-permute-start | bytes 196616 | tf_op jit(solution)/shard_map/ppermute | solution.py:284
  118.8 1.0 copy-start.7
  119.8 1.0 copy-start.9

commit v4 on v3

--- a/solution.py
+++ b/solution.py
@@ -20,7 +20,7 @@
 ROW_BITS, Z_BITS, P_BITS = 12, 7, 12
 BODY = (12, 11, 11, 10, 10, 9, 9, 8)
 GROUP = 16
-LIMIT = 28 * 1024 * 1024
+LIMIT = 58 * 1024 * 1024
 
 
 def vmem_spec():
@@ -66,10 +66,10 @@
 
 
 def middle_kernel(moved_ref, table_ref, owner_ref, cell_ref, now_hbm, before_hbm, mod_hbm, ylo_hbm, yhi_hbm,
-                  out_ref, low_hbm, high_hbm, wide_ref, sems):
+                  out_ref, low_ref, high_ref, wide_ref, sems):
     copies = []
     for k, own in enumerate((now_hbm, before_hbm, mod_hbm)):
-        for n, (slab, x) in enumerate(((low_hbm, 0), (high_hbm, CX - H))):
+        for n, (slab, x) in enumerate(((low_ref, 0), (high_ref, CX - H))):
             rows = slab.at[pl.ds(k * H, H)]
             for m, (src, y, wide) in enumerate((
                 (ylo_hbm.at[pl.ds(k * CX + x, H)], 0, H),
@@ -310,11 +310,12 @@
         middle_kernel,
         out_shape=(jax.ShapeDtypeStruct((tiles, 16, NPT), jnp.float32), slab, slab),
         in_specs=[vmem_spec()] * 4 + [any_spec()] * 5,
-        out_specs=(vmem_spec(), any_spec(), any_spec()),
+        out_specs=(vmem_spec(),) * 3,
         scratch_shapes=[
             pltpu.VMEM((2 * local_freqs * sources, NPT), jnp.float32),
             pltpu.SemaphoreType.DMA((3, 2, 3)),
         ],
+        compiler_params=pltpu.CompilerParams(vmem_limit_bytes=LIMIT),
     )(moved, jnp.asarray(split_table(sources, local_freqs)), owner.reshape(1, NPT), local_cell, *arrays, ylo, yhi)
     xlo, xhi = neighbours(low, high, "along")
     center = lax.all_to_all(payload, "across", 0, 0, tiled=True)

time: 140 us -> 102 us (0.73)
  Pallas kernels: 58.3 us -> 26.6 us
  local copies, waits for them, and re-layouts: 8.3 us -> 1.9 us
    pallas_call x1, Pallas kernels: 38.7 us -> 3.45 us  [shards(): pl.pallas_call(middle_kernel, out_shape=(jax.ShapeDtypeStruct((tiles, 16,...]
    unnamed x26 -> x14, local copies, waits for them, and re-layouts: 8.3 us -> 1.9 us
    pallas_call x1, Pallas kernels: 1 us -> 2.89 us  [shards(): pl.pallas_call(prepare_kernel, out_shape=(slab, slab, jax.ShapeDtypeStruc...]
    pallas_call x1, Pallas kernels: 18.7 us -> 20.3 us  [window(): pl.pallas_call(window_kernel, out_shape=(grid, grid), in_specs=[pl.BlockS...]
where the time goes in v4:
time: 102 us
  blocking collectives  50.3 us (49%)
  Pallas kernels  26.6 us (26%)
  starting transfers between devices  16.8 us (16%)
  waiting for transfers between devices  5.27 us (5%)
  local copies, waits for them, and re-layouts  1.9 us (2%)
    all_to_all x1, blocking collectives, shards(): moved = lax.all_to_all(dealt, 'along', 0, 0, tiled=True)  32.6 us
    pallas_call x1, Pallas kernels, window(): pl.pallas_call(window_kernel, out_shape=(grid, grid), in_specs=[pl.BlockS...  20.3 us
    all_to_all x1, blocking collectives, shards(): center = lax.all_to_all(payload, 'across', 0, 0, tiled=True)  17.7 us
    ppermute x6, starting transfers between devices, neighbours(): return (lax.ppermute(high, axis, up), lax.ppermute(low, axis, down))  16.8 us
    ppermute x6, waiting for transfers between devices, neighbours(): return (lax.ppermute(high, axis, up), lax.ppermute(low, axis, down))  5.27 us
    pallas_call x1, Pallas kernels, shards(): pl.pallas_call(middle_kernel, out_shape=(jax.ShapeDtypeStruct((tiles, 16,...  3.45 us
    pallas_call x1, Pallas kernels, shards(): pl.pallas_call(prepare_kernel, out_shape=(slab, slab, jax.ShapeDtypeStruc...  2.89 us
  transfers between devices with their start and end apart: 6, of which 1 were waited for; matrix products, arithmetic and copies ran while one was open for 0% of the time, Pallas kernels for 0%

profile of v4, /device:TPU:2, one launch (start us, length us, event | category | flops | bytes accessed | tf_op | source)
XLA Modules:
  0.0 101.6 jit_solution(1111067201641338358)
XLA Ops:
  0.6 2.9 %shard_map.95 = (f32[96,8,128]{2,1,0:T(8,128)}, f32[96,8,128]{2,1,0:T(8,128)}, bf16[96,4,128]{2,1,0:T(4,128)(2,1)}, f32[32,32,128]{2,1,0:T(8,128)}) custom-call(f32[8]{0:T(128)} %table_ref.2, f32[32,32,128]{2,1,0:T(8,128)} %now_hbm.3, f32[32,32,128]{2,1,0:T(8,128)} %before_hbm.3, s32[32,32,128]{2,1,0:T(8,128)} %layer_ref.1, bf16[2,2,12288]{2,1,0:T(2,128)(2,1)} %bitcast.3), custom_call_target="tpu_custom_call" | custom-call | tf_op jit(solution)/shard_map/pallas_call | solution.py:291
  3.5 3.5 %collective-permute-start = (f32[96,8,128]{2,1,0:T(8,128)}, f32[96,8,128]{2,1,0:T(8,128)S(1)}, u32[]{:S(2)}, u32[]{:S(2)}) collective-permute-start(f32[96,8,128]{2,1,0:T(8,128)} %get-tuple-element.13), channel_id=1, source_target_pairs={{0,1},{1,2},{2,3},{3,4},{4,5},{5,6},{6,7},{8,9},{9,10},{10,11},{11... | collective-permute-start | bytes 1179656 | tf_op jit(solution)/shard_map/ppermute | solution.py:284
  7.0 1.3 %collective-permute-start.1 = (f32[96,8,128]{2,1,0:T(8,128)}, f32[96,8,128]{2,1,0:T(8,128)S(1)}, u32[]{:S(2)}, u32[]{:S(2)}) collective-permute-start(f32[96,8,128]{2,1,0:T(8,128)} %get-tuple-element.14), channel_id=1, source_target_pairs={{1,0},{2,1},{3,2},{4,3},{5,4},{6,5},{7,6},{9,8},{10,9},{11,10},{12... | collective-permute-start | bytes 1179656 | tf_op jit(solution)/shard_map/ppermute | solution.py:284
  8.3 32.6 %all_to_all.10.moved_ref = bf16[96,4,128]{2,1,0:T(4,128)(2,1)} all-to-all(bf16[96,4,128]{2,1,0:T(4,128)(2,1)} %get-tuple-element.15), channel_id=1, replica_groups=mesh['along'=96,'across'=8] {'along'}, dimensions={0} | all-to-all | bytes 196608 | tf_op jit(solution)/shard_map/all_to_all | solution.py:305
  40.9 0.0 collective-permute-done.ylo_hbm
  40.9 0.0 copy-start
  40.9 0.0 collective-permute-done.1.yhi_hbm
  40.9 0.0 copy-start.1
  40.9 0.7 copy-done
  41.7 0.1 copy-done.1
  41.8 3.4 %shard_map.96 = (f32[8,16,128]{2,1,0:T(8,128)}, f32[24,48,128]{2,1,0:T(8,128)}, f32[24,48,128]{2,1,0:T(8,128)}) custom-call(bf16[96,4,128]{2,1,0:T(4,128)(2,1)} %all_to_all.10.moved_ref, bf16[24,384]{1,0:T(8,128)(2,1)} %constant.6.clone.table_ref, s32[1,128]{1,0:T(1,128)} %bitcast.4, s32[1,128]{1,0:T(1,128)} %cell_ref.1, f32[32,32,128]{2,1,0:T(8,128)} %now_hbm.3, ...), custom_call_target="tpu_custom_call" | custom-call | tf_op jit(solution)/shard_map/pallas_call | solution.py:309
  45.3 1.9 %collective-permute-start.2 = (f32[24,48,128]{2,1,0:T(8,128)}, f32[24,48,128]{2,1,0:T(8,128)S(1)}, u32[]{:S(2)}, u32[]{:S(2)}) collective-permute-start(f32[24,48,128]{2,1,0:T(8,128)} %get-tuple-element.19), channel_id=1, source_target_pairs={{0,8},{8,16},{16,24},{24,32},{32,40},{40,48},{48,56},{56,64},{64,7... | collective-permute-start | bytes 1769480 | tf_op jit(solution)/shard_map/ppermute | solution.py:284
  47.2 5.8 %collective-permute-start.3 = (f32[24,48,128]{2,1,0:T(8,128)}, f32[24,48,128]{2,1,0:T(8,128)S(1)}, u32[]{:S(2)}, u32[]{:S(2)}) collective-permute-start(f32[24,48,128]{2,1,0:T(8,128)} %get-tuple-element.20), channel_id=1, source_target_pairs={{8,0},{16,8},{24,16},{32,24},{40,32},{48,40},{56,48},{64,56},{72,6... | collective-permute-start | bytes 1769480 | tf_op jit(solution)/shard_map/ppermute | solution.py:284
  52.9 17.7 %all_to_all.11.fc_ref = f32[8,16,128]{2,1,0:T(8,128)S(1)} all-to-all(f32[8,16,128]{2,1,0:T(8,128)} %get-tuple-element.21), channel_id=1, replica_groups=mesh['along'=96,'across'=8] {'across'}, dimensions={0} | all-to-all | bytes 131072 | tf_op jit(solution)/shard_map/all_to_all | solution.py:321
  70.7 0.0 copy-start.4
  70.7 1.9 %collective-permute-start.5 = (f32[8,16,128]{2,1,0:T(8,128)S(1)}, f32[8,16,128]{2,1,0:T(8,128)S(1)}, u32[]{:S(2)}, u32[]{:S(2)}) collective-permute-start(f32[8,16,128]{2,1,0:T(8,128)S(1)} %all_to_all.11.fc_ref), channel_id=1, source_target_pairs={{8,0},{16,8},{24,16},{32,24},{40,32},{48,40},{56,48},{64,56},{72,6... | collective-permute-start | bytes 196616 | tf_op jit(solution)/shard_map/ppermute | solution.py:284
  72.6 2.4 %collective-permute-start.4 = (f32[8,16,128]{2,1,0:T(8,128)S(1)}, f32[8,16,128]{2,1,0:T(8,128)S(1)}, u32[]{:S(2)}, u32[]{:S(2)}) collective-permute-start(f32[8,16,128]{2,1,0:T(8,128)S(1)} %all_to_all.11.fc_ref), channel_id=1, source_target_pairs={{0,8},{8,16},{16,24},{24,32},{32,40},{40,48},{48,56},{56,64},{64,7... | collective-permute-start | bytes 196616 | tf_op jit(solution)/shard_map/ppermute | solution.py:284
  75.0 0.0 collective-permute-done.5.fr_ref
  75.0 0.0 copy-start.5
  75.0 5.3 %collective-permute-done.4.fl_ref = f32[8,16,128]{2,1,0:T(8,128)S(1)} collective-permute-done((f32[8,16,128]{2,1,0:T(8,128)S(1)}, f32[8,16,128]{2,1,0:T(8,128)S(1)}, u32[]{:S(2)}, u32[]{:S(2)}) %collective-permute-start.4) | collective-permute-done | bytes 65568 | tf_op jit(solution)/shard_map/ppermute | solution.py:284
  80.3 0.0 copy-start.6
  80.3 0.0 collective-permute-done.2.xlo_hbm
  80.3 0.0 copy-start.2
  80.3 0.0 collective-permute-done.3.xhi_hbm
  80.3 0.0 copy-start.3
  80.3 0.0 copy-done.4
  80.3 0.0 copy-done.5
  80.3 0.6 copy-done.6
  80.9 0.2 copy-done.2
  81.1 0.2 copy-done.3
  81.4 20.3 %shard_map.97 = (f32[32,32,128]{2,1,0:T(8,128)}, f32[32,32,128]{2,1,0:T(8,128)}) custom-call(s32[1]{0:T(128)} %bitcast.place_ref, f32[32,32,128]{2,1,0:T(8,128)} %now_hbm.3, f32[32,32,128]{2,1,0:T(8,128)} %before_hbm.3, f32[32,32,128]{2,1,0:T(8,128)} %get-tuple-element.12.mod_hbm, f32[96,8,128]{2,1,0:T(8,128)} %copy-done, f32[96,8,128]{2,1,0:T(8,128)} %copy-done.1, ...), custom_call_target="tpu_custom_call" | custom-call | tf_op jit(solution)/shard_map/pallas_call | solution.py:260
Async XLA Ops:
  3.5 37.4 %collective-permute-start = (f32[96,8,128]{2,1,0:T(8,128)}, f32[96,8,128]{2,1,0:T(8,128)S(1)}, u32[]{:S(2)}, u32[]{:S(2)}) collective-permute-start(f32[96,8,128]{2,1,0:T(8,128)} %get-tuple-element.13), channel_id=1, source_target_pairs={{0,1},{1,2},{2,3},{3,4},{4,5},{5,6},{6,7},{8,9},{9,10},{10,11},{11... | collective-permute-start | bytes 1179656 | tf_op jit(solution)/shard_map/ppermute | solution.py:284
  7.0 33.9 %collective-permute-start.1 = (f32[96,8,128]{2,1,0:T(8,128)}, f32[96,8,128]{2,1,0:T(8,128)S(1)}, u32[]{:S(2)}, u32[]{:S(2)}) collective-permute-start(f32[96,8,128]{2,1,0:T(8,128)} %get-tuple-element.14), channel_id=1, source_target_pairs={{1,0},{2,1},{3,2},{4,3},{5,4},{6,5},{7,6},{9,8},{10,9},{11,10},{12... | collective-permute-start | bytes 1179656 | tf_op jit(solution)/shard_map/ppermute | solution.py:284
  40.9 0.8 copy-start
  40.9 0.9 copy-start.1
  45.3 35.0 %collective-permute-start.2 = (f32[24,48,128]{2,1,0:T(8,128)}, f32[24,48,128]{2,1,0:T(8,128)S(1)}, u32[]{:S(2)}, u32[]{:S(2)}) collective-permute-start(f32[24,48,128]{2,1,0:T(8,128)} %get-tuple-element.19), channel_id=1, source_target_pairs={{0,8},{8,16},{16,24},{24,32},{32,40},{40,48},{48,56},{56,64},{64,7... | collective-permute-start | bytes 1769480 | tf_op jit(solution)/shard_map/ppermute | solution.py:284
  47.2 33.1 %collective-permute-start.3 = (f32[24,48,128]{2,1,0:T(8,128)}, f32[24,48,128]{2,1,0:T(8,128)S(1)}, u32[]{:S(2)}, u32[]{:S(2)}) collective-permute-start(f32[24,48,128]{2,1,0:T(8,128)} %get-tuple-element.20), channel_id=1, source_target_pairs={{8,0},{16,8},{24,16},{32,24},{40,32},{48,40},{56,48},{64,56},{72,6... | collective-permute-start | bytes 1769480 | tf_op jit(solution)/shard_map/ppermute | solution.py:284
  70.7 9.6 %copy-start.4 = (f32[8,16,128]{2,1,0:T(8,128)}, f32[8,16,128]{2,1,0:T(8,128)S(1)}, u32[]{:S(2)}) copy-start(f32[8,16,128]{2,1,0:T(8,128)S(1)} %all_to_all.11.fc_ref) | copy-start | bytes 196612
  70.7 4.3 %collective-permute-start.5 = (f32[8,16,128]{2,1,0:T(8,128)S(1)}, f32[8,16,128]{2,1,0:T(8,128)S(1)}, u32[]{:S(2)}, u32[]{:S(2)}) collective-permute-start(f32[8,16,128]{2,1,0:T(8,128)S(1)} %all_to_all.11.fc_ref), channel_id=1, source_target_pairs={{8,0},{16,8},{24,16},{32,24},{40,32},{48,40},{56,48},{64,56},{72,6... | collective-permute-start | bytes 196616 | tf_op jit(solution)/shard_map/ppermute | solution.py:284
  72.6 7.7 %collective-permute-start.4 = (f32[8,16,128]{2,1,0:T(8,128)S(1)}, f32[8,16,128]{2,1,0:T(8,128)S(1)}, u32[]{:S(2)}, u32[]{:S(2)}) collective-permute-start(f32[8,16,128]{2,1,0:T(8,128)S(1)} %all_to_all.11.fc_ref), channel_id=1, source_target_pairs={{0,8},{8,16},{16,24},{24,32},{32,40},{40,48},{48,56},{56,64},{64,7... | collective-permute-start | bytes 196616 | tf_op jit(solution)/shard_map/ppermute | solution.py:284
  75.0 5.3 %copy-start.5 = (f32[8,16,128]{2,1,0:T(8,128)}, f32[8,16,128]{2,1,0:T(8,128)S(1)}, u32[]{:S(2)}) copy-start(f32[8,16,128]{2,1,0:T(8,128)S(1)} %collective-permute-done.5.fr_ref) | copy-start | bytes 196612
  80.3 0.6 copy-start.6
  80.3 0.8 copy-start.2
  80.3 1.0 %copy-start.3 = (f32[24,48,128]{2,1,0:T(8,128)}, f32[24,48,128]{2,1,0:T(8,128)S(1)}, u32[]{:S(2)}) copy-start(f32[24,48,128]{2,1,0:T(8,128)S(1)} %collective-permute-done.3.xhi_hbm) | copy-start | bytes 1769476

commit v5 on v4

--- a/solution.py
+++ b/solution.py
@@ -20,7 +20,8 @@
 ROW_BITS, Z_BITS, P_BITS = 12, 7, 12
 BODY = (12, 11, 11, 10, 10, 9, 9, 8)
 GROUP = 16
-LIMIT = 58 * 1024 * 1024
+MIB = 1024 * 1024
+PARTS = 4 * H
 
 
 def vmem_spec():
@@ -65,8 +66,18 @@
         high_ref[pl.ds(k * CX, CX)] = ref[:, pl.ds(CY - H, H), :]
 
 
-def middle_kernel(moved_ref, table_ref, owner_ref, cell_ref, now_hbm, before_hbm, mod_hbm, ylo_hbm, yhi_hbm,
-                  out_ref, low_ref, high_ref, wide_ref, sems):
+def transform_kernel(moved_ref, table_ref, owner_ref, cell_ref, out_ref, wide_ref):
+    for i in range(moved_ref.shape[0]):
+        wide_ref[pl.ds(4 * i, 4), :] = moved_ref[i].astype(jnp.float32)
+    panel = wide_ref[...].astype(jnp.bfloat16)
+    parts = jnp.dot(table_ref[...], panel, preferred_element_type=jnp.float32)
+    out_ref[0:8, :] = parts[0:8] + parts[8:16] + parts[16:24]
+    key = (owner_ref[...] * CELLS + cell_ref[...] + 1).astype(jnp.float32)
+    out_ref[8:16, :] = jnp.broadcast_to(key, (8, NPT))
+
+
+def spread_kernel(own_ref, left_ref, right_ref, now_hbm, before_hbm, mod_hbm, ylo_hbm, yhi_hbm,
+                  out_ref, low_ref, high_ref, sems):
     copies = []
     for k, own in enumerate((now_hbm, before_hbm, mod_hbm)):
         for n, (slab, x) in enumerate(((low_ref, 0), (high_ref, CX - H))):
@@ -79,25 +90,22 @@
                 copies.append(pltpu.make_async_copy(src, rows.at[:, pl.ds(y, wide)], sems.at[k, n, m]))
     for c in copies:
         c.start()
-    for i in range(moved_ref.shape[0]):
-        wide_ref[pl.ds(4 * i, 4), :] = moved_ref[i].astype(jnp.float32)
-    panel = wide_ref[...].astype(jnp.bfloat16)
-    parts = jnp.dot(table_ref[...], panel, preferred_element_type=jnp.float32)
-    force = parts[0:8] + parts[8:16] + parts[16:24]
-    key = (owner_ref[...] * CELLS + cell_ref[...] + 1).astype(jnp.float32)
-    keys = jnp.broadcast_to(key, (8, NPT))
+    line = lax.broadcasted_iota(jnp.int32, (8, NPT), 0)
+    keys = jnp.where(line == 0, own_ref[8:16, :], jnp.where(line == 1, left_ref[8:16, :], right_ref[8:16, :]))
     for a in range(out_ref.shape[0]):
-        out_ref[a, 0:8, :] = force
-        out_ref[a, 8:16, :] = keys
+        out_ref[a, 0:8, :] = own_ref[0:8, :]
+        out_ref[a, 8:16, :] = left_ref[0:8, :]
+        out_ref[a, 16:24, :] = right_ref[0:8, :]
+        out_ref[a, 24:32, :] = keys
     for c in copies:
         c.wait()
 
 
 def window_kernel(place_ref, now_hbm, before_hbm, mod_hbm, ylo_hbm, yhi_hbm, xlo_hbm, xhi_hbm,
-                  fl_ref, fc_ref, fr_ref, next_hbm, prior_hbm,
-                  a_ref, b_ref, m_ref, kx_ref, ky_ref, kz_ref, kc_ref, d_ref, code_ref, rank_ref, code_smem, rank_smem, list_smem,
+                  got_ref, next_hbm, prior_hbm,
+                  a_ref, b_ref, m_ref, kx_ref, ky_ref, kz_ref, kc_ref, d_ref, code_ref, code_smem, list_smem,
                   sems, sem_code, sem_out):
-    tiles = fc_ref.shape[0]
+    tiles = got_ref.shape[0]
     copies = []
     for k, (own, ext) in enumerate(((now_hbm, a_ref), (before_hbm, b_ref), (mod_hbm, m_ref))):
         pieces = (
@@ -115,36 +123,44 @@
     my_y = place_ref[0]
     lane = lax.broadcasted_iota(jnp.int32, (tiles, NPT), 1)
     part = lax.broadcasted_iota(jnp.int32, (tiles, NPT), 0)
-    for side, f_ref in enumerate((fl_ref, fc_ref, fr_ref)):
-        key = f_ref[:, 8, :].astype(jnp.int32) - 1
+    codes = []
+    for side in range(3):
+        key = got_ref[:, 24 + side, :].astype(jnp.int32) - 1
         own = key >> 17
         cell = key & (CELLS - 1)
-        gx = (cell >> 12) + (side - 1) * CX + H
+        gx = (cell >> 12) + (0, -CX, CX)[side] + H
         gy = (own - my_y) * CY + ((cell >> 7) & (CY - 1)) + H
         inside = (key >= 0) & (gx >= 1) & (gx < EX - 1) & (gy >= 1) & (gy < EY - 1)
         row = gx * EY + gy
-        place = (side * tiles + part) * NPT + lane
+        place = (part * 4 + side) * NPT + lane
         packed = (row << (Z_BITS + P_BITS)) | ((cell & (CZ - 1)) << P_BITS) | place
-        code_ref[pl.ds(side * tiles, tiles), :] = jnp.where(inside, packed, -1)
-    code = code_ref[...]
+        codes.append(jnp.where(inside, packed, -1))
+
+    rows = 3 * tiles
+    code = jnp.concatenate(codes, axis=0)
     found = jnp.where(code >= 0, 1.0, 0.0)
     ahead = jnp.where(
         lax.broadcasted_iota(jnp.int32, (NPT, NPT), 0) < lax.broadcasted_iota(jnp.int32, (NPT, NPT), 1), 1.0, 0.0)
-    in_row = jnp.dot(found.astype(jnp.bfloat16), ahead.astype(jnp.bfloat16), preferred_element_type=jnp.float32)
-    below = jnp.where(
-        lax.broadcasted_iota(jnp.int32, (4 * tiles, 3 * tiles), 0) > lax.broadcasted_iota(jnp.int32, (4 * tiles, 3 * tiles), 1),
-        1.0, 0.0)
-    rows_before = jnp.dot(below.astype(jnp.bfloat16), found.astype(jnp.bfloat16), preferred_element_type=jnp.float32)
-    before = jnp.sum(rows_before, axis=1, keepdims=True)
-    rank_ref[pl.ds(0, 3 * tiles), :] = jnp.where(
-        code >= 0, in_row + before[0:3 * tiles], 3.0 * tiles * NPT + GROUP).astype(jnp.int32)
-    rank_ref[pl.ds(3 * tiles, tiles), :] = jnp.broadcast_to(before[3 * tiles:4 * tiles], (tiles, NPT)).astype(jnp.int32)
-    code_copies = (
-        pltpu.make_async_copy(code_ref, code_smem, sem_code.at[0]),
-        pltpu.make_async_copy(rank_ref, rank_smem, sem_code.at[1]),
-    )
-    for c in code_copies:
-        c.start()
+    rank = jnp.dot(found.astype(jnp.bfloat16), ahead.astype(jnp.bfloat16), preferred_element_type=jnp.float32)
+    rank = jnp.where(code >= 0, rank, -1.0)
+    held = jnp.maximum(code, 0)
+    pieces = jnp.concatenate([(held >> (8 * k)) & 255 for k in range(4)], axis=0).astype(jnp.float32)
+    slot = lax.broadcasted_iota(jnp.int32, (NPT, NPT), 0).astype(jnp.float32)
+    which = lax.broadcasted_iota(jnp.int32, (rows, NPT), 0)
+    which = jnp.concatenate([which] * 4, axis=0)
+    front = jnp.zeros((4 * rows, NPT), jnp.float32)
+    for r in range(rows):
+        hot = jnp.where(jnp.broadcast_to(rank[r:r + 1, :], (NPT, NPT)) == slot, 1.0, 0.0).astype(jnp.bfloat16)
+        mine = jnp.where(which == r, pieces, 0.0).astype(jnp.bfloat16)
+        front = front + lax.dot_general(mine, hot, (((1,), (1,)), ((), ())), preferred_element_type=jnp.float32)
+    front = front.astype(jnp.int32)
+    ordered = front[0:rows]
+    for k in range(1, 4):
+        ordered = ordered | (front[k * rows:(k + 1) * rows] << (8 * k))
+    code_ref[0:rows, :] = ordered
+    code_ref[rows:2 * rows, :] = jnp.broadcast_to(jnp.sum(found, axis=1, keepdims=True), (rows, NPT)).astype(jnp.int32)
+    code_copy = pltpu.make_async_copy(code_ref, code_smem, sem_code)
+    code_copy.start()
 
     def clear(i, _):
         base = pl.multiple_of(i * 64, 64)
@@ -153,19 +169,21 @@
         return 0
 
     lax.fori_loop(0, ROWS * STEPS // 64, clear, 0)
-    for c in code_copies:
-        c.wait()
-
-    def pick_row(r, _):
-        for c in range(NPT):
-            list_smem[rank_smem[r, c]] = code_smem[r, c]
-        return 0
-
-    lax.fori_loop(0, 3 * tiles, pick_row, 0)
-    count = rank_smem[3 * tiles, 0]
+    code_copy.wait()
+
+    def join_row(r, count):
+        def move(i, _):
+            for j in range(8):
+                list_smem[count + 8 * i + j] = code_smem[r, 8 * i + j]
+            return 0
+
+        held_here = code_smem[rows + r, 0]
+        lax.fori_loop(0, (held_here + 7) // 8, move, 0)
+        return count + held_here
+
+    count = lax.fori_loop(0, rows, join_row, 0)
     for j in range(GROUP):
         list_smem[count + j] = 0
-
     zline = lax.broadcasted_iota(jnp.int32, (STEPS, CZ), 1)
 
     def add_points(i, _):
@@ -175,17 +193,14 @@
             place = code & ((1 << P_BITS) - 1)
             z = (code >> P_BITS) & (CZ - 1)
             row = code >> (Z_BITS + P_BITS)
-            force = f_all[place >> 7, 0:8, :]
+            side = (place >> 7) & 3
+            force = got_ref[place >> 9, pl.ds(pl.multiple_of(side * STEPS, STEPS), STEPS), :]
             column = jnp.take_along_axis(force, jnp.full((STEPS, CZ), place & (NPT - 1), jnp.int32), axis=1)
             adds.append((pl.ds(pl.multiple_of(row * STEPS, STEPS), STEPS), jnp.where(zline == z, column, 0.0)))
         for at, add in adds:
             d_ref[at, :] = d_ref[at, :] + add
         return 0
 
-    f_all = kc_ref
-    for side, f_ref in enumerate((fl_ref, fc_ref, fr_ref)):
-        for a in range(tiles):
-            kc_ref[side * tiles + a, 0:8, :] = f_ref[a, 0:8, :]
     lax.fori_loop(0, (count + GROUP - 1) // GROUP, add_points, 0)
 
     for c in copies:
@@ -253,28 +268,26 @@
     prior_copy.wait()
 
 
-def window(place, fields, forces):
-    tiles = forces[0].shape[0]
+def window(place, fields, got):
+    tiles = got.shape[0]
     grid = jax.ShapeDtypeStruct((CX, CY, CZ), jnp.float32)
     buffer = pltpu.VMEM((EX + 2, PY, CZ), jnp.float32)
     return pl.pallas_call(
         window_kernel,
         out_shape=(grid, grid),
-        in_specs=[pl.BlockSpec(memory_space=pltpu.SMEM)] + [any_spec()] * 7 + [vmem_spec()] * 3,
+        in_specs=[pl.BlockSpec(memory_space=pltpu.SMEM)] + [any_spec()] * 7 + [vmem_spec()],
         out_specs=(any_spec(), any_spec()),
         scratch_shapes=[buffer] * 7 + [
             pltpu.VMEM((ROWS * STEPS, CZ), jnp.float32),
-            pltpu.VMEM((3 * tiles, NPT), jnp.int32),
-            pltpu.VMEM((4 * tiles, NPT), jnp.int32),
-            pltpu.SMEM((3 * tiles, NPT), jnp.int32),
-            pltpu.SMEM((4 * tiles, NPT), jnp.int32),
+            pltpu.VMEM((6 * tiles, NPT), jnp.int32),
+            pltpu.SMEM((6 * tiles, NPT), jnp.int32),
             pltpu.SMEM((3 * tiles * NPT + 2 * GROUP,), jnp.int32),
             pltpu.SemaphoreType.DMA((3, 5)),
-            pltpu.SemaphoreType.DMA((2,)),
+            pltpu.SemaphoreType.DMA,
             pltpu.SemaphoreType.DMA((2,)),
         ],
-        compiler_params=pltpu.CompilerParams(vmem_limit_bytes=LIMIT),
-    )(place, *fields, *forces)
+        compiler_params=pltpu.CompilerParams(vmem_limit_bytes=28 * MIB),
+    )(place, *fields, got)
 
 
 def neighbours(low, high, axis):
@@ -298,30 +311,35 @@
         ),
         in_specs=[pl.BlockSpec(memory_space=pltpu.SMEM)] + [vmem_spec()] * 4,
         out_specs=(vmem_spec(),) * 4,
-        compiler_params=pltpu.CompilerParams(vmem_limit_bytes=LIMIT),
+        compiler_params=pltpu.CompilerParams(vmem_limit_bytes=58 * MIB),
     )(modulus_table, field_now, field_before, layer, fk_panel.reshape(2, local_freqs, sources * NPT))
     arrays = (field_now, field_before, modulus)
     ylo, yhi = neighbours(low, high, "across")
     moved = lax.all_to_all(dealt, "along", 0, 0, tiled=True)
     ylo, yhi, moved = lax.optimization_barrier((ylo, yhi, moved))
 
+    samples = pl.pallas_call(
+        transform_kernel,
+        out_shape=jax.ShapeDtypeStruct((2 * STEPS, NPT), jnp.float32),
+        in_specs=[vmem_spec()] * 4,
+        out_specs=vmem_spec(),
+        scratch_shapes=[pltpu.VMEM((2 * local_freqs * sources, NPT), jnp.float32)],
+        compiler_params=pltpu.CompilerParams(vmem_limit_bytes=4 * MIB),
+    )(moved, jnp.asarray(split_table(sources, local_freqs)), owner.reshape(1, NPT), local_cell)
+    left, right = neighbours(samples, samples, "along")
     slab = jax.ShapeDtypeStruct((3 * H, EY, CZ), jnp.float32)
-    payload, low, high = pl.pallas_call(
-        middle_kernel,
-        out_shape=(jax.ShapeDtypeStruct((tiles, 16, NPT), jnp.float32), slab, slab),
-        in_specs=[vmem_spec()] * 4 + [any_spec()] * 5,
+    spread, low, high = pl.pallas_call(
+        spread_kernel,
+        out_shape=(jax.ShapeDtypeStruct((tiles, PARTS, NPT), jnp.float32), slab, slab),
+        in_specs=[vmem_spec()] * 3 + [any_spec()] * 5,
         out_specs=(vmem_spec(),) * 3,
-        scratch_shapes=[
-            pltpu.VMEM((2 * local_freqs * sources, NPT), jnp.float32),
-            pltpu.SemaphoreType.DMA((3, 2, 3)),
-        ],
-        compiler_params=pltpu.CompilerParams(vmem_limit_bytes=LIMIT),
-    )(moved, jnp.asarray(split_table(sources, local_freqs)), owner.reshape(1, NPT), local_cell, *arrays, ylo, yhi)
+        scratch_shapes=[pltpu.SemaphoreType.DMA((3, 2, 3))],
+        compiler_params=pltpu.CompilerParams(vmem_limit_bytes=8 * MIB),
+    )(samples, left, right, *arrays, ylo, yhi)
     xlo, xhi = neighbours(low, high, "along")
-    center = lax.all_to_all(payload, "across", 0, 0, tiled=True)
-    left, right = neighbours(center, center, "along")
+    got = lax.all_to_all(spread, "across", 0, 0, tiled=True)
     place = lax.axis_index("across").astype(jnp.int32).reshape(1)
-    return window(place, (*arrays, ylo, yhi, xlo, xhi), (left, center, right))
+    return window(place, (*arrays, ylo, yhi, xlo, xhi), got)
 
 
 def solution(mesh):

time: 102 us -> 99 us (0.971)
  the two profiles are of different devices: /device:TPU:2 before, /device:TPU:26 now
where the time goes in v5:
time: 99 us; the launch traced here: 98.5 us
  blocking collectives  32.4 us (33%)
  Pallas kernels  26.4 us (27%)
  starting transfers between devices  26.3 us (27%)
  waiting for transfers between devices  10.3 us (10%)
  local copies, waits for them, and re-layouts  2.36 us (2%)
    all_to_all x1, blocking collectives, shards(): moved = lax.all_to_all(dealt, 'along', 0, 0, tiled=True)  32.4 us
    pallas_call x1, Pallas kernels, window(): pl.pallas_call(window_kernel, out_shape=(grid, grid), in_specs=[pl.BlockS...  21.9 us
    ppermute x6, starting transfers between devices, neighbours(): return (lax.ppermute(high, axis, up), lax.ppermute(low, axis, down))  18.6 us
    all_to_all x1, starting transfers between devices, shards(): got = lax.all_to_all(spread, 'across', 0, 0, tiled=True)  7.77 us
    all_to_all x1, waiting for transfers between devices, shards(): got = lax.all_to_all(spread, 'across', 0, 0, tiled=True)  5.58 us
    ppermute x6, waiting for transfers between devices, neighbours(): return (lax.ppermute(high, axis, up), lax.ppermute(low, axis, down))  4.67 us
    pallas_call x1, Pallas kernels, shards(): pl.pallas_call(prepare_kernel, out_shape=(slab, slab, jax.ShapeDtypeStruc...  2.97 us
    unnamed x16, local copies, waits for them, and re-layouts  2.36 us
  transfers between devices with their start and end apart: 7, of which 2 were waited for; matrix products, arithmetic and copies ran while one was open for 0% of the time, Pallas kernels for 0%

profile of v5, /device:TPU:26, one launch (start us, length us, event | category | flops | bytes accessed | tf_op | source)
XLA Modules:
  0.0 98.5 jit_solution(7948915128147332485)
XLA Ops:
  0.6 0.0 copy-start
  0.6 0.0 copy-start.1
  0.7 3.0 %shard_map.95 = (f32[96,8,128]{2,1,0:T(8,128)}, f32[96,8,128]{2,1,0:T(8,128)}, bf16[96,4,128]{2,1,0:T(4,128)(2,1)}, f32[32,32,128]{2,1,0:T(8,128)}) custom-call(f32[8]{0:T(128)} %table_ref.2, f32[32,32,128]{2,1,0:T(8,128)} %now_hbm.3, f32[32,32,128]{2,1,0:T(8,128)} %before_hbm.3, s32[32,32,128]{2,1,0:T(8,128)} %layer_ref.1, bf16[2,2,12288]{2,1,0:T(2,128)(2,1)} %bitcast.4), custom_call_target="tpu_custom_call" | custom-call | tf_op jit(solution)/shard_map/pallas_call | solution.py:304
  3.6 4.7 %collective-permute-start = (f32[96,8,128]{2,1,0:T(8,128)}, f32[96,8,128]{2,1,0:T(8,128)S(1)}, u32[]{:S(2)}, u32[]{:S(2)}) collective-permute-start(f32[96,8,128]{2,1,0:T(8,128)} %get-tuple-element.13), channel_id=1, source_target_pairs={{0,1},{1,2},{2,3},{3,4},{4,5},{5,6},{6,7},{8,9},{9,10},{10,11},{11... | collective-permute-start | bytes 1179656 | tf_op jit(solution)/shard_map/ppermute | solution.py:297
  8.3 1.9 %collective-permute-start.1 = (f32[96,8,128]{2,1,0:T(8,128)}, f32[96,8,128]{2,1,0:T(8,128)S(1)}, u32[]{:S(2)}, u32[]{:S(2)}) collective-permute-start(f32[96,8,128]{2,1,0:T(8,128)} %get-tuple-element.14), channel_id=1, source_target_pairs={{1,0},{2,1},{3,2},{4,3},{5,4},{6,5},{7,6},{9,8},{10,9},{11,10},{12... | collective-permute-start | bytes 1179656 | tf_op jit(solution)/shard_map/ppermute | solution.py:297
  10.2 0.0 copy-start.5
  10.3 32.4 %all_to_all.10.moved_ref = bf16[96,4,128]{2,1,0:T(4,128)(2,1)S(1)} all-to-all(bf16[96,4,128]{2,1,0:T(4,128)(2,1)} %get-tuple-element.15), channel_id=1, replica_groups=mesh['along'=96,'across'=8] {'along'}, dimensions={0} | all-to-all | bytes 196608 | tf_op jit(solution)/shard_map/all_to_all | solution.py:318
  42.6 0.0 copy-start.6
  42.6 0.0 copy-start.7
  42.6 0.0 collective-permute-done.ylo_hbm
  42.6 0.0 collective-permute-done.1.yhi_hbm
  42.6 0.0 copy-done.5
  42.7 0.6 copy-done.6
  43.3 0.0 copy-done.7
  43.3 0.1 shard_map.96.own_ref
  43.4 1.9 %collective-permute-start.3 = (f32[16,128]{1,0:T(8,128)S(1)}, f32[16,128]{1,0:T(8,128)S(1)}, u32[]{:S(2)}, u32[]{:S(2)}) collective-permute-start(f32[16,128]{1,0:T(8,128)S(1)} %shard_map.96.own_ref), channel_id=1, source_target_pairs={{8,0},{16,8},{24,16},{32,24},{40,32},{48,40},{56,48},{64,56},{72,6... | collective-permute-start | bytes 24584 | tf_op jit(solution)/shard_map/ppermute | solution.py:297
  45.4 2.4 %collective-permute-start.2 = (f32[16,128]{1,0:T(8,128)S(1)}, f32[16,128]{1,0:T(8,128)S(1)}, u32[]{:S(2)}, u32[]{:S(2)}) collective-permute-start(f32[16,128]{1,0:T(8,128)S(1)} %shard_map.96.own_ref), channel_id=1, source_target_pairs={{0,8},{8,16},{16,24},{24,32},{32,40},{40,48},{48,56},{56,64},{64,7... | collective-permute-start | bytes 24584 | tf_op jit(solution)/shard_map/ppermute | solution.py:297
  47.8 0.0 collective-permute-done.3.right_ref
  47.8 4.7 %collective-permute-done.2.left_ref = f32[16,128]{1,0:T(8,128)S(1)} collective-permute-done((f32[16,128]{1,0:T(8,128)S(1)}, f32[16,128]{1,0:T(8,128)S(1)}, u32[]{:S(2)}, u32[]{:S(2)}) %collective-permute-start.2) | collective-permute-done | bytes 8224 | tf_op jit(solution)/shard_map/ppermute | solution.py:297
  52.4 0.0 copy-done
  52.5 0.0 copy-done.1
  52.5 0.0 copy-start.2
  52.5 1.0 %copy-done.2 = f32[32,32,128]{2,1,0:T(8,128)S(1)} copy-done((f32[32,32,128]{2,1,0:T(8,128)S(1)}, f32[32,32,128]{2,1,0:T(8,128)}, u32[]{:S(2)}) %copy-start.2) | copy-done | bytes 524312
  53.5 0.0 copy-start.3
  53.5 1.4 %shard_map.97 = (f32[8,32,128]{2,1,0:T(8,128)S(1)}, f32[24,48,128]{2,1,0:T(8,128)}, f32[24,48,128]{2,1,0:T(8,128)}) custom-call(f32[16,128]{1,0:T(8,128)S(1)} %shard_map.96.own_ref, f32[16,128]{1,0:T(8,128)S(1)} %collective-permute-done.2.left_ref, f32[16,128]{1,0:T(8,128)S(1)} %collective-permute-done.3.right_ref, f32[32,32,128]{2,1,0:T(8,128)S(1)} %copy-done, ...), custom_call_target="tpu_custom_call" | custom-call | tf_op jit(solution)/shard_map/pallas_call | solution.py:331
  54.9 0.0 copy-start.4
  55.0 0.6 copy-done.4
  55.6 1.9 %collective-permute-start.4 = (f32[24,48,128]{2,1,0:T(8,128)}, f32[24,48,128]{2,1,0:T(8,128)S(1)}, u32[]{:S(2)}, u32[]{:S(2)}) collective-permute-start(f32[24,48,128]{2,1,0:T(8,128)} %get-tuple-element.19), channel_id=1, source_target_pairs={{0,8},{8,16},{16,24},{24,32},{32,40},{40,48},{48,56},{56,64},{64,7... | collective-permute-start | bytes 1769480 | tf_op jit(solution)/shard_map/ppermute | solution.py:297
  57.5 5.8 %collective-permute-start.5 = (f32[24,48,128]{2,1,0:T(8,128)}, f32[24,48,128]{2,1,0:T(8,128)S(1)}, u32[]{:S(2)}, u32[]{:S(2)}) collective-permute-start(f32[24,48,128]{2,1,0:T(8,128)} %get-tuple-element.20), channel_id=1, source_target_pairs={{8,0},{16,8},{24,16},{32,24},{40,32},{48,40},{56,48},{64,56},{72,6... | collective-permute-start | bytes 1769480 | tf_op jit(solution)/shard_map/ppermute | solution.py:297
  63.3 7.8 %all-to-all-start.1 = ((f32[8,32,128]{2,1,0:T(8,128)}), f32[8,32,128]{2,1,0:T(8,128)}, u32[]{:S(2)}, u32[]{:S(2)}) async-start(f32[8,32,128]{2,1,0:T(8,128)} %copy-done.4), calls=%async_computation.1 | async-start | bytes 262144 | tf_op jit(solution)/shard_map/all_to_all | solution.py:340
  71.0 5.6 %all-to-all-done.1.got_ref = f32[8,32,128]{2,1,0:T(8,128)} async-done(((f32[8,32,128]{2,1,0:T(8,128)}), f32[8,32,128]{2,1,0:T(8,128)}, u32[]{:S(2)}, u32[]{:S(2)}) %all-to-all-start.1) | async-done | bytes 131104 | tf_op jit(solution)/shard_map/all_to_all | solution.py:340
  76.6 0.0 collective-permute-done.4.xlo_hbm
  76.6 0.0 collective-permute-done.5.xhi_hbm
  76.6 0.0 copy-done.3
  76.6 21.9 %shard_map.98 = (f32[32,32,128]{2,1,0:T(8,128)}, f32[32,32,128]{2,1,0:T(8,128)}) custom-call(s32[1]{0:T(128)} %bitcast.place_ref, f32[32,32,128]{2,1,0:T(8,128)S(1)} %copy-done, f32[32,32,128]{2,1,0:T(8,128)S(1)} %copy-done.1, f32[32,32,128]{2,1,0:T(8,128)S(1)} %copy-done.3, f32[96,8,128]{2,1,0:T(8,128)S(1)} %collective-permute-done.ylo_hbm, ...), custom_call_target="tpu_custom_call" | custom-call | tf_op jit(solution)/shard_map/pallas_call | solution.py:275
Async XLA Ops:
  0.6 51.8 %copy-start = (f32[32,32,128]{2,1,0:T(8,128)S(1)}, f32[32,32,128]{2,1,0:T(8,128)}, u32[]{:S(2)}) copy-start(f32[32,32,128]{2,1,0:T(8,128)} %now_hbm.3) | copy-start | bytes 1572868
  0.6 51.8 %copy-start.1 = (f32[32,32,128]{2,1,0:T(8,128)S(1)}, f32[32,32,128]{2,1,0:T(8,128)}, u32[]{:S(2)}) copy-start(f32[32,32,128]{2,1,0:T(8,128)} %before_hbm.3) | copy-start | bytes 1572868
  3.6 39.0 %collective-permute-start = (f32[96,8,128]{2,1,0:T(8,128)}, f32[96,8,128]{2,1,0:T(8,128)S(1)}, u32[]{:S(2)}, u32[]{:S(2)}) collective-permute-start(f32[96,8,128]{2,1,0:T(8,128)} %get-tuple-element.13), channel_id=1, source_target_pairs={{0,1},{1,2},{2,3},{3,4},{4,5},{5,6},{6,7},{8,9},{9,10},{10,11},{11... | collective-permute-start | bytes 1179656 | tf_op jit(solution)/shard_map/ppermute | solution.py:297
  8.3 34.3 %collective-permute-start.1 = (f32[96,8,128]{2,1,0:T(8,128)}, f32[96,8,128]{2,1,0:T(8,128)S(1)}, u32[]{:S(2)}, u32[]{:S(2)}) collective-permute-start(f32[96,8,128]{2,1,0:T(8,128)} %get-tuple-element.14), channel_id=1, source_target_pairs={{1,0},{2,1},{3,2},{4,3},{5,4},{6,5},{7,6},{9,8},{10,9},{11,10},{12... | collective-permute-start | bytes 1179656 | tf_op jit(solution)/shard_map/ppermute | solution.py:297
  10.2 32.4 %copy-start.5 = (bf16[24,384]{1,0:T(8,128)(2,1)S(1)}, bf16[24,384]{1,0:T(8,128)(2,1)}, u32[]{:S(2)}) copy-start(bf16[24,384]{1,0:T(8,128)(2,1)} %constant.6.clone.table_ref) | copy-start | bytes 55300
  42.6 0.7 copy-start.6
  42.6 0.7 copy-start.7
  43.4 4.3 %collective-permute-start.3 = (f32[16,128]{1,0:T(8,128)S(1)}, f32[16,128]{1,0:T(8,128)S(1)}, u32[]{:S(2)}, u32[]{:S(2)}) collective-permute-start(f32[16,128]{1,0:T(8,128)S(1)} %shard_map.96.own_ref), channel_id=1, source_target_pairs={{8,0},{16,8},{24,16},{32,24},{40,32},{48,40},{56,48},{64,56},{72,6... | collective-permute-start | bytes 24584 | tf_op jit(solution)/shard_map/ppermute | solution.py:297
  45.4 7.1 %collective-permute-start.2 = (f32[16,128]{1,0:T(8,128)S(1)}, f32[16,128]{1,0:T(8,128)S(1)}, u32[]{:S(2)}, u32[]{:S(2)}) collective-permute-start(f32[16,128]{1,0:T(8,128)S(1)} %shard_map.96.own_ref), channel_id=1, source_target_pairs={{0,8},{8,16},{16,24},{24,32},{32,40},{40,48},{48,56},{56,64},{64,7... | collective-permute-start | bytes 24584 | tf_op jit(solution)/shard_map/ppermute | solution.py:297
  52.5 1.0 %copy-start.2 = (f32[32,32,128]{2,1,0:T(8,128)S(1)}, f32[32,32,128]{2,1,0:T(8,128)}, u32[]{:S(2)}) copy-start(f32[32,32,128]{2,1,0:T(8,128)} %get-tuple-element.12.mod_hbm) | copy-start | bytes 1572868
  53.5 23.1 %copy-start.3 = (f32[32,32,128]{2,1,0:T(8,128)S(1)}, f32[32,32,128]{2,1,0:T(8,128)}, u32[]{:S(2)}) copy-start(f32[32,32,128]{2,1,0:T(8,128)} %get-tuple-element.12.mod_hbm) | copy-start | bytes 1572868
  54.9 0.7 copy-start.4
  55.6 21.0 %collective-permute-start.4 = (f32[24,48,128]{2,1,0:T(8,128)}, f32[24,48,128]{2,1,0:T(8,128)S(1)}, u32[]{:S(2)}, u32[]{:S(2)}) collective-permute-start(f32[24,48,128]{2,1,0:T(8,128)} %get-tuple-element.19), channel_id=1, source_target_pairs={{0,8},{8,16},{16,24},{24,32},{32,40},{40,48},{48,56},{56,64},{64,7... | collective-permute-start | bytes 1769480 | tf_op jit(solution)/shard_map/ppermute | solution.py:297
  57.5 19.1 %collective-permute-start.5 = (f32[24,48,128]{2,1,0:T(8,128)}, f32[24,48,128]{2,1,0:T(8,128)S(1)}, u32[]{:S(2)}, u32[]{:S(2)}) collective-permute-start(f32[24,48,128]{2,1,0:T(8,128)} %get-tuple-element.20), channel_id=1, source_target_pairs={{8,0},{16,8},{24,16},{32,24},{40,32},{48,40},{56,48},{64,56},{72,6... | collective-permute-start | bytes 1769480 | tf_op jit(solution)/shard_map/ppermute | solution.py:297
  63.3 13.4 %all-to-all-start.1 = ((f32[8,32,128]{2,1,0:T(8,128)}), f32[8,32,128]{2,1,0:T(8,128)}, u32[]{:S(2)}, u32[]{:S(2)}) async-start(f32[8,32,128]{2,1,0:T(8,128)} %copy-done.4), calls=%async_computation.1 | async-start | bytes 262144 | tf_op jit(solution)/shard_map/all_to_all | solution.py:340

commit v6 on v5

--- a/solution.py
+++ b/solution.py
@@ -19,7 +19,7 @@
 NPT = 128
 ROW_BITS, Z_BITS, P_BITS = 12, 7, 12
 BODY = (12, 11, 11, 10, 10, 9, 9, 8)
-GROUP = 16
+GROUP = 32
 MIB = 1024 * 1024
 PARTS = 4 * H
 
@@ -47,23 +47,31 @@
     return np.concatenate(parts, axis=0)
 
 
-def prepare_kernel(table_ref, now_ref, before_ref, layer_ref, fk_ref, low_ref, high_ref, dealt_ref, mod_ref):
+def modulus_of(level, table_ref):
+    modulus = jnp.full(level.shape, table_ref[0], jnp.float32)
+    for k in range(1, table_ref.shape[0]):
+        modulus = jnp.where(level == k, table_ref[k], modulus)
+    return modulus
+
+
+def prepare_kernel(table_ref, now_hbm, before_hbm, layer_hbm, fk_ref, low_ref, high_ref, dealt_ref, level_ref, sems):
+    copies = []
+    for n, (slab, y) in enumerate(((low_ref, 0), (high_ref, CY - H))):
+        for k, (own, dst) in enumerate((
+            (now_hbm, slab.at[pl.ds(0, CX)]),
+            (before_hbm, slab.at[pl.ds(CX, CX)]),
+            (layer_hbm, level_ref.at[n]),
+        )):
+            copies.append(pltpu.make_async_copy(own.at[:, pl.ds(y, H)], dst, sems.at[n, k]))
+    for c in copies:
+        c.start()
     for i in range(dealt_ref.shape[0]):
         for c in range(2):
             dealt_ref[i, pl.ds(2 * c, 2), :] = fk_ref[c, :, pl.ds(i * NPT, NPT)]
-
-    def fill(x, _):
-        level = layer_ref[x]
-        modulus = jnp.full(level.shape, table_ref[0], jnp.float32)
-        for k in range(1, table_ref.shape[0]):
-            modulus = jnp.where(level == k, table_ref[k], modulus)
-        mod_ref[x] = modulus
-        return 0
-
-    lax.fori_loop(0, CX, fill, 0, unroll=2)
-    for k, ref in enumerate((now_ref, before_ref, mod_ref)):
-        low_ref[pl.ds(k * CX, CX)] = ref[:, pl.ds(0, H), :]
-        high_ref[pl.ds(k * CX, CX)] = ref[:, pl.ds(CY - H, H), :]
+    for c in copies:
+        c.wait()
+    for n, slab in enumerate((low_ref, high_ref)):
+        slab[pl.ds(2 * CX, CX)] = modulus_of(level_ref[n], table_ref)
 
 
 def transform_kernel(moved_ref, table_ref, owner_ref, cell_ref, out_ref, wide_ref):
@@ -76,20 +84,26 @@
     out_ref[8:16, :] = jnp.broadcast_to(key, (8, NPT))
 
 
-def spread_kernel(own_ref, left_ref, right_ref, now_hbm, before_hbm, mod_hbm, ylo_hbm, yhi_hbm,
-                  out_ref, low_ref, high_ref, sems):
+def slab_kernel(table_ref, now_hbm, before_hbm, layer_hbm, ylo_hbm, yhi_hbm, low_ref, high_ref, level_ref, sems):
     copies = []
-    for k, own in enumerate((now_hbm, before_hbm, mod_hbm)):
-        for n, (slab, x) in enumerate(((low_ref, 0), (high_ref, CX - H))):
+    for n, (slab, x) in enumerate(((low_ref, 0), (high_ref, CX - H))):
+        for k, own in enumerate((now_hbm, before_hbm, layer_hbm)):
             rows = slab.at[pl.ds(k * H, H)]
-            for m, (src, y, wide) in enumerate((
-                (ylo_hbm.at[pl.ds(k * CX + x, H)], 0, H),
-                (own.at[pl.ds(x, H)], H, CY),
-                (yhi_hbm.at[pl.ds(k * CX + x, H)], H + CY, H),
+            for m, (src, dst) in enumerate((
+                (ylo_hbm.at[pl.ds(k * CX + x, H)], rows.at[:, pl.ds(0, H)]),
+                (own.at[pl.ds(x, H)], level_ref.at[n] if k == 2 else rows.at[:, pl.ds(H, CY)]),
+                (yhi_hbm.at[pl.ds(k * CX + x, H)], rows.at[:, pl.ds(H + CY, H)]),
             )):
-                copies.append(pltpu.make_async_copy(src, rows.at[:, pl.ds(y, wide)], sems.at[k, n, m]))
+                copies.append(pltpu.make_async_copy(src, dst, sems.at[k, n, m]))
     for c in copies:
         c.start()
+    for c in copies:
+        c.wait()
+    for n, slab in enumerate((low_ref, high_ref)):
+        slab[pl.ds(2 * H, H), pl.ds(H, CY), :] = modulus_of(level_ref[n], table_ref)
+
+
+def spread_kernel(own_ref, left_ref, right_ref, out_hbm, out_ref, sem):
     line = lax.broadcasted_iota(jnp.int32, (8, NPT), 0)
     keys = jnp.where(line == 0, own_ref[8:16, :], jnp.where(line == 1, left_ref[8:16, :], right_ref[8:16, :]))
     for a in range(out_ref.shape[0]):
@@ -97,35 +111,19 @@
         out_ref[a, 8:16, :] = left_ref[0:8, :]
         out_ref[a, 16:24, :] = right_ref[0:8, :]
         out_ref[a, 24:32, :] = keys
-    for c in copies:
-        c.wait()
-
-
-def window_kernel(place_ref, now_hbm, before_hbm, mod_hbm, ylo_hbm, yhi_hbm, xlo_hbm, xhi_hbm,
-                  got_ref, next_hbm, prior_hbm,
-                  a_ref, b_ref, m_ref, kx_ref, ky_ref, kz_ref, kc_ref, d_ref, code_ref, code_smem, list_smem,
-                  sems, sem_code, sem_out):
-    tiles = got_ref.shape[0]
-    copies = []
-    for k, (own, ext) in enumerate(((now_hbm, a_ref), (before_hbm, b_ref), (mod_hbm, m_ref))):
-        pieces = (
-            (own, ext.at[pl.ds(1 + H, CX), pl.ds(2 * H, CY)]),
-            (ylo_hbm.at[pl.ds(k * CX, CX)], ext.at[pl.ds(1 + H, CX), pl.ds(H, H)]),
-            (yhi_hbm.at[pl.ds(k * CX, CX)], ext.at[pl.ds(1 + H, CX), pl.ds(2 * H + CY, H)]),
-            (xlo_hbm.at[pl.ds(k * H, H)], ext.at[pl.ds(1, H), pl.ds(H, EY)]),
-            (xhi_hbm.at[pl.ds(k * H, H)], ext.at[pl.ds(1 + H + CX, H), pl.ds(H, EY)]),
-        )
-        for n, (src, dst) in enumerate(pieces):
-            copies.append(pltpu.make_async_copy(src, dst, sems.at[k, n]))
-    for c in copies:
-        c.start()
-
+    copy = pltpu.make_async_copy(out_ref, out_hbm, sem)
+    copy.start()
+    copy.wait()
+
+
+def points_kernel(place_ref, got_ref, d_ref, code_ref, code_smem, list_smem, sem_code):
+    tiles = got_ref.shape[0] // PARTS
     my_y = place_ref[0]
     lane = lax.broadcasted_iota(jnp.int32, (tiles, NPT), 1)
     part = lax.broadcasted_iota(jnp.int32, (tiles, NPT), 0)
     codes = []
     for side in range(3):
-        key = got_ref[:, 24 + side, :].astype(jnp.int32) - 1
+        key = got_ref[pl.ds(24 + side, tiles, stride=PARTS), :].astype(jnp.int32) - 1
         own = key >> 17
         cell = key & (CELLS - 1)
         gx = (cell >> 12) + (0, -CX, CX)[side] + H
@@ -190,22 +188,52 @@
         adds = []
         for j in range(GROUP):
             code = list_smem[GROUP * i + j]
-            place = code & ((1 << P_BITS) - 1)
-            z = (code >> P_BITS) & (CZ - 1)
-            row = code >> (Z_BITS + P_BITS)
-            side = (place >> 7) & 3
-            force = got_ref[place >> 9, pl.ds(pl.multiple_of(side * STEPS, STEPS), STEPS), :]
-            column = jnp.take_along_axis(force, jnp.full((STEPS, CZ), place & (NPT - 1), jnp.int32), axis=1)
-            adds.append((pl.ds(pl.multiple_of(row * STEPS, STEPS), STEPS), jnp.where(zline == z, column, 0.0)))
-        for at, add in adds:
-            d_ref[at, :] = d_ref[at, :] + add
+            force = got_ref[pl.ds(pl.multiple_of((code >> 4) & (31 * STEPS), STEPS), STEPS), :]
+            whole = jnp.full((STEPS, CZ), code, jnp.int32)
+            column = jnp.take_along_axis(force, whole & (NPT - 1), axis=1, mode="promise_in_bounds")
+            add = jnp.where(zline == ((whole >> P_BITS) & (CZ - 1)), column, 0.0)
+            row = (code >> (Z_BITS + P_BITS - 3)) & -STEPS
+            adds.append((pl.ds(pl.multiple_of(row, STEPS), STEPS), row, add))
+        for first in range(0, GROUP, 4):
+            part = adds[first:first + 4]
+            sums = []
+            for k, (at, row, add) in enumerate(part):
+                total = d_ref[at, :] + add
+                for _, other, more in part[:k]:
+                    total = total + jnp.where(other == row, more, 0.0)
+                sums.append(total)
+            for (at, _, _), total in zip(part, sums):
+                d_ref[at, :] = total
         return 0
 
     lax.fori_loop(0, (count + GROUP - 1) // GROUP, add_points, 0)
 
+
+def window_kernel(table_ref, d_ref, now_hbm, before_hbm, layer_hbm, ylo_hbm, yhi_hbm, xlo_hbm, xhi_hbm,
+                  next_hbm, prior_hbm, a_ref, b_ref, m_ref, kx_ref, ky_ref, kz_ref, kc_ref, level_ref, sems, sem_out):
+    copies = []
+    for k, (own, ext) in enumerate(((now_hbm, a_ref), (before_hbm, b_ref), (layer_hbm, m_ref))):
+        pieces = (
+            (own, level_ref if k == 2 else ext.at[pl.ds(1 + H, CX), pl.ds(2 * H, CY)]),
+            (ylo_hbm.at[pl.ds(k * CX, CX)], ext.at[pl.ds(1 + H, CX), pl.ds(H, H)]),
+            (yhi_hbm.at[pl.ds(k * CX, CX)], ext.at[pl.ds(1 + H, CX), pl.ds(2 * H + CY, H)]),
+            (xlo_hbm.at[pl.ds(k * H, H)], ext.at[pl.ds(1, H), pl.ds(H, EY)]),
+            (xhi_hbm.at[pl.ds(k * H, H)], ext.at[pl.ds(1 + H + CX, H), pl.ds(H, EY)]),
+        )
+        for n, (src, dst) in enumerate(pieces):
+            copies.append(pltpu.make_async_copy(src, dst, sems.at[k, n]))
+    for c in copies:
+        c.start()
     for c in copies:
         c.wait()
 
+    def fill(i, _):
+        for k in range(4):
+            x = 4 * i + k
+            m_ref[1 + H + x, pl.ds(2 * H, CY), :] = modulus_of(level_ref[x], table_ref)
+        return 0
+
+    lax.fori_loop(0, CX // 4, fill, 0)
     zpos = lax.broadcasted_iota(jnp.int32, (8, CZ), 1)
 
     def face(c, n):
@@ -268,26 +296,39 @@
     prior_copy.wait()
 
 
-def window(place, fields, got):
+def points(place, got):
     tiles = got.shape[0]
+    return pl.pallas_call(
+        points_kernel,
+        out_shape=pltpu.VMEM((ROWS * STEPS, CZ), jnp.float32),
+        in_specs=[pl.BlockSpec(memory_space=pltpu.SMEM), vmem_spec()],
+        out_specs=vmem_spec(),
+        scratch_shapes=[
+            pltpu.VMEM((6 * tiles, NPT), jnp.int32),
+            pltpu.SMEM((6 * tiles, NPT), jnp.int32),
+            pltpu.SMEM((3 * tiles * NPT + 2 * GROUP,), jnp.int32),
+            pltpu.SemaphoreType.DMA,
+        ],
+        cost_estimate=pl.CostEstimate(flops=10**9, transcendentals=0, bytes_accessed=64 * MIB),
+        compiler_params=pltpu.CompilerParams(vmem_limit_bytes=4 * MIB),
+    )(place, got.reshape(tiles * PARTS, NPT))
+
+
+def window(table, drive, fields):
     grid = jax.ShapeDtypeStruct((CX, CY, CZ), jnp.float32)
     buffer = pltpu.VMEM((EX + 2, PY, CZ), jnp.float32)
     return pl.pallas_call(
         window_kernel,
         out_shape=(grid, grid),
-        in_specs=[pl.BlockSpec(memory_space=pltpu.SMEM)] + [any_spec()] * 7 + [vmem_spec()],
+        in_specs=[pl.BlockSpec(memory_space=pltpu.SMEM), vmem_spec()] + [any_spec()] * 7,
         out_specs=(any_spec(), any_spec()),
         scratch_shapes=[buffer] * 7 + [
-            pltpu.VMEM((ROWS * STEPS, CZ), jnp.float32),
-            pltpu.VMEM((6 * tiles, NPT), jnp.int32),
-            pltpu.SMEM((6 * tiles, NPT), jnp.int32),
-            pltpu.SMEM((3 * tiles * NPT + 2 * GROUP,), jnp.int32),
+            pltpu.VMEM((CX, CY, CZ), jnp.int32),
             pltpu.SemaphoreType.DMA((3, 5)),
-            pltpu.SemaphoreType.DMA,
             pltpu.SemaphoreType.DMA((2,)),
         ],
-        compiler_params=pltpu.CompilerParams(vmem_limit_bytes=28 * MIB),
-    )(place, *fields, got)
+        compiler_params=pltpu.CompilerParams(vmem_limit_bytes=16 * MIB),
+    )(table, pltpu.with_memory_space_constraint(drive, pltpu.VMEM), *fields)
 
 
 def neighbours(low, high, axis):
@@ -300,20 +341,17 @@
 def shards(field_now, field_before, layer, modulus_table, fk_panel, owner, local_cell):
     sources, tiles = lax.axis_size("along"), lax.axis_size("across")
     local_freqs = fk_panel.shape[1]
+    arrays = (field_now, field_before, layer)
+    smem = pl.BlockSpec(memory_space=pltpu.SMEM)
     slab = jax.ShapeDtypeStruct((3 * CX, H, CZ), jnp.float32)
-    low, high, dealt, modulus = pl.pallas_call(
+    low, high, dealt = pl.pallas_call(
         prepare_kernel,
-        out_shape=(
-            slab,
-            slab,
-            jax.ShapeDtypeStruct((sources, 2 * local_freqs, NPT), jnp.bfloat16),
-            jax.ShapeDtypeStruct(field_now.shape, jnp.float32),
-        ),
-        in_specs=[pl.BlockSpec(memory_space=pltpu.SMEM)] + [vmem_spec()] * 4,
-        out_specs=(vmem_spec(),) * 4,
+        out_shape=(slab, slab, jax.ShapeDtypeStruct((sources, 2 * local_freqs, NPT), jnp.bfloat16)),
+        in_specs=[smem] + [any_spec()] * 3 + [vmem_spec()],
+        out_specs=(vmem_spec(),) * 3,
+        scratch_shapes=[pltpu.VMEM((2, CX, H, CZ), jnp.int32), pltpu.SemaphoreType.DMA((2, 3))],
         compiler_params=pltpu.CompilerParams(vmem_limit_bytes=58 * MIB),
-    )(modulus_table, field_now, field_before, layer, fk_panel.reshape(2, local_freqs, sources * NPT))
-    arrays = (field_now, field_before, modulus)
+    )(modulus_table, *arrays, fk_panel.reshape(2, local_freqs, sources * NPT))
     ylo, yhi = neighbours(low, high, "across")
     moved = lax.all_to_all(dealt, "along", 0, 0, tiled=True)
     ylo, yhi, moved = lax.optimization_barrier((ylo, yhi, moved))
@@ -324,22 +362,31 @@
         in_specs=[vmem_spec()] * 4,
         out_specs=vmem_spec(),
         scratch_shapes=[pltpu.VMEM((2 * local_freqs * sources, NPT), jnp.float32)],
-        compiler_params=pltpu.CompilerParams(vmem_limit_bytes=4 * MIB),
+        compiler_params=pltpu.CompilerParams(vmem_limit_bytes=58 * MIB),
     )(moved, jnp.asarray(split_table(sources, local_freqs)), owner.reshape(1, NPT), local_cell)
     left, right = neighbours(samples, samples, "along")
+    spread = pl.pallas_call(
+        spread_kernel,
+        out_shape=pltpu.HBM((tiles, PARTS, NPT), jnp.float32),
+        in_specs=[vmem_spec()] * 3,
+        out_specs=pl.BlockSpec(memory_space=pltpu.HBM),
+        scratch_shapes=[pltpu.VMEM((tiles, PARTS, NPT), jnp.float32), pltpu.SemaphoreType.DMA],
+        compiler_params=pltpu.CompilerParams(vmem_limit_bytes=4 * MIB),
+    )(samples, left, right)
+    got = lax.all_to_all(spread, "across", 0, 0, tiled=True)
     slab = jax.ShapeDtypeStruct((3 * H, EY, CZ), jnp.float32)
-    spread, low, high = pl.pallas_call(
-        spread_kernel,
-        out_shape=(jax.ShapeDtypeStruct((tiles, PARTS, NPT), jnp.float32), slab, slab),
-        in_specs=[vmem_spec()] * 3 + [any_spec()] * 5,
-        out_specs=(vmem_spec(),) * 3,
-        scratch_shapes=[pltpu.SemaphoreType.DMA((3, 2, 3))],
-        compiler_params=pltpu.CompilerParams(vmem_limit_bytes=8 * MIB),
-    )(samples, left, right, *arrays, ylo, yhi)
+    low, high = pl.pallas_call(
+        slab_kernel,
+        out_shape=(slab, slab),
+        in_specs=[smem] + [any_spec()] * 5,
+        out_specs=(vmem_spec(),) * 2,
+        scratch_shapes=[pltpu.VMEM((2, H, CY, CZ), jnp.int32), pltpu.SemaphoreType.DMA((3, 2, 3))],
+        compiler_params=pltpu.CompilerParams(vmem_limit_bytes=58 * MIB),
+    )(modulus_table, *arrays, *lax.optimization_barrier((ylo, yhi, spread))[:2])
     xlo, xhi = neighbours(low, high, "along")
-    got = lax.all_to_all(spread, "across", 0, 0, tiled=True)
     place = lax.axis_index("across").astype(jnp.int32).reshape(1)
-    return window(place, (*arrays, ylo, yhi, xlo, xhi), got)
+    drive = points(place, got)
+    return window(modulus_table, drive, (*arrays, ylo, yhi, xlo, xhi))
 
 
 def solution(mesh):

time: 99 us -> 105 us (1.061)
  the two profiles are of different devices: /device:TPU:26 before, /device:TPU:2 now
where the time goes in v6:
time: 105 us
  blocking collectives  32.5 us (31%)
  Pallas kernels  30.2 us (29%)
  starting transfers between devices  26.3 us (25%)
  waiting for transfers between devices  14.1 us (13%)
    all_to_all x1, blocking collectives, shards(): moved = lax.all_to_all(dealt, 'along', 0, 0, tiled=True)  32.5 us
    ppermute x6, starting transfers between devices, neighbours(): return (lax.ppermute(high, axis, up), lax.ppermute(low, axis, down))  16.9 us
    pallas_call x1, Pallas kernels, window(): pl.pallas_call(window_kernel, out_shape=(grid, grid), in_specs=[pl.BlockS...  11.9 us
    all_to_all x1, starting transfers between devices, shards(): got = lax.all_to_all(spread, 'across', 0, 0, tiled=True)  9.37 us
    pallas_call x1, Pallas kernels, points(): pl.pallas_call(points_kernel, out_shape=pltpu.VMEM((ROWS * STEPS, CZ), jn...  9.3 us
    all_to_all x1, waiting for transfers between devices, shards(): got = lax.all_to_all(spread, 'across', 0, 0, tiled=True)  9.18 us
    ppermute x6, waiting for transfers between devices, neighbours(): return (lax.ppermute(high, axis, up), lax.ppermute(low, axis, down))  4.91 us
    pallas_call x1, Pallas kernels, shards(): pl.pallas_call(slab_kernel, out_shape=(slab, slab), in_specs=[smem] + [an...  3.27 us
  transfers between devices with their start and end apart: 7, of which 2 were waited for; matrix products, arithmetic and copies ran while one was open for 0% of the time, Pallas kernels for 9%

profile of v6, /device:TPU:2, one launch (start us, length us, event | category | flops | bytes accessed | tf_op | source)
XLA Modules:
  0.0 104.7 jit_solution(5719768159067205176)
XLA Ops:
  0.6 0.0 copy-start.8
  0.6 0.0 copy-start.2
  0.7 0.0 copy-start.1
  0.7 0.0 copy-start
  0.7 3.3 %shard_map.95 = (f32[96,8,128]{2,1,0:T(8,128)}, f32[96,8,128]{2,1,0:T(8,128)}, bf16[96,4,128]{2,1,0:T(4,128)(2,1)}) custom-call(f32[8]{0:T(128)} %table_ref.6, f32[32,32,128]{2,1,0:T(8,128)} %now_hbm.5, f32[32,32,128]{2,1,0:T(8,128)} %before_hbm.5, s32[32,32,128]{2,1,0:T(8,128)} %layer_hbm.5, bf16[2,2,12288]{2,1,0:T(2,128)(2,1)} %bitcast.4), custom_call_target="tpu_custom_call" | custom-call | tf_op jit(solution)/shard_map/pallas_call | solution.py:347
  3.9 3.5 %collective-permute-start = (f32[96,8,128]{2,1,0:T(8,128)}, f32[96,8,128]{2,1,0:T(8,128)S(1)}, u32[]{:S(2)}, u32[]{:S(2)}) collective-permute-start(f32[96,8,128]{2,1,0:T(8,128)} %get-tuple-element.12), channel_id=1, source_target_pairs={{0,1},{1,2},{2,3},{3,4},{4,5},{5,6},{6,7},{8,9},{9,10},{10,11},{11... | collective-permute-start | bytes 1179656 | tf_op jit(solution)/shard_map/ppermute | solution.py:338
  7.5 1.3 %collective-permute-start.1 = (f32[96,8,128]{2,1,0:T(8,128)}, f32[96,8,128]{2,1,0:T(8,128)S(1)}, u32[]{:S(2)}, u32[]{:S(2)}) collective-permute-start(f32[96,8,128]{2,1,0:T(8,128)} %get-tuple-element.13), channel_id=1, source_target_pairs={{1,0},{2,1},{3,2},{4,3},{5,4},{6,5},{7,6},{9,8},{10,9},{11,10},{12... | collective-permute-start | bytes 1179656 | tf_op jit(solution)/shard_map/ppermute | solution.py:338
  8.8 32.5 %all_to_all.10.moved_ref = bf16[96,4,128]{2,1,0:T(4,128)(2,1)} all-to-all(bf16[96,4,128]{2,1,0:T(4,128)(2,1)} %get-tuple-element.14), channel_id=1, replica_groups=mesh['along'=96,'across'=8] {'along'}, dimensions={0} | all-to-all | bytes 196608 | tf_op jit(solution)/shard_map/all_to_all | solution.py:356
  41.2 0.0 collective-permute-done.ylo_hbm
  41.2 0.0 copy-start.3
  41.2 0.0 collective-permute-done.1.yhi_hbm
  41.2 0.0 copy-start.5
  41.3 1.8 %shard_map.96.own_ref = f32[16,128]{1,0:T(8,128)} custom-call(bf16[96,4,128]{2,1,0:T(4,128)(2,1)} %all_to_all.10.moved_ref, bf16[24,384]{1,0:T(8,128)(2,1)} %constant.6.clone.table_ref, s32[1,128]{1,0:T(1,128)} %bitcast.5, s32[1,128]{1,0:T(1,128)} %cell_ref.1), custom_call_target="tpu_custom_call" | custom-call | tf_op jit(solution)/shard_map/pallas_call | solution.py:359
  43.1 1.9 %collective-permute-start.3 = (f32[16,128]{1,0:T(8,128)}, f32[16,128]{1,0:T(8,128)S(1)}, u32[]{:S(2)}, u32[]{:S(2)}) collective-permute-start(f32[16,128]{1,0:T(8,128)} %shard_map.96.own_ref), channel_id=1, source_target_pairs={{8,0},{16,8},{24,16},{32,24},{40,32},{48,40},{56,48},{64,56},{72,6... | collective-permute-start | bytes 24584 | tf_op jit(solution)/shard_map/ppermute | solution.py:338
  45.0 2.4 %collective-permute-start.2 = (f32[16,128]{1,0:T(8,128)}, f32[16,128]{1,0:T(8,128)S(1)}, u32[]{:S(2)}, u32[]{:S(2)}) collective-permute-start(f32[16,128]{1,0:T(8,128)} %shard_map.96.own_ref), channel_id=1, source_target_pairs={{0,8},{8,16},{16,24},{24,32},{32,40},{40,48},{48,56},{56,64},{64,7... | collective-permute-start | bytes 24584 | tf_op jit(solution)/shard_map/ppermute | solution.py:338
  47.4 0.0 collective-permute-done.3.right_ref
  47.4 4.9 %collective-permute-done.2.left_ref = f32[16,128]{1,0:T(8,128)S(1)} collective-permute-done((f32[16,128]{1,0:T(8,128)}, f32[16,128]{1,0:T(8,128)S(1)}, u32[]{:S(2)}, u32[]{:S(2)}) %collective-permute-start.2) | collective-permute-done | bytes 8224 | tf_op jit(solution)/shard_map/ppermute | solution.py:338
  52.3 0.0 copy-start.7
  52.3 0.7 copy-done.7
  53.0 0.7 shard_map.97
  53.7 0.0 copy-done.3
  53.7 0.0 copy-done.5
  53.7 3.3 %shard_map.99 = (f32[24,48,128]{2,1,0:T(8,128)}, f32[24,48,128]{2,1,0:T(8,128)}) custom-call(f32[8]{0:T(128)} %table_ref.6, f32[32,32,128]{2,1,0:T(8,128)} %now_hbm.5, f32[32,32,128]{2,1,0:T(8,128)} %before_hbm.5, s32[32,32,128]{2,1,0:T(8,128)} %layer_hbm.5, f32[96,8,128]{2,1,0:T(8,128)} %copy-done.3, f32[96,8,128]{2,1,0:T(8,128)} %copy-done.5), custom_call_target="tpu_custom_call" | custom-call | tf_op jit(solution)/shard_map/pallas_call | solution.py:378
  57.0 0.0 copy-start.4
  57.0 0.0 copy-start.6
  57.0 2.1 %collective-permute-start.4 = (f32[24,48,128]{2,1,0:T(8,128)}, f32[24,48,128]{2,1,0:T(8,128)S(1)}, u32[]{:S(2)}, u32[]{:S(2)}) collective-permute-start(f32[24,48,128]{2,1,0:T(8,128)} %get-tuple-element.20), channel_id=1, source_target_pairs={{0,8},{8,16},{16,24},{24,32},{32,40},{40,48},{48,56},{56,64},{64,7... | collective-permute-start | bytes 1769480 | tf_op jit(solution)/shard_map/ppermute | solution.py:338
  59.1 5.8 %collective-permute-start.5 = (f32[24,48,128]{2,1,0:T(8,128)}, f32[24,48,128]{2,1,0:T(8,128)S(1)}, u32[]{:S(2)}, u32[]{:S(2)}) collective-permute-start(f32[24,48,128]{2,1,0:T(8,128)} %get-tuple-element.21), channel_id=1, source_target_pairs={{8,0},{16,8},{24,16},{32,24},{40,32},{48,40},{56,48},{64,56},{72,6... | collective-permute-start | bytes 1769480 | tf_op jit(solution)/shard_map/ppermute | solution.py:338
  64.8 9.4 %all-to-all-start.1 = ((f32[8,32,128]{2,1,0:T(8,128)}), f32[8,32,128]{2,1,0:T(8,128)}, u32[]{:S(2)}, u32[]{:S(2)}) async-start(f32[8,32,128]{2,1,0:T(8,128)} %shard_map.97), calls=%async_computation.1 | async-start | bytes 262144 | tf_op jit(solution)/shard_map/all_to_all | solution.py:376
  74.2 9.2 %all-to-all-done.1 = f32[8,32,128]{2,1,0:T(8,128)} async-done(((f32[8,32,128]{2,1,0:T(8,128)}), f32[8,32,128]{2,1,0:T(8,128)}, u32[]{:S(2)}, u32[]{:S(2)}) %all-to-all-start.1) | async-done | bytes 131104 | tf_op jit(solution)/shard_map/all_to_all | solution.py:376
  83.4 9.3 %shard_map.98.d_ref = f32[18432,128]{1,0:T(8,128)S(1)} custom-call(s32[1]{0:T(128)} %bitcast.place_ref, f32[256,128]{1,0:T(8,128)} %bitcast.3.got_ref), custom_call_target="tpu_custom_call" | custom-call | flops 1000000000 | bytes 67108864 | tf_op jit(solution)/shard_map/pallas_call | solution.py:301
  92.7 0.0 collective-permute-done.4.xlo_hbm
  92.7 0.0 collective-permute-done.5.xhi_hbm
  92.7 0.0 copy-done.8
  92.7 0.0 copy-done.2
  92.7 0.0 copy-done.1
  92.7 0.0 copy-done
  92.7 0.0 copy-done.4
  92.7 0.0 copy-done.6
  92.8 11.9 %shard_map.100 = (f32[32,32,128]{2,1,0:T(8,128)}, f32[32,32,128]{2,1,0:T(8,128)}) custom-call(f32[8]{0:T(128)S(1)} %copy-done.8, f32[18432,128]{1,0:T(8,128)S(1)} %shard_map.98.d_ref, f32[32,32,128]{2,1,0:T(8,128)S(1)} %copy-done, f32[32,32,128]{2,1,0:T(8,128)S(1)} %copy-done.1, s32[32,32,128]{2,1,0:T(8,128)S(1)} %copy-done.2, f32[96,8,128]{2,1,0:T(8,128)S(1)} %copy-done.4, ...), custom_call_target="tpu_custom_call" | custom-call | tf_op jit(solution)/shard_map/pallas_call | solution.py:320
Async XLA Ops:
  0.6 92.1 %copy-start.8 = (f32[8]{0:T(128)S(1)}, f32[8]{0:T(128)}, u32[]{:S(2)}) copy-start(f32[8]{0:T(128)} %table_ref.6) | copy-start | bytes 100
  0.6 92.1 %copy-start.2 = (s32[32,32,128]{2,1,0:T(8,128)S(1)}, s32[32,32,128]{2,1,0:T(8,128)}, u32[]{:S(2)}) copy-start(s32[32,32,128]{2,1,0:T(8,128)} %layer_hbm.5) | copy-start | bytes 1572868
  0.7 92.1 %copy-start.1 = (f32[32,32,128]{2,1,0:T(8,128)S(1)}, f32[32,32,128]{2,1,0:T(8,128)}, u32[]{:S(2)}) copy-start(f32[32,32,128]{2,1,0:T(8,128)} %before_hbm.5) | copy-start | bytes 1572868
  0.7 92.1 %copy-start = (f32[32,32,128]{2,1,0:T(8,128)S(1)}, f32[32,32,128]{2,1,0:T(8,128)}, u32[]{:S(2)}) copy-start(f32[32,32,128]{2,1,0:T(8,128)} %now_hbm.5) | copy-start | bytes 1572868
  3.9 37.3 %collective-permute-start = (f32[96,8,128]{2,1,0:T(8,128)}, f32[96,8,128]{2,1,0:T(8,128)S(1)}, u32[]{:S(2)}, u32[]{:S(2)}) collective-permute-start(f32[96,8,128]{2,1,0:T(8,128)} %get-tuple-element.12), channel_id=1, source_target_pairs={{0,1},{1,2},{2,3},{3,4},{4,5},{5,6},{6,7},{8,9},{9,10},{10,11},{11... | collective-permute-start | bytes 1179656 | tf_op jit(solution)/shard_map/ppermute | solution.py:338
  7.5 33.8 %collective-permute-start.1 = (f32[96,8,128]{2,1,0:T(8,128)}, f32[96,8,128]{2,1,0:T(8,128)S(1)}, u32[]{:S(2)}, u32[]{:S(2)}) collective-permute-start(f32[96,8,128]{2,1,0:T(8,128)} %get-tuple-element.13), channel_id=1, source_target_pairs={{1,0},{2,1},{3,2},{4,3},{5,4},{6,5},{7,6},{9,8},{10,9},{11,10},{12... | collective-permute-start | bytes 1179656 | tf_op jit(solution)/shard_map/ppermute | solution.py:338
  41.2 12.4 %copy-start.3 = (f32[96,8,128]{2,1,0:T(8,128)}, f32[96,8,128]{2,1,0:T(8,128)S(1)}, u32[]{:S(2)}) copy-start(f32[96,8,128]{2,1,0:T(8,128)S(1)} %collective-permute-done.ylo_hbm) | copy-start | bytes 1179652
  41.2 12.4 %copy-start.5 = (f32[96,8,128]{2,1,0:T(8,128)}, f32[96,8,128]{2,1,0:T(8,128)S(1)}, u32[]{:S(2)}) copy-start(f32[96,8,128]{2,1,0:T(8,128)S(1)} %collective-permute-done.1.yhi_hbm) | copy-start | bytes 1179652
  43.1 4.3 %collective-permute-start.3 = (f32[16,128]{1,0:T(8,128)}, f32[16,128]{1,0:T(8,128)S(1)}, u32[]{:S(2)}, u32[]{:S(2)}) collective-permute-start(f32[16,128]{1,0:T(8,128)} %shard_map.96.own_ref), channel_id=1, source_target_pairs={{8,0},{16,8},{24,16},{32,24},{40,32},{48,40},{56,48},{64,56},{72,6... | collective-permute-start | bytes 24584 | tf_op jit(solution)/shard_map/ppermute | solution.py:338
  45.0 7.3 %collective-permute-start.2 = (f32[16,128]{1,0:T(8,128)}, f32[16,128]{1,0:T(8,128)S(1)}, u32[]{:S(2)}, u32[]{:S(2)}) collective-permute-start(f32[16,128]{1,0:T(8,128)} %shard_map.96.own_ref), channel_id=1, source_target_pairs={{0,8},{8,16},{16,24},{24,32},{32,40},{40,48},{48,56},{56,64},{64,7... | collective-permute-start | bytes 24584 | tf_op jit(solution)/shard_map/ppermute | solution.py:338
  52.3 0.7 copy-start.7
  57.0 35.8 %copy-start.4 = (f32[96,8,128]{2,1,0:T(8,128)S(1)}, f32[96,8,128]{2,1,0:T(8,128)}, u32[]{:S(2)}) copy-start(f32[96,8,128]{2,1,0:T(8,128)} %copy-done.3) | copy-start | bytes 1179652
  57.0 35.8 %copy-start.6 = (f32[96,8,128]{2,1,0:T(8,128)S(1)}, f32[96,8,128]{2,1,0:T(8,128)}, u32[]{:S(2)}) copy-start(f32[96,8,128]{2,1,0:T(8,128)} %copy-done.5) | copy-start | bytes 1179652
  57.0 35.7 %collective-permute-start.4 = (f32[24,48,128]{2,1,0:T(8,128)}, f32[24,48,128]{2,1,0:T(8,128)S(1)}, u32[]{:S(2)}, u32[]{:S(2)}) collective-permute-start(f32[24,48,128]{2,1,0:T(8,128)} %get-tuple-element.20), channel_id=1, source_target_pairs={{0,8},{8,16},{16,24},{24,32},{32,40},{40,48},{48,56},{56,64},{64,7... | collective-permute-start | bytes 1769480 | tf_op jit(solution)/shard_map/ppermute | solution.py:338
  59.1 33.6 %collective-permute-start.5 = (f32[24,48,128]{2,1,0:T(8,128)}, f32[24,48,128]{2,1,0:T(8,128)S(1)}, u32[]{:S(2)}, u32[]{:S(2)}) collective-permute-start(f32[24,48,128]{2,1,0:T(8,128)} %get-tuple-element.21), channel_id=1, source_target_pairs={{8,0},{16,8},{24,16},{32,24},{40,32},{48,40},{56,48},{64,56},{72,6... | collective-permute-start | bytes 1769480 | tf_op jit(solution)/shard_map/ppermute | solution.py:338
  64.8 18.6 %all-to-all-start.1 = ((f32[8,32,128]{2,1,0:T(8,128)}), f32[8,32,128]{2,1,0:T(8,128)}, u32[]{:S(2)}, u32[]{:S(2)}) async-start(f32[8,32,128]{2,1,0:T(8,128)} %shard_map.97), calls=%async_computation.1 | async-start | bytes 262144 | tf_op jit(solution)/shard_map/all_to_all | solution.py:376

commit v7 on v6

--- a/solution.py
+++ b/solution.py
@@ -18,7 +18,7 @@
 CELLS = CX * CY * CZ
 NPT = 128
 ROW_BITS, Z_BITS, P_BITS = 12, 7, 12
-BODY = (12, 11, 11, 10, 10, 9, 9, 8)
+BODY = (24, 22, 21, 20, 19, 18, 17, 16)
 GROUP = 32
 MIB = 1024 * 1024
 PARTS = 4 * H
@@ -267,7 +267,7 @@
         u_ref, w_ref = (a_ref, b_ref) if step % 2 == 0 else (b_ref, a_ref)
 
         planes = BODY[step]
-        start = EX // 2 - 2 * planes
+        start = EX // 2 - planes
         rows = range(0, EY // 8) if step < STEPS - 1 else range(1, 1 + CY // 8)
 
         def advance(i, _, u_ref=u_ref, w_ref=w_ref, step=step, planes=planes, start=start, rows=rows):
@@ -287,7 +287,7 @@
                     w_ref[x + 1, pl.ds(y, 8), :] = (own + drive) + ((in_x + in_y) + in_z)
             return 0
 
-        lax.fori_loop(0, 4, advance, 0)
+        lax.fori_loop(0, 2, advance, 0)
 
         if step == STEPS - 2:
             prior_copy.start()
@@ -309,7 +309,7 @@
             pltpu.SMEM((3 * tiles * NPT + 2 * GROUP,), jnp.int32),
             pltpu.SemaphoreType.DMA,
         ],
-        cost_estimate=pl.CostEstimate(flops=10**9, transcendentals=0, bytes_accessed=64 * MIB),
+        cost_estimate=pl.CostEstimate(flops=10**12, transcendentals=0, bytes_accessed=1024 * MIB),
         compiler_params=pltpu.CompilerParams(vmem_limit_bytes=4 * MIB),
     )(place, got.reshape(tiles * PARTS, NPT))
 
@@ -343,10 +343,10 @@
     local_freqs = fk_panel.shape[1]
     arrays = (field_now, field_before, layer)
     smem = pl.BlockSpec(memory_space=pltpu.SMEM)
-    slab = jax.ShapeDtypeStruct((3 * CX, H, CZ), jnp.float32)
+    slab = pltpu.VMEM((3 * CX, H, CZ), jnp.float32)
     low, high, dealt = pl.pallas_call(
         prepare_kernel,
-        out_shape=(slab, slab, jax.ShapeDtypeStruct((sources, 2 * local_freqs, NPT), jnp.bfloat16)),
+        out_shape=(slab, slab, pltpu.VMEM((sources, 2 * local_freqs, NPT), jnp.bfloat16)),
         in_specs=[smem] + [any_spec()] * 3 + [vmem_spec()],
         out_specs=(vmem_spec(),) * 3,
         scratch_shapes=[pltpu.VMEM((2, CX, H, CZ), jnp.int32), pltpu.SemaphoreType.DMA((2, 3))],
@@ -358,7 +358,7 @@
 
     samples = pl.pallas_call(
         transform_kernel,
-        out_shape=jax.ShapeDtypeStruct((2 * STEPS, NPT), jnp.float32),
+        out_shape=pltpu.VMEM((2 * STEPS, NPT), jnp.float32),
         in_specs=[vmem_spec()] * 4,
         out_specs=vmem_spec(),
         scratch_shapes=[pltpu.VMEM((2 * local_freqs * sources, NPT), jnp.float32)],
@@ -382,7 +382,7 @@
         out_specs=(vmem_spec(),) * 2,
         scratch_shapes=[pltpu.VMEM((2, H, CY, CZ), jnp.int32), pltpu.SemaphoreType.DMA((3, 2, 3))],
         compiler_params=pltpu.CompilerParams(vmem_limit_bytes=58 * MIB),
-    )(modulus_table, *arrays, *lax.optimization_barrier((ylo, yhi, spread))[:2])
+    )(modulus_table, *arrays, *lax.optimization_barrier((ylo, yhi, samples))[:2])
     xlo, xhi = neighbours(low, high, "along")
     place = lax.axis_index("across").astype(jnp.int32).reshape(1)
     drive = points(place, got)

time: 105 us -> 91.8 us (0.87)
  the two profiles are of different devices: /device:TPU:2 before, /device:TPU:58 now
where the time goes in v7:
time: 91.8 us; the launch traced here: 91.3 us
  blocking collectives  32.3 us (35%)
  Pallas kernels  27.5 us (30%)
  starting transfers between devices  25.9 us (28%)
  waiting for transfers between devices  4.7 us (5%)
    all_to_all x1, blocking collectives, shards(): moved = lax.all_to_all(dealt, 'along', 0, 0, tiled=True)  32.3 us
    ppermute x6, starting transfers between devices, neighbours(): return (lax.ppermute(high, axis, up), lax.ppermute(low, axis, down))  17.9 us
    pallas_call x1, Pallas kernels, window(): pl.pallas_call(window_kernel, out_shape=(grid, grid), in_specs=[pl.BlockS...  11.6 us
    pallas_call x1, Pallas kernels, points(): pl.pallas_call(points_kernel, out_shape=pltpu.VMEM((ROWS * STEPS, CZ), jn...  8.4 us
    all_to_all x1, starting transfers between devices, shards(): got = lax.all_to_all(spread, 'across', 0, 0, tiled=True)  8.07 us
    ppermute x6, waiting for transfers between devices, neighbours(): return (lax.ppermute(high, axis, up), lax.ppermute(low, axis, down))  4.7 us
    pallas_call x1, Pallas kernels, shards(): pl.pallas_call(slab_kernel, out_shape=(slab, slab), in_specs=[smem] + [an...  3.26 us
    pallas_call x1, Pallas kernels, shards(): pl.pallas_call(prepare_kernel, out_shape=(slab, slab, pltpu.VMEM((sources...  2.3 us
  transfers between devices with their start and end apart: 7, of which 1 were waited for; matrix products, arithmetic and copies ran while one was open for 0% of the time, Pallas kernels for 13%

profile of v7, /device:TPU:58, one launch (start us, length us, event | category | flops | bytes accessed | tf_op | source)
XLA Modules:
  0.0 91.3 jit_solution(15578842781430842762)
XLA Ops:
  0.6 2.3 %shard_map.95 = (f32[96,8,128]{2,1,0:T(8,128)S(1)}, f32[96,8,128]{2,1,0:T(8,128)S(1)}, bf16[96,4,128]{2,1,0:T(4,128)(2,1)S(1)}) custom-call(f32[8]{0:T(128)} %table_ref.6, f32[32,32,128]{2,1,0:T(8,128)} %now_hbm.5, f32[32,32,128]{2,1,0:T(8,128)} %before_hbm.5, s32[32,32,128]{2,1,0:T(8,128)} %layer_hbm.5, bf16[2,2,12288]{2,1,0:T(2,128)(2,1)} %bitcast.5), custom_call_target="tpu_custom_call" | custom-call | tf_op jit(solution)/shard_map/pallas_call | solution.py:347
  2.9 1.3 %collective-permute-start = (f32[96,8,128]{2,1,0:T(8,128)S(1)}, f32[96,8,128]{2,1,0:T(8,128)S(1)}, u32[]{:S(2)}, u32[]{:S(2)}) collective-permute-start(f32[96,8,128]{2,1,0:T(8,128)S(1)} %get-tuple-element.12), channel_id=1, source_target_pairs={{0,1},{1,2},{2,3},{3,4},{4,5},{5,6},{6,7},{8,9},{9,10},{10,11},{11... | collective-permute-start | bytes 1179656 | tf_op jit(solution)/shard_map/ppermute | solution.py:338
  4.2 4.6 %collective-permute-start.1 = (f32[96,8,128]{2,1,0:T(8,128)S(1)}, f32[96,8,128]{2,1,0:T(8,128)S(1)}, u32[]{:S(2)}, u32[]{:S(2)}) collective-permute-start(f32[96,8,128]{2,1,0:T(8,128)S(1)} %get-tuple-element.13), channel_id=1, source_target_pairs={{1,0},{2,1},{3,2},{4,3},{5,4},{6,5},{7,6},{9,8},{10,9},{11,10},{12... | collective-permute-start | bytes 1179656 | tf_op jit(solution)/shard_map/ppermute | solution.py:338
  8.8 32.3 %all_to_all.10.moved_ref = bf16[96,4,128]{2,1,0:T(4,128)(2,1)} all-to-all(bf16[96,4,128]{2,1,0:T(4,128)(2,1)S(1)} %get-tuple-element.14), channel_id=1, replica_groups=mesh['along'=96,'across'=8] {'along'}, dimensions={0} | all-to-all | bytes 196608 | tf_op jit(solution)/shard_map/all_to_all | solution.py:356
  41.1 0.0 collective-permute-done.ylo_hbm
  41.1 0.0 copy-start.3
  41.1 0.0 collective-permute-done.1.yhi_hbm
  41.1 0.0 copy-start.5
  41.1 1.2 %shard_map.96.own_ref = f32[16,128]{1,0:T(8,128)S(1)} custom-call(bf16[96,4,128]{2,1,0:T(4,128)(2,1)} %all_to_all.10.moved_ref, bf16[24,384]{1,0:T(8,128)(2,1)} %constant.6.clone.table_ref, s32[1,128]{1,0:T(1,128)} %bitcast.6, s32[1,128]{1,0:T(1,128)} %cell_ref.1), custom_call_target="tpu_custom_call" | custom-call | tf_op jit(solution)/shard_map/pallas_call | solution.py:359
  42.3 1.9 %collective-permute-start.3 = (f32[16,128]{1,0:T(8,128)S(1)}, f32[16,128]{1,0:T(8,128)S(1)}, u32[]{:S(2)}, u32[]{:S(2)}) collective-permute-start(f32[16,128]{1,0:T(8,128)S(1)} %shard_map.96.own_ref), channel_id=1, source_target_pairs={{8,0},{16,8},{24,16},{32,24},{40,32},{48,40},{56,48},{64,56},{72,6... | collective-permute-start | bytes 24584 | tf_op jit(solution)/shard_map/ppermute | solution.py:338
  44.3 2.4 %collective-permute-start.2 = (f32[16,128]{1,0:T(8,128)S(1)}, f32[16,128]{1,0:T(8,128)S(1)}, u32[]{:S(2)}, u32[]{:S(2)}) collective-permute-start(f32[16,128]{1,0:T(8,128)S(1)} %shard_map.96.own_ref), channel_id=1, source_target_pairs={{0,8},{8,16},{16,24},{24,32},{32,40},{40,48},{48,56},{56,64},{64,7... | collective-permute-start | bytes 24584 | tf_op jit(solution)/shard_map/ppermute | solution.py:338
  46.7 0.0 collective-permute-done.3.right_ref
  46.7 4.7 %collective-permute-done.2.left_ref = f32[16,128]{1,0:T(8,128)S(1)} collective-permute-done((f32[16,128]{1,0:T(8,128)S(1)}, f32[16,128]{1,0:T(8,128)S(1)}, u32[]{:S(2)}, u32[]{:S(2)}) %collective-permute-start.2) | collective-permute-done | bytes 8224 | tf_op jit(solution)/shard_map/ppermute | solution.py:338
  51.4 0.7 shard_map.97
  52.0 8.1 %all-to-all-start.1 = ((f32[8,32,128]{2,1,0:T(8,128)}), f32[8,32,128]{2,1,0:T(8,128)S(1)}, u32[]{:S(2)}, u32[]{:S(2)}) async-start(f32[8,32,128]{2,1,0:T(8,128)} %shard_map.97), calls=%async_computation.1 | async-start | bytes 262144 | tf_op jit(solution)/shard_map/all_to_all | solution.py:376
  60.1 0.0 copy-done.3
  60.1 0.0 copy-done.5
  60.1 3.3 %shard_map.99 = (f32[24,48,128]{2,1,0:T(8,128)}, f32[24,48,128]{2,1,0:T(8,128)}) custom-call(f32[8]{0:T(128)} %table_ref.6, f32[32,32,128]{2,1,0:T(8,128)} %now_hbm.5, f32[32,32,128]{2,1,0:T(8,128)} %before_hbm.5, s32[32,32,128]{2,1,0:T(8,128)} %layer_hbm.5, f32[96,8,128]{2,1,0:T(8,128)} %copy-done.3, f32[96,8,128]{2,1,0:T(8,128)} %copy-done.5), custom_call_target="tpu_custom_call" | custom-call | tf_op jit(solution)/shard_map/pallas_call | solution.py:378
  63.4 1.9 %collective-permute-start.4 = (f32[24,48,128]{2,1,0:T(8,128)}, f32[24,48,128]{2,1,0:T(8,128)}, u32[]{:S(2)}, u32[]{:S(2)}) collective-permute-start(f32[24,48,128]{2,1,0:T(8,128)} %get-tuple-element.20), channel_id=1, source_target_pairs={{0,8},{8,16},{16,24},{24,32},{32,40},{40,48},{48,56},{56,64},{64,7... | collective-permute-start | bytes 1769480 | tf_op jit(solution)/shard_map/ppermute | solution.py:338
  65.3 5.8 %collective-permute-start.5 = (f32[24,48,128]{2,1,0:T(8,128)}, f32[24,48,128]{2,1,0:T(8,128)}, u32[]{:S(2)}, u32[]{:S(2)}) collective-permute-start(f32[24,48,128]{2,1,0:T(8,128)} %get-tuple-element.21), channel_id=1, source_target_pairs={{8,0},{16,8},{24,16},{32,24},{40,32},{48,40},{56,48},{64,56},{72,6... | collective-permute-start | bytes 1769480 | tf_op jit(solution)/shard_map/ppermute | solution.py:338
  71.1 0.0 all-to-all-done.1
  71.1 0.0 copy-start
  71.1 0.0 copy-start.1
  71.1 0.0 copy-start.2
  71.1 0.0 copy-start.4
  71.1 0.0 copy-start.6
  71.1 0.0 copy-start.7
  71.1 8.4 %shard_map.98.d_ref = f32[18432,128]{1,0:T(8,128)S(1)} custom-call(s32[1]{0:T(128)} %bitcast.place_ref, f32[256,128]{1,0:T(8,128)S(1)} %bitcast.4), custom_call_target="tpu_custom_call" | custom-call | flops 999999995904 | bytes 1073741824 | tf_op jit(solution)/shard_map/pallas_call | solution.py:301
  79.6 0.0 collective-permute-done.4.xlo_hbm
  79.6 0.0 collective-permute-done.5.xhi_hbm
  79.6 0.0 copy-done
  79.6 0.0 copy-done.1
  79.6 0.0 copy-done.2
  79.6 0.0 copy-done.4
  79.6 0.0 copy-done.6
  79.6 0.0 copy-done.7
  79.6 11.6 %shard_map.100 = (f32[32,32,128]{2,1,0:T(8,128)}, f32[32,32,128]{2,1,0:T(8,128)}) custom-call(f32[8]{0:T(128)S(1)} %copy-done.7, f32[18432,128]{1,0:T(8,128)S(1)} %shard_map.98.d_ref, f32[32,32,128]{2,1,0:T(8,128)S(1)} %copy-done, f32[32,32,128]{2,1,0:T(8,128)S(1)} %copy-done.1, s32[32,32,128]{2,1,0:T(8,128)S(1)} %copy-done.2, f32[96,8,128]{2,1,0:T(8,128)S(1)} %copy-done.4, ...), custom_call_target="tpu_custom_call" | custom-call | tf_op jit(solution)/shard_map/pallas_call | solution.py:320
Async XLA Ops:
  2.9 38.2 %collective-permute-start = (f32[96,8,128]{2,1,0:T(8,128)S(1)}, f32[96,8,128]{2,1,0:T(8,128)S(1)}, u32[]{:S(2)}, u32[]{:S(2)}) collective-permute-start(f32[96,8,128]{2,1,0:T(8,128)S(1)} %get-tuple-element.12), channel_id=1, source_target_pairs={{0,1},{1,2},{2,3},{3,4},{4,5},{5,6},{6,7},{8,9},{9,10},{10,11},{11... | collective-permute-start | bytes 1179656 | tf_op jit(solution)/shard_map/ppermute | solution.py:338
  4.2 36.9 %collective-permute-start.1 = (f32[96,8,128]{2,1,0:T(8,128)S(1)}, f32[96,8,128]{2,1,0:T(8,128)S(1)}, u32[]{:S(2)}, u32[]{:S(2)}) collective-permute-start(f32[96,8,128]{2,1,0:T(8,128)S(1)} %get-tuple-element.13), channel_id=1, source_target_pairs={{1,0},{2,1},{3,2},{4,3},{5,4},{6,5},{7,6},{9,8},{10,9},{11,10},{12... | collective-permute-start | bytes 1179656 | tf_op jit(solution)/shard_map/ppermute | solution.py:338
  41.1 19.0 %copy-start.3 = (f32[96,8,128]{2,1,0:T(8,128)}, f32[96,8,128]{2,1,0:T(8,128)S(1)}, u32[]{:S(2)}) copy-start(f32[96,8,128]{2,1,0:T(8,128)S(1)} %collective-permute-done.ylo_hbm) | copy-start | bytes 1179652
  41.1 19.0 %copy-start.5 = (f32[96,8,128]{2,1,0:T(8,128)}, f32[96,8,128]{2,1,0:T(8,128)S(1)}, u32[]{:S(2)}) copy-start(f32[96,8,128]{2,1,0:T(8,128)S(1)} %collective-permute-done.1.yhi_hbm) | copy-start | bytes 1179652
  42.3 4.3 %collective-permute-start.3 = (f32[16,128]{1,0:T(8,128)S(1)}, f32[16,128]{1,0:T(8,128)S(1)}, u32[]{:S(2)}, u32[]{:S(2)}) collective-permute-start(f32[16,128]{1,0:T(8,128)S(1)} %shard_map.96.own_ref), channel_id=1, source_target_pairs={{8,0},{16,8},{24,16},{32,24},{40,32},{48,40},{56,48},{64,56},{72,6... | collective-permute-start | bytes 24584 | tf_op jit(solution)/shard_map/ppermute | solution.py:338
  44.3 7.1 %collective-permute-start.2 = (f32[16,128]{1,0:T(8,128)S(1)}, f32[16,128]{1,0:T(8,128)S(1)}, u32[]{:S(2)}, u32[]{:S(2)}) collective-permute-start(f32[16,128]{1,0:T(8,128)S(1)} %shard_map.96.own_ref), channel_id=1, source_target_pairs={{0,8},{8,16},{16,24},{24,32},{32,40},{40,48},{48,56},{56,64},{64,7... | collective-permute-start | bytes 24584 | tf_op jit(solution)/shard_map/ppermute | solution.py:338
  52.0 19.0 %all-to-all-start.1 = ((f32[8,32,128]{2,1,0:T(8,128)}), f32[8,32,128]{2,1,0:T(8,128)S(1)}, u32[]{:S(2)}, u32[]{:S(2)}) async-start(f32[8,32,128]{2,1,0:T(8,128)} %shard_map.97), calls=%async_computation.1 | async-start | bytes 262144 | tf_op jit(solution)/shard_map/all_to_all | solution.py:376
  63.4 16.2 %collective-permute-start.4 = (f32[24,48,128]{2,1,0:T(8,128)}, f32[24,48,128]{2,1,0:T(8,128)}, u32[]{:S(2)}, u32[]{:S(2)}) collective-permute-start(f32[24,48,128]{2,1,0:T(8,128)} %get-tuple-element.20), channel_id=1, source_target_pairs={{0,8},{8,16},{16,24},{24,32},{32,40},{40,48},{48,56},{56,64},{64,7... | collective-permute-start | bytes 1769480 | tf_op jit(solution)/shard_map/ppermute | solution.py:338
  65.3 14.3 %collective-permute-start.5 = (f32[24,48,128]{2,1,0:T(8,128)}, f32[24,48,128]{2,1,0:T(8,128)}, u32[]{:S(2)}, u32[]{:S(2)}) collective-permute-start(f32[24,48,128]{2,1,0:T(8,128)} %get-tuple-element.21), channel_id=1, source_target_pairs={{8,0},{16,8},{24,16},{32,24},{40,32},{48,40},{56,48},{64,56},{72,6... | collective-permute-start | bytes 1769480 | tf_op jit(solution)/shard_map/ppermute | solution.py:338
  71.1 8.5 %copy-start = (f32[32,32,128]{2,1,0:T(8,128)S(1)}, f32[32,32,128]{2,1,0:T(8,128)}, u32[]{:S(2)}) copy-start(f32[32,32,128]{2,1,0:T(8,128)} %now_hbm.5) | copy-start | bytes 1572868
  71.1 8.5 %copy-start.1 = (f32[32,32,128]{2,1,0:T(8,128)S(1)}, f32[32,32,128]{2,1,0:T(8,128)}, u32[]{:S(2)}) copy-start(f32[32,32,128]{2,1,0:T(8,128)} %before_hbm.5) | copy-start | bytes 1572868
  71.1 8.5 %copy-start.2 = (s32[32,32,128]{2,1,0:T(8,128)S(1)}, s32[32,32,128]{2,1,0:T(8,128)}, u32[]{:S(2)}) copy-start(s32[32,32,128]{2,1,0:T(8,128)} %layer_hbm.5) | copy-start | bytes 1572868
  71.1 8.5 %copy-start.4 = (f32[96,8,128]{2,1,0:T(8,128)S(1)}, f32[96,8,128]{2,1,0:T(8,128)}, u32[]{:S(2)}) copy-start(f32[96,8,128]{2,1,0:T(8,128)} %copy-done.3) | copy-start | bytes 1179652
  71.1 8.5 %copy-start.6 = (f32[96,8,128]{2,1,0:T(8,128)S(1)}, f32[96,8,128]{2,1,0:T(8,128)}, u32[]{:S(2)}) copy-start(f32[96,8,128]{2,1,0:T(8,128)} %copy-done.5) | copy-start | bytes 1179652
  71.1 8.5 %copy-start.7 = (f32[8]{0:T(128)S(1)}, f32[8]{0:T(128)}, u32[]{:S(2)}) copy-start(f32[8]{0:T(128)} %table_ref.6) | copy-start | bytes 100

commit v8 on v7

--- a/solution.py
+++ b/solution.py
@@ -309,7 +309,7 @@
             pltpu.SMEM((3 * tiles * NPT + 2 * GROUP,), jnp.int32),
             pltpu.SemaphoreType.DMA,
         ],
-        cost_estimate=pl.CostEstimate(flops=10**12, transcendentals=0, bytes_accessed=1024 * MIB),
+        cost_estimate=pl.CostEstimate(flops=10**6, transcendentals=0, bytes_accessed=10 * MIB),
         compiler_params=pltpu.CompilerParams(vmem_limit_bytes=4 * MIB),
     )(place, got.reshape(tiles * PARTS, NPT))
 
@@ -365,6 +365,17 @@
         compiler_params=pltpu.CompilerParams(vmem_limit_bytes=58 * MIB),
     )(moved, jnp.asarray(split_table(sources, local_freqs)), owner.reshape(1, NPT), local_cell)
     left, right = neighbours(samples, samples, "along")
+    slab = pltpu.VMEM((3 * H, EY, CZ), jnp.float32)
+    low, high = pl.pallas_call(
+        slab_kernel,
+        out_shape=(slab, slab),
+        in_specs=[smem] + [any_spec()] * 5,
+        out_specs=(vmem_spec(),) * 2,
+        scratch_shapes=[pltpu.VMEM((2, H, CY, CZ), jnp.int32), pltpu.SemaphoreType.DMA((3, 2, 3))],
+        compiler_params=pltpu.CompilerParams(vmem_limit_bytes=58 * MIB),
+    )(modulus_table, *arrays, *lax.optimization_barrier((ylo, yhi, samples))[:2])
+    low, high, left, right = lax.optimization_barrier((low, high, left, right))
+    xlo, xhi = neighbours(low, high, "along")
     spread = pl.pallas_call(
         spread_kernel,
         out_shape=pltpu.HBM((tiles, PARTS, NPT), jnp.float32),
@@ -374,16 +385,6 @@
         compiler_params=pltpu.CompilerParams(vmem_limit_bytes=4 * MIB),
     )(samples, left, right)
     got = lax.all_to_all(spread, "across", 0, 0, tiled=True)
-    slab = jax.ShapeDtypeStruct((3 * H, EY, CZ), jnp.float32)
-    low, high = pl.pallas_call(
-        slab_kernel,
-        out_shape=(slab, slab),
-        in_specs=[smem] + [any_spec()] * 5,
-        out_specs=(vmem_spec(),) * 2,
-        scratch_shapes=[pltpu.VMEM((2, H, CY, CZ), jnp.int32), pltpu.SemaphoreType.DMA((3, 2, 3))],
-        compiler_params=pltpu.CompilerParams(vmem_limit_bytes=58 * MIB),
-    )(modulus_table, *arrays, *lax.optimization_barrier((ylo, yhi, samples))[:2])
-    xlo, xhi = neighbours(low, high, "along")
     place = lax.axis_index("across").astype(jnp.int32).reshape(1)
     drive = points(place, got)
     return window(modulus_table, drive, (*arrays, ylo, yhi, xlo, xhi))

time: 91.8 us -> 94.9 us (1.034)
  the two profiles are of different devices: /device:TPU:58 before, /device:TPU:2 now
where the time goes in v8:
time: 94.9 us; the launch traced here: 94.3 us
  blocking collectives  32.3 us (34%)
  starting transfers between devices  26.1 us (28%)
  Pallas kernels  24.4 us (26%)
  waiting for transfers between devices  10.6 us (11%)
    all_to_all x1, blocking collectives, shards(): moved = lax.all_to_all(dealt, 'along', 0, 0, tiled=True)  32.3 us
    ppermute x6, starting transfers between devices, neighbours(): return (lax.ppermute(high, axis, up), lax.ppermute(low, axis, down))  16.8 us
    pallas_call x1, Pallas kernels, window(): pl.pallas_call(window_kernel, out_shape=(grid, grid), in_specs=[pl.BlockS...  10.7 us
    all_to_all x1, starting transfers between devices, shards(): got = lax.all_to_all(spread, 'across', 0, 0, tiled=True)  9.37 us
    all_to_all x1, waiting for transfers between devices, shards(): got = lax.all_to_all(spread, 'across', 0, 0, tiled=True)  9.18 us
    pallas_call x1, Pallas kernels, points(): pl.pallas_call(points_kernel, out_shape=pltpu.VMEM((ROWS * STEPS, CZ), jn...  6.19 us
    pallas_call x1, Pallas kernels, shards(): pl.pallas_call(slab_kernel, out_shape=(slab, slab), in_specs=[smem] + [an...  3.26 us
    pallas_call x1, Pallas kernels, shards(): pl.pallas_call(prepare_kernel, out_shape=(slab, slab, pltpu.VMEM((sources...  2.41 us
  transfers between devices with their start and end apart: 7, of which 2 were waited for; matrix products, arithmetic and copies ran while one was open for 0% of the time, Pallas kernels for 11%

profile of v8, /device:TPU:2, one launch (start us, length us, event | category | flops | bytes accessed | tf_op | source)
XLA Modules:
  0.0 94.3 jit_solution(13377126352849843523)
XLA Ops:
  0.6 0.0 copy-start.7
  0.6 0.0 copy-start.2
  0.7 0.0 copy-start.1
  0.7 0.0 copy-start
  0.7 2.4 %shard_map.95 = (f32[96,8,128]{2,1,0:T(8,128)S(1)}, f32[96,8,128]{2,1,0:T(8,128)S(1)}, bf16[96,4,128]{2,1,0:T(4,128)(2,1)S(1)}) custom-call(f32[8]{0:T(128)} %table_ref.6, f32[32,32,128]{2,1,0:T(8,128)} %now_hbm.5, f32[32,32,128]{2,1,0:T(8,128)} %before_hbm.5, s32[32,32,128]{2,1,0:T(8,128)} %layer_hbm.5, bf16[2,2,12288]{2,1,0:T(2,128)(2,1)} %bitcast.4), custom_call_target="tpu_custom_call" | custom-call | tf_op jit(solution)/shard_map/pallas_call | solution.py:347
  3.1 3.5 %collective-permute-start = (f32[96,8,128]{2,1,0:T(8,128)S(1)}, f32[96,8,128]{2,1,0:T(8,128)S(1)}, u32[]{:S(2)}, u32[]{:S(2)}) collective-permute-start(f32[96,8,128]{2,1,0:T(8,128)S(1)} %get-tuple-element.16), channel_id=1, source_target_pairs={{0,1},{1,2},{2,3},{3,4},{4,5},{5,6},{6,7},{8,9},{9,10},{10,11},{11... | collective-permute-start | bytes 1179656 | tf_op jit(solution)/shard_map/ppermute | solution.py:338
  6.6 1.3 %collective-permute-start.1 = (f32[96,8,128]{2,1,0:T(8,128)S(1)}, f32[96,8,128]{2,1,0:T(8,128)S(1)}, u32[]{:S(2)}, u32[]{:S(2)}) collective-permute-start(f32[96,8,128]{2,1,0:T(8,128)S(1)} %get-tuple-element.17), channel_id=1, source_target_pairs={{1,0},{2,1},{3,2},{4,3},{5,4},{6,5},{7,6},{9,8},{10,9},{11,10},{12... | collective-permute-start | bytes 1179656 | tf_op jit(solution)/shard_map/ppermute | solution.py:338
  7.9 32.3 %all_to_all.10.moved_ref = bf16[96,4,128]{2,1,0:T(4,128)(2,1)} all-to-all(bf16[96,4,128]{2,1,0:T(4,128)(2,1)S(1)} %get-tuple-element.18), channel_id=1, replica_groups=mesh['along'=96,'across'=8] {'along'}, dimensions={0} | all-to-all | bytes 196608 | tf_op jit(solution)/shard_map/all_to_all | solution.py:356
  40.2 0.0 collective-permute-done.ylo_hbm
  40.2 0.0 copy-start.3
  40.2 0.0 collective-permute-done.1.yhi_hbm
  40.2 0.0 copy-start.5
  40.2 1.2 %shard_map.96.own_ref = f32[16,128]{1,0:T(8,128)S(1)} custom-call(bf16[96,4,128]{2,1,0:T(4,128)(2,1)} %all_to_all.10.moved_ref, bf16[24,384]{1,0:T(8,128)(2,1)} %constant.6.clone.table_ref, s32[1,128]{1,0:T(1,128)} %bitcast.5, s32[1,128]{1,0:T(1,128)} %cell_ref.1), custom_call_target="tpu_custom_call" | custom-call | tf_op jit(solution)/shard_map/pallas_call | solution.py:359
  41.4 1.9 %collective-permute-start.3 = (f32[16,128]{1,0:T(8,128)S(1)}, f32[16,128]{1,0:T(8,128)S(1)}, u32[]{:S(2)}, u32[]{:S(2)}) collective-permute-start(f32[16,128]{1,0:T(8,128)S(1)} %shard_map.96.own_ref), channel_id=1, source_target_pairs={{8,0},{16,8},{24,16},{32,24},{40,32},{48,40},{56,48},{64,56},{72,6... | collective-permute-start | bytes 24584 | tf_op jit(solution)/shard_map/ppermute | solution.py:338
  43.4 2.4 %collective-permute-start.2 = (f32[16,128]{1,0:T(8,128)S(1)}, f32[16,128]{1,0:T(8,128)S(1)}, u32[]{:S(2)}, u32[]{:S(2)}) collective-permute-start(f32[16,128]{1,0:T(8,128)S(1)} %shard_map.96.own_ref), channel_id=1, source_target_pairs={{0,8},{8,16},{16,24},{24,32},{32,40},{40,48},{48,56},{56,64},{64,7... | collective-permute-start | bytes 24584 | tf_op jit(solution)/shard_map/ppermute | solution.py:338
  45.8 0.0 copy-done.3
  45.8 0.0 copy-done.5
  45.8 3.3 %shard_map.97 = (f32[24,48,128]{2,1,0:T(8,128)}, f32[24,48,128]{2,1,0:T(8,128)}) custom-call(f32[8]{0:T(128)} %table_ref.6, f32[32,32,128]{2,1,0:T(8,128)} %now_hbm.5, f32[32,32,128]{2,1,0:T(8,128)} %before_hbm.5, s32[32,32,128]{2,1,0:T(8,128)} %layer_hbm.5, f32[96,8,128]{2,1,0:T(8,128)} %copy-done.3, f32[96,8,128]{2,1,0:T(8,128)} %copy-done.5), custom_call_target="tpu_custom_call" | custom-call | tf_op jit(solution)/shard_map/pallas_call | solution.py:369
  49.0 0.0 copy-start.4
  49.1 0.0 copy-start.6
  49.1 0.0 collective-permute-done.3.right_ref
  49.1 1.4 %collective-permute-done.2.left_ref = f32[16,128]{1,0:T(8,128)S(1)} collective-permute-done((f32[16,128]{1,0:T(8,128)S(1)}, f32[16,128]{1,0:T(8,128)S(1)}, u32[]{:S(2)}, u32[]{:S(2)}) %collective-permute-start.2) | collective-permute-done | bytes 8224 | tf_op jit(solution)/shard_map/ppermute | solution.py:338
  50.5 1.9 %collective-permute-start.4 = (f32[24,48,128]{2,1,0:T(8,128)}, f32[24,48,128]{2,1,0:T(8,128)S(1)}, u32[]{:S(2)}, u32[]{:S(2)}) collective-permute-start(f32[24,48,128]{2,1,0:T(8,128)} %get-tuple-element.28), channel_id=1, source_target_pairs={{0,8},{8,16},{16,24},{24,32},{32,40},{40,48},{48,56},{56,64},{64,7... | collective-permute-start | bytes 1769480 | tf_op jit(solution)/shard_map/ppermute | solution.py:338
  52.4 5.8 %collective-permute-start.5 = (f32[24,48,128]{2,1,0:T(8,128)}, f32[24,48,128]{2,1,0:T(8,128)S(1)}, u32[]{:S(2)}, u32[]{:S(2)}) collective-permute-start(f32[24,48,128]{2,1,0:T(8,128)} %get-tuple-element.29), channel_id=1, source_target_pairs={{8,0},{16,8},{24,16},{32,24},{40,32},{48,40},{56,48},{64,56},{72,6... | collective-permute-start | bytes 1769480 | tf_op jit(solution)/shard_map/ppermute | solution.py:338
  58.1 0.7 shard_map.98
  58.8 9.4 %all-to-all-start.1 = ((f32[8,32,128]{2,1,0:T(8,128)}), f32[8,32,128]{2,1,0:T(8,128)}, u32[]{:S(2)}, u32[]{:S(2)}) async-start(f32[8,32,128]{2,1,0:T(8,128)} %shard_map.98), calls=%async_computation.1 | async-start | bytes 262144 | tf_op jit(solution)/shard_map/all_to_all | solution.py:387
  68.2 9.2 %all-to-all-done.1 = f32[8,32,128]{2,1,0:T(8,128)} async-done(((f32[8,32,128]{2,1,0:T(8,128)}), f32[8,32,128]{2,1,0:T(8,128)}, u32[]{:S(2)}, u32[]{:S(2)}) %all-to-all-start.1) | async-done | bytes 131104 | tf_op jit(solution)/shard_map/all_to_all | solution.py:387
  77.4 6.2 %shard_map.99.d_ref = f32[18432,128]{1,0:T(8,128)S(1)} custom-call(s32[1]{0:T(128)} %bitcast.place_ref, f32[256,128]{1,0:T(8,128)} %bitcast.3.got_ref), custom_call_target="tpu_custom_call" | custom-call | flops 1000000 | bytes 10485760 | tf_op jit(solution)/shard_map/pallas_call | solution.py:301
  83.6 0.0 collective-permute-done.4.xlo_hbm
  83.6 0.0 collective-permute-done.5.xhi_hbm
  83.6 0.0 copy-done.7
  83.6 0.0 copy-done.2
  83.6 0.0 copy-done.1
  83.6 0.0 copy-done
  83.6 0.0 copy-done.4
  83.6 0.0 copy-done.6
  83.6 10.7 %shard_map.100 = (f32[32,32,128]{2,1,0:T(8,128)}, f32[32,32,128]{2,1,0:T(8,128)}) custom-call(f32[8]{0:T(128)S(1)} %copy-done.7, f32[18432,128]{1,0:T(8,128)S(1)} %shard_map.99.d_ref, f32[32,32,128]{2,1,0:T(8,128)S(1)} %copy-done, f32[32,32,128]{2,1,0:T(8,128)S(1)} %copy-done.1, s32[32,32,128]{2,1,0:T(8,128)S(1)} %copy-done.2, f32[96,8,128]{2,1,0:T(8,128)S(1)} %copy-done.4, ...), custom_call_target="tpu_custom_call" | custom-call | tf_op jit(solution)/shard_map/pallas_call | solution.py:320
Async XLA Ops:
  0.6 83.0 %copy-start.7 = (f32[8]{0:T(128)S(1)}, f32[8]{0:T(128)}, u32[]{:S(2)}) copy-start(f32[8]{0:T(128)} %table_ref.6) | copy-start | bytes 100
  0.6 82.9 %copy-start.2 = (s32[32,32,128]{2,1,0:T(8,128)S(1)}, s32[32,32,128]{2,1,0:T(8,128)}, u32[]{:S(2)}) copy-start(s32[32,32,128]{2,1,0:T(8,128)} %layer_hbm.5) | copy-start | bytes 1572868
  0.7 82.9 %copy-start.1 = (f32[32,32,128]{2,1,0:T(8,128)S(1)}, f32[32,32,128]{2,1,0:T(8,128)}, u32[]{:S(2)}) copy-start(f32[32,32,128]{2,1,0:T(8,128)} %before_hbm.5) | copy-start | bytes 1572868
  0.7 82.9 %copy-start = (f32[32,32,128]{2,1,0:T(8,128)S(1)}, f32[32,32,128]{2,1,0:T(8,128)}, u32[]{:S(2)}) copy-start(f32[32,32,128]{2,1,0:T(8,128)} %now_hbm.5) | copy-start | bytes 1572868
  3.1 37.1 %collective-permute-start = (f32[96,8,128]{2,1,0:T(8,128)S(1)}, f32[96,8,128]{2,1,0:T(8,128)S(1)}, u32[]{:S(2)}, u32[]{:S(2)}) collective-permute-start(f32[96,8,128]{2,1,0:T(8,128)S(1)} %get-tuple-element.16), channel_id=1, source_target_pairs={{0,1},{1,2},{2,3},{3,4},{4,5},{5,6},{6,7},{8,9},{9,10},{10,11},{11... | collective-permute-start | bytes 1179656 | tf_op jit(solution)/shard_map/ppermute | solution.py:338
  6.6 33.6 %collective-permute-start.1 = (f32[96,8,128]{2,1,0:T(8,128)S(1)}, f32[96,8,128]{2,1,0:T(8,128)S(1)}, u32[]{:S(2)}, u32[]{:S(2)}) collective-permute-start(f32[96,8,128]{2,1,0:T(8,128)S(1)} %get-tuple-element.17), channel_id=1, source_target_pairs={{1,0},{2,1},{3,2},{4,3},{5,4},{6,5},{7,6},{9,8},{10,9},{11,10},{12... | collective-permute-start | bytes 1179656 | tf_op jit(solution)/shard_map/ppermute | solution.py:338
  40.2 5.6 %copy-start.3 = (f32[96,8,128]{2,1,0:T(8,128)}, f32[96,8,128]{2,1,0:T(8,128)S(1)}, u32[]{:S(2)}) copy-start(f32[96,8,128]{2,1,0:T(8,128)S(1)} %collective-permute-done.ylo_hbm) | copy-start | bytes 1179652
  40.2 5.6 %copy-start.5 = (f32[96,8,128]{2,1,0:T(8,128)}, f32[96,8,128]{2,1,0:T(8,128)S(1)}, u32[]{:S(2)}) copy-start(f32[96,8,128]{2,1,0:T(8,128)S(1)} %collective-permute-done.1.yhi_hbm) | copy-start | bytes 1179652
  41.4 7.6 %collective-permute-start.3 = (f32[16,128]{1,0:T(8,128)S(1)}, f32[16,128]{1,0:T(8,128)S(1)}, u32[]{:S(2)}, u32[]{:S(2)}) collective-permute-start(f32[16,128]{1,0:T(8,128)S(1)} %shard_map.96.own_ref), channel_id=1, source_target_pairs={{8,0},{16,8},{24,16},{32,24},{40,32},{48,40},{56,48},{64,56},{72,6... | collective-permute-start | bytes 24584 | tf_op jit(solution)/shard_map/ppermute | solution.py:338
  43.4 7.1 %collective-permute-start.2 = (f32[16,128]{1,0:T(8,128)S(1)}, f32[16,128]{1,0:T(8,128)S(1)}, u32[]{:S(2)}, u32[]{:S(2)}) collective-permute-start(f32[16,128]{1,0:T(8,128)S(1)} %shard_map.96.own_ref), channel_id=1, source_target_pairs={{0,8},{8,16},{16,24},{24,32},{32,40},{40,48},{48,56},{56,64},{64,7... | collective-permute-start | bytes 24584 | tf_op jit(solution)/shard_map/ppermute | solution.py:338
  49.0 34.6 %copy-start.4 = (f32[96,8,128]{2,1,0:T(8,128)S(1)}, f32[96,8,128]{2,1,0:T(8,128)}, u32[]{:S(2)}) copy-start(f32[96,8,128]{2,1,0:T(8,128)} %copy-done.3) | copy-start | bytes 1179652
  49.1 34.6 %copy-start.6 = (f32[96,8,128]{2,1,0:T(8,128)S(1)}, f32[96,8,128]{2,1,0:T(8,128)}, u32[]{:S(2)}) copy-start(f32[96,8,128]{2,1,0:T(8,128)} %copy-done.5) | copy-start | bytes 1179652
  50.5 33.1 %collective-permute-start.4 = (f32[24,48,128]{2,1,0:T(8,128)}, f32[24,48,128]{2,1,0:T(8,128)S(1)}, u32[]{:S(2)}, u32[]{:S(2)}) collective-permute-start(f32[24,48,128]{2,1,0:T(8,128)} %get-tuple-element.28), channel_id=1, source_target_pairs={{0,8},{8,16},{16,24},{24,32},{32,40},{40,48},{48,56},{56,64},{64,7... | collective-permute-start | bytes 1769480 | tf_op jit(solution)/shard_map/ppermute | solution.py:338
  52.4 31.2 %collective-permute-start.5 = (f32[24,48,128]{2,1,0:T(8,128)}, f32[24,48,128]{2,1,0:T(8,128)S(1)}, u32[]{:S(2)}, u32[]{:S(2)}) collective-permute-start(f32[24,48,128]{2,1,0:T(8,128)} %get-tuple-element.29), channel_id=1, source_target_pairs={{8,0},{16,8},{24,16},{32,24},{40,32},{48,40},{56,48},{64,56},{72,6... | collective-permute-start | bytes 1769480 | tf_op jit(solution)/shard_map/ppermute | solution.py:338
  58.8 18.6 %all-to-all-start.1 = ((f32[8,32,128]{2,1,0:T(8,128)}), f32[8,32,128]{2,1,0:T(8,128)}, u32[]{:S(2)}, u32[]{:S(2)}) async-start(f32[8,32,128]{2,1,0:T(8,128)} %shard_map.98), calls=%async_computation.1 | async-start | bytes 262144 | tf_op jit(solution)/shard_map/all_to_all | solution.py:387

commit v9 on v7

--- a/solution.py
+++ b/solution.py
@@ -18,7 +18,7 @@
 CELLS = CX * CY * CZ
 NPT = 128
 ROW_BITS, Z_BITS, P_BITS = 12, 7, 12
-BODY = (24, 22, 21, 20, 19, 18, 17, 16)
+PLANES = (48, 44, 42, 40, 38, 36, 34, 32)
 GROUP = 32
 MIB = 1024 * 1024
 PARTS = 4 * H
@@ -222,9 +222,10 @@
         )
         for n, (src, dst) in enumerate(pieces):
             copies.append(pltpu.make_async_copy(src, dst, sems.at[k, n]))
-    for c in copies:
+    fields, layers = copies[:10], copies[10:]
+    for c in layers + fields:
         c.start()
-    for c in copies:
+    for c in layers:
         c.wait()
 
     def fill(i, _):
@@ -258,6 +259,8 @@
         return 0
 
     lax.fori_loop(0, EX // 8, coefficients, 0)
+    for c in fields:
+        c.wait()
 
     next_copy, prior_copy = (
         pltpu.make_async_copy(ref.at[pl.ds(1 + H, CX), pl.ds(2 * H, CY)], hbm, sem_out.at[n])
@@ -266,28 +269,23 @@
     for step in range(STEPS):
         u_ref, w_ref = (a_ref, b_ref) if step % 2 == 0 else (b_ref, a_ref)
 
-        planes = BODY[step]
-        start = EX // 2 - planes
+        planes = PLANES[step]
+        start = EX // 2 - planes // 2
         rows = range(0, EY // 8) if step < STEPS - 1 else range(1, 1 + CY // 8)
 
-        def advance(i, _, u_ref=u_ref, w_ref=w_ref, step=step, planes=planes, start=start, rows=rows):
-            for k in range(planes):
-                x = start + planes * i + k
-                for j in rows:
-                    y = H + 8 * j
-                    u = u_ref[x + 1, pl.ds(y, 8), :]
-                    kz = kz_ref[x + 1, pl.ds(y, 8), :]
-                    in_z = kz * pltpu.roll(u, CZ - 1, 1) + pltpu.roll(kz * u, 1, 1)
-                    in_x = (kx_ref[x + 1, pl.ds(y, 8), :] * u_ref[x + 2, pl.ds(y, 8), :]
-                            + kx_ref[x, pl.ds(y, 8), :] * u_ref[x, pl.ds(y, 8), :])
-                    in_y = (ky_ref[x + 1, pl.ds(y, 8), :] * u_ref[x + 1, pl.ds(y + 1, 8), :]
-                            + ky_ref[x + 1, pl.ds(y - 1, 8), :] * u_ref[x + 1, pl.ds(y - 1, 8), :])
-                    drive = d_ref[pl.ds((x * EY + 8 * j) * STEPS + step, 8, stride=STEPS), :]
-                    own = kc_ref[x + 1, pl.ds(y, 8), :] * u - w_ref[x + 1, pl.ds(y, 8), :]
-                    w_ref[x + 1, pl.ds(y, 8), :] = (own + drive) + ((in_x + in_y) + in_z)
-            return 0
-
-        lax.fori_loop(0, 2, advance, 0)
+        for x in range(start, start + planes):
+            for j in rows:
+                y = H + 8 * j
+                u = u_ref[x + 1, pl.ds(y, 8), :]
+                kz = kz_ref[x + 1, pl.ds(y, 8), :]
+                in_z = kz * pltpu.roll(u, CZ - 1, 1) + pltpu.roll(kz * u, 1, 1)
+                in_x = (kx_ref[x + 1, pl.ds(y, 8), :] * u_ref[x + 2, pl.ds(y, 8), :]
+                        + kx_ref[x, pl.ds(y, 8), :] * u_ref[x, pl.ds(y, 8), :])
+                in_y = (ky_ref[x + 1, pl.ds(y, 8), :] * u_ref[x + 1, pl.ds(y + 1, 8), :]
+                        + ky_ref[x + 1, pl.ds(y - 1, 8), :] * u_ref[x + 1, pl.ds(y - 1, 8), :])
+                drive = d_ref[pl.ds((x * EY + 8 * j) * STEPS + step, 8, stride=STEPS), :]
+                own = kc_ref[x + 1, pl.ds(y, 8), :] * u - w_ref[x + 1, pl.ds(y, 8), :]
+                w_ref[x + 1, pl.ds(y, 8), :] = (own + drive) + ((in_x + in_y) + in_z)
 
         if step == STEPS - 2:
             prior_copy.start()

time: 91.8 us -> 90.4 us (0.985)
  the two profiles are of different devices: /device:TPU:58 before, /device:TPU:34 now
where the time goes in v9:
time: 90.4 us; the launch traced here: 89.9 us
  blocking collectives  32.3 us (36%)
  starting transfers between devices  26.3 us (29%)
  Pallas kernels  25.7 us (28%)
  waiting for transfers between devices  4.7 us (5%)
    all_to_all x1, blocking collectives, shards(): moved = lax.all_to_all(dealt, 'along', 0, 0, tiled=True)  32.3 us
    ppermute x6, starting transfers between devices, neighbours(): return (lax.ppermute(high, axis, up), lax.ppermute(low, axis, down))  19 us
    pallas_call x1, Pallas kernels, window(): pl.pallas_call(window_kernel, out_shape=(grid, grid), in_specs=[pl.BlockS...  10.2 us
    pallas_call x1, Pallas kernels, points(): pl.pallas_call(points_kernel, out_shape=pltpu.VMEM((ROWS * STEPS, CZ), jn...  8.12 us
    all_to_all x1, starting transfers between devices, shards(): got = lax.all_to_all(spread, 'across', 0, 0, tiled=True)  7.22 us
    ppermute x6, waiting for transfers between devices, neighbours(): return (lax.ppermute(high, axis, up), lax.ppermute(low, axis, down))  4.7 us
    pallas_call x1, Pallas kernels, shards(): pl.pallas_call(slab_kernel, out_shape=(slab, slab), in_specs=[smem] + [an...  3.26 us
    pallas_call x1, Pallas kernels, shards(): pl.pallas_call(prepare_kernel, out_shape=(slab, slab, pltpu.VMEM((sources...  2.3 us
  transfers between devices with their start and end apart: 7, of which 1 were waited for; matrix products, arithmetic and copies ran while one was open for 0% of the time, Pallas kernels for 13%

profile of v9, /device:TPU:34, one launch (start us, length us, event | category | flops | bytes accessed | tf_op | source)
XLA Modules:
  0.0 89.9 jit_solution(13998376029441406695)
XLA Ops:
  0.6 2.3 %shard_map.95 = (f32[96,8,128]{2,1,0:T(8,128)S(1)}, f32[96,8,128]{2,1,0:T(8,128)S(1)}, bf16[96,4,128]{2,1,0:T(4,128)(2,1)S(1)}) custom-call(f32[8]{0:T(128)} %table_ref.6, f32[32,32,128]{2,1,0:T(8,128)} %now_hbm.5, f32[32,32,128]{2,1,0:T(8,128)} %before_hbm.5, s32[32,32,128]{2,1,0:T(8,128)} %layer_hbm.5, bf16[2,2,12288]{2,1,0:T(2,128)(2,1)} %bitcast.5), custom_call_target="tpu_custom_call" | custom-call | tf_op jit(solution)/shard_map/pallas_call | solution.py:345
  2.9 2.6 %collective-permute-start = (f32[96,8,128]{2,1,0:T(8,128)S(1)}, f32[96,8,128]{2,1,0:T(8,128)S(1)}, u32[]{:S(2)}, u32[]{:S(2)}) collective-permute-start(f32[96,8,128]{2,1,0:T(8,128)S(1)} %get-tuple-element.12), channel_id=1, source_target_pairs={{0,1},{1,2},{2,3},{3,4},{4,5},{5,6},{6,7},{8,9},{9,10},{10,11},{11... | collective-permute-start | bytes 1179656 | tf_op jit(solution)/shard_map/ppermute | solution.py:336
  5.5 4.5 %collective-permute-start.1 = (f32[96,8,128]{2,1,0:T(8,128)S(1)}, f32[96,8,128]{2,1,0:T(8,128)S(1)}, u32[]{:S(2)}, u32[]{:S(2)}) collective-permute-start(f32[96,8,128]{2,1,0:T(8,128)S(1)} %get-tuple-element.13), channel_id=1, source_target_pairs={{1,0},{2,1},{3,2},{4,3},{5,4},{6,5},{7,6},{9,8},{10,9},{11,10},{12... | collective-permute-start | bytes 1179656 | tf_op jit(solution)/shard_map/ppermute | solution.py:336
  10.0 32.3 %all_to_all.10.moved_ref = bf16[96,4,128]{2,1,0:T(4,128)(2,1)} all-to-all(bf16[96,4,128]{2,1,0:T(4,128)(2,1)S(1)} %get-tuple-element.14), channel_id=1, replica_groups=mesh['along'=96,'across'=8] {'along'}, dimensions={0} | all-to-all | bytes 196608 | tf_op jit(solution)/shard_map/all_to_all | solution.py:354
  42.3 0.0 collective-permute-done.ylo_hbm
  42.3 0.0 copy-start.3
  42.3 0.0 collective-permute-done.1.yhi_hbm
  42.3 0.0 copy-start.5
  42.3 1.2 %shard_map.96.own_ref = f32[16,128]{1,0:T(8,128)S(1)} custom-call(bf16[96,4,128]{2,1,0:T(4,128)(2,1)} %all_to_all.10.moved_ref, bf16[24,384]{1,0:T(8,128)(2,1)} %constant.6.clone.table_ref, s32[1,128]{1,0:T(1,128)} %bitcast.6, s32[1,128]{1,0:T(1,128)} %cell_ref.1), custom_call_target="tpu_custom_call" | custom-call | tf_op jit(solution)/shard_map/pallas_call | solution.py:357
  43.5 1.9 %collective-permute-start.3 = (f32[16,128]{1,0:T(8,128)S(1)}, f32[16,128]{1,0:T(8,128)S(1)}, u32[]{:S(2)}, u32[]{:S(2)}) collective-permute-start(f32[16,128]{1,0:T(8,128)S(1)} %shard_map.96.own_ref), channel_id=1, source_target_pairs={{8,0},{16,8},{24,16},{32,24},{40,32},{48,40},{56,48},{64,56},{72,6... | collective-permute-start | bytes 24584 | tf_op jit(solution)/shard_map/ppermute | solution.py:336
  45.5 2.4 %collective-permute-start.2 = (f32[16,128]{1,0:T(8,128)S(1)}, f32[16,128]{1,0:T(8,128)S(1)}, u32[]{:S(2)}, u32[]{:S(2)}) collective-permute-start(f32[16,128]{1,0:T(8,128)S(1)} %shard_map.96.own_ref), channel_id=1, source_target_pairs={{0,8},{8,16},{16,24},{24,32},{32,40},{40,48},{48,56},{56,64},{64,7... | collective-permute-start | bytes 24584 | tf_op jit(solution)/shard_map/ppermute | solution.py:336
  47.9 0.0 collective-permute-done.3.right_ref
  47.9 4.7 %collective-permute-done.2.left_ref = f32[16,128]{1,0:T(8,128)S(1)} collective-permute-done((f32[16,128]{1,0:T(8,128)S(1)}, f32[16,128]{1,0:T(8,128)S(1)}, u32[]{:S(2)}, u32[]{:S(2)}) %collective-permute-start.2) | collective-permute-done | bytes 8224 | tf_op jit(solution)/shard_map/ppermute | solution.py:336
  52.6 0.7 shard_map.97
  53.2 7.2 %all-to-all-start.1 = ((f32[8,32,128]{2,1,0:T(8,128)}), f32[8,32,128]{2,1,0:T(8,128)S(1)}, u32[]{:S(2)}, u32[]{:S(2)}) async-start(f32[8,32,128]{2,1,0:T(8,128)} %shard_map.97), calls=%async_computation.1 | async-start | bytes 262144 | tf_op jit(solution)/shard_map/all_to_all | solution.py:374
  60.4 0.0 copy-done.3
  60.4 0.0 copy-done.5
  60.4 3.3 %shard_map.99 = (f32[24,48,128]{2,1,0:T(8,128)}, f32[24,48,128]{2,1,0:T(8,128)}) custom-call(f32[8]{0:T(128)} %table_ref.6, f32[32,32,128]{2,1,0:T(8,128)} %now_hbm.5, f32[32,32,128]{2,1,0:T(8,128)} %before_hbm.5, s32[32,32,128]{2,1,0:T(8,128)} %layer_hbm.5, f32[96,8,128]{2,1,0:T(8,128)} %copy-done.3, f32[96,8,128]{2,1,0:T(8,128)} %copy-done.5), custom_call_target="tpu_custom_call" | custom-call | tf_op jit(solution)/shard_map/pallas_call | solution.py:376
  63.7 1.9 %collective-permute-start.4 = (f32[24,48,128]{2,1,0:T(8,128)}, f32[24,48,128]{2,1,0:T(8,128)}, u32[]{:S(2)}, u32[]{:S(2)}) collective-permute-start(f32[24,48,128]{2,1,0:T(8,128)} %get-tuple-element.20), channel_id=1, source_target_pairs={{0,8},{8,16},{16,24},{24,32},{32,40},{40,48},{48,56},{56,64},{64,7... | collective-permute-start | bytes 1769480 | tf_op jit(solution)/shard_map/ppermute | solution.py:336
  65.6 5.8 %collective-permute-start.5 = (f32[24,48,128]{2,1,0:T(8,128)}, f32[24,48,128]{2,1,0:T(8,128)}, u32[]{:S(2)}, u32[]{:S(2)}) collective-permute-start(f32[24,48,128]{2,1,0:T(8,128)} %get-tuple-element.21), channel_id=1, source_target_pairs={{8,0},{16,8},{24,16},{32,24},{40,32},{48,40},{56,48},{64,56},{72,6... | collective-permute-start | bytes 1769480 | tf_op jit(solution)/shard_map/ppermute | solution.py:336
  71.4 0.0 all-to-all-done.1
  71.4 0.0 copy-start
  71.4 0.0 copy-start.1
  71.4 0.0 copy-start.2
  71.5 0.0 copy-start.4
  71.5 0.0 copy-start.6
  71.5 0.0 copy-start.7
  71.5 8.1 %shard_map.98.d_ref = f32[18432,128]{1,0:T(8,128)S(1)} custom-call(s32[1]{0:T(128)} %bitcast.place_ref, f32[256,128]{1,0:T(8,128)S(1)} %bitcast.4), custom_call_target="tpu_custom_call" | custom-call | flops 999999995904 | bytes 1073741824 | tf_op jit(solution)/shard_map/pallas_call | solution.py:299
  79.6 0.0 collective-permute-done.4.xlo_hbm
  79.6 0.0 collective-permute-done.5.xhi_hbm
  79.6 0.0 copy-done
  79.6 0.0 copy-done.1
  79.7 0.0 copy-done.2
  79.7 0.0 copy-done.4
  79.7 0.0 copy-done.6
  79.7 0.0 copy-done.7
  79.7 10.2 %shard_map.100 = (f32[32,32,128]{2,1,0:T(8,128)}, f32[32,32,128]{2,1,0:T(8,128)}) custom-call(f32[8]{0:T(128)S(1)} %copy-done.7, f32[18432,128]{1,0:T(8,128)S(1)} %shard_map.98.d_ref, f32[32,32,128]{2,1,0:T(8,128)S(1)} %copy-done, f32[32,32,128]{2,1,0:T(8,128)S(1)} %copy-done.1, s32[32,32,128]{2,1,0:T(8,128)S(1)} %copy-done.2, f32[96,8,128]{2,1,0:T(8,128)S(1)} %copy-done.4, ...), custom_call_target="tpu_custom_call" | custom-call | tf_op jit(solution)/shard_map/pallas_call | solution.py:318
Async XLA Ops:
  2.9 39.3 %collective-permute-start = (f32[96,8,128]{2,1,0:T(8,128)S(1)}, f32[96,8,128]{2,1,0:T(8,128)S(1)}, u32[]{:S(2)}, u32[]{:S(2)}) collective-permute-start(f32[96,8,128]{2,1,0:T(8,128)S(1)} %get-tuple-element.12), channel_id=1, source_target_pairs={{0,1},{1,2},{2,3},{3,4},{4,5},{5,6},{6,7},{8,9},{9,10},{10,11},{11... | collective-permute-start | bytes 1179656 | tf_op jit(solution)/shard_map/ppermute | solution.py:336
  5.5 36.8 %collective-permute-start.1 = (f32[96,8,128]{2,1,0:T(8,128)S(1)}, f32[96,8,128]{2,1,0:T(8,128)S(1)}, u32[]{:S(2)}, u32[]{:S(2)}) collective-permute-start(f32[96,8,128]{2,1,0:T(8,128)S(1)} %get-tuple-element.13), channel_id=1, source_target_pairs={{1,0},{2,1},{3,2},{4,3},{5,4},{6,5},{7,6},{9,8},{10,9},{11,10},{12... | collective-permute-start | bytes 1179656 | tf_op jit(solution)/shard_map/ppermute | solution.py:336
  42.3 18.2 %copy-start.3 = (f32[96,8,128]{2,1,0:T(8,128)}, f32[96,8,128]{2,1,0:T(8,128)S(1)}, u32[]{:S(2)}) copy-start(f32[96,8,128]{2,1,0:T(8,128)S(1)} %collective-permute-done.ylo_hbm) | copy-start | bytes 1179652
  42.3 18.2 %copy-start.5 = (f32[96,8,128]{2,1,0:T(8,128)}, f32[96,8,128]{2,1,0:T(8,128)S(1)}, u32[]{:S(2)}) copy-start(f32[96,8,128]{2,1,0:T(8,128)S(1)} %collective-permute-done.1.yhi_hbm) | copy-start | bytes 1179652
  43.5 4.3 %collective-permute-start.3 = (f32[16,128]{1,0:T(8,128)S(1)}, f32[16,128]{1,0:T(8,128)S(1)}, u32[]{:S(2)}, u32[]{:S(2)}) collective-permute-start(f32[16,128]{1,0:T(8,128)S(1)} %shard_map.96.own_ref), channel_id=1, source_target_pairs={{8,0},{16,8},{24,16},{32,24},{40,32},{48,40},{56,48},{64,56},{72,6... | collective-permute-start | bytes 24584 | tf_op jit(solution)/shard_map/ppermute | solution.py:336
  45.5 7.1 %collective-permute-start.2 = (f32[16,128]{1,0:T(8,128)S(1)}, f32[16,128]{1,0:T(8,128)S(1)}, u32[]{:S(2)}, u32[]{:S(2)}) collective-permute-start(f32[16,128]{1,0:T(8,128)S(1)} %shard_map.96.own_ref), channel_id=1, source_target_pairs={{0,8},{8,16},{16,24},{24,32},{32,40},{40,48},{48,56},{56,64},{64,7... | collective-permute-start | bytes 24584 | tf_op jit(solution)/shard_map/ppermute | solution.py:336
  53.2 18.2 %all-to-all-start.1 = ((f32[8,32,128]{2,1,0:T(8,128)}), f32[8,32,128]{2,1,0:T(8,128)S(1)}, u32[]{:S(2)}, u32[]{:S(2)}) async-start(f32[8,32,128]{2,1,0:T(8,128)} %shard_map.97), calls=%async_computation.1 | async-start | bytes 262144 | tf_op jit(solution)/shard_map/all_to_all | solution.py:374
  63.7 15.9 %collective-permute-start.4 = (f32[24,48,128]{2,1,0:T(8,128)}, f32[24,48,128]{2,1,0:T(8,128)}, u32[]{:S(2)}, u32[]{:S(2)}) collective-permute-start(f32[24,48,128]{2,1,0:T(8,128)} %get-tuple-element.20), channel_id=1, source_target_pairs={{0,8},{8,16},{16,24},{24,32},{32,40},{40,48},{48,56},{56,64},{64,7... | collective-permute-start | bytes 1769480 | tf_op jit(solution)/shard_map/ppermute | solution.py:336
  65.6 14.0 %collective-permute-start.5 = (f32[24,48,128]{2,1,0:T(8,128)}, f32[24,48,128]{2,1,0:T(8,128)}, u32[]{:S(2)}, u32[]{:S(2)}) collective-permute-start(f32[24,48,128]{2,1,0:T(8,128)} %get-tuple-element.21), channel_id=1, source_target_pairs={{8,0},{16,8},{24,16},{32,24},{40,32},{48,40},{56,48},{64,56},{72,6... | collective-permute-start | bytes 1769480 | tf_op jit(solution)/shard_map/ppermute | solution.py:336
  71.4 8.2 %copy-start = (f32[32,32,128]{2,1,0:T(8,128)S(1)}, f32[32,32,128]{2,1,0:T(8,128)}, u32[]{:S(2)}) copy-start(f32[32,32,128]{2,1,0:T(8,128)} %now_hbm.5) | copy-start | bytes 1572868
  71.4 8.2 %copy-start.1 = (f32[32,32,128]{2,1,0:T(8,128)S(1)}, f32[32,32,128]{2,1,0:T(8,128)}, u32[]{:S(2)}) copy-start(f32[32,32,128]{2,1,0:T(8,128)} %before_hbm.5) | copy-start | bytes 1572868
  71.4 8.2 %copy-start.2 = (s32[32,32,128]{2,1,0:T(8,128)S(1)}, s32[32,32,128]{2,1,0:T(8,128)}, u32[]{:S(2)}) copy-start(s32[32,32,128]{2,1,0:T(8,128)} %layer_hbm.5) | copy-start | bytes 1572868
  71.5 8.2 %copy-start.4 = (f32[96,8,128]{2,1,0:T(8,128)S(1)}, f32[96,8,128]{2,1,0:T(8,128)}, u32[]{:S(2)}) copy-start(f32[96,8,128]{2,1,0:T(8,128)} %copy-done.3) | copy-start | bytes 1179652
  71.5 8.2 %copy-start.6 = (f32[96,8,128]{2,1,0:T(8,128)S(1)}, f32[96,8,128]{2,1,0:T(8,128)}, u32[]{:S(2)}) copy-start(f32[96,8,128]{2,1,0:T(8,128)} %copy-done.5) | copy-start | bytes 1179652
  71.5 8.2 %copy-start.7 = (f32[8]{0:T(128)S(1)}, f32[8]{0:T(128)}, u32[]{:S(2)}) copy-start(f32[8]{0:T(128)} %table_ref.6) | copy-start | bytes 100
